TPU v7x, 128 devices: a whole 4x4x4 slice. The times are simulated.
128 devices in a mesh: gx: 8 (over z, core), gy: 16 (over y, x).
Axes of the slice: x: 4, y: 4, z: 4, core: 2. Of those that a mesh axis runs over, the one named last changes fastest.
Arguments:
- queries: bfloat16 [2048, 1536], P(('gx', 'gy')), may hold values from -40 to 40
- new_kv: bfloat16 [2048, 1024], P(('gx', 'gy')), may hold values from -6 to 6
- cache_pool: bfloat16 [16384, 16, 1024], P(('gx', 'gy')), may hold values from -6 to 6
- cache_len: int32 [2048], P(('gx', 'gy')), may hold values from 1 to 512, as said below
- local_pages: int32 [1024, 32], P(('gx', 'gy')), may hold values from 0 to 127
- anchor: int32 [1024], P(('gx', 'gy')), may hold values from 0 to 15, as said below
- push_pages: int32 [2048, 32], P(('gx', 'gy')), may hold values from 0 to 127
- prefill_attn: bfloat16 [14336, 1536], P(('gx', 'gy')), may hold values from -4 to 4
- residual: bfloat16 [16384, 1536], P(('gx', 'gy')), may hold values from -7 to 7
- out_weight: bfloat16 [1536, 1536], P('gx'), may hold values from -0.15625 to 0.15625
- norm_gain: bfloat16 [1536], replicated, may hold values from 0.099609375 to 1.8984375
- router: bfloat16 [1536, 32], replicated, may hold values from -4 to 4
- routes: int32 [16384, 8], P(('gx', 'gy')), may hold values from 0 to 31, all different within a row; in each aligned block of 128 rows (0 to 127, 128 to 255, ...) at most 48 rows name the same one
- gate_up: bfloat16 [1536, 32, 1024], P('gx', 'gy'), may hold values from -0.15625 to 0.15625
- down_proj: bfloat16 [1536, 32, 512], P('gx', 'gy'), may hold values from -0.25 to 0.25
Outputs:
- attended: bfloat16 [2048, 1536], P(('gx', 'gy'))
- layer_out: float32 [16384, 1536], P(('gx', 'gy'))
Inputs may be any that keep to these rules, and one draw needn't show every extreme that they name: `cache_len`: every device holds a request with exactly 512 cached tokens. The last 8 requests of a device continue from the device in the same gx row whose gy column is anchor, never from the device itself; one column sends at most 1 of them to one device, and some column sends exactly 1 to each device. `routes`: no expert is named by more than 48 of the rows of one device.
All inputs are finite; a program needn't handle non-finite values.
Results may differ from a plain program's by a relative error of at most 0.0038.
Values may be sent and summed in bfloat16 or wider, within the bound.
A program may use at most 192 MiB of HBM per device.

v0:
```python
import math

import jax
import jax.numpy as jnp
from jax import lax
from jax.sharding import PartitionSpec as P

D = 1536
HEADS = 24
KV_HEADS = 8
HEAD = 64
EXPERTS = 32
FF = 512
TOP = 8
MAXLEN = 512
R_DEV = 16
LOCAL = 8
MOVED = 8
CAP = 48


def in_one_piece(arrays, axis, split_dim, concat_dim, along):
    columns = [a.reshape(*a.shape[:along], -1) for a in arrays]
    both = jnp.concatenate(columns, axis=along)
    result, at, gathered = (
        lax.all_to_all(both, axis, split_axis=split_dim, concat_axis=concat_dim, tiled=True),
        0,
        [],
    )
    for a, column in zip(arrays, columns):
        share = result[..., at : at + column.shape[along]]
        gathered.append(share.reshape(*share.shape[:along], *a.shape[along:]))
        at += column.shape[along]
    return tuple(gathered)


def side_by_side(arrays, axis, dim, along):
    widths = [math.prod(a.shape[along:]) for a in arrays]
    both = jnp.concatenate(
        [a.reshape(*a.shape[:along], w) for a, w in zip(arrays, widths)], axis=along
    )
    result = lax.all_gather(both, axis, axis=dim, tiled=True)
    blocks = jnp.split(result, [sum(widths[:k]) for k in range(1, len(widths))], axis=along)
    return tuple(
        (b.reshape(*result.shape[:along], *a.shape[along:]) for a, b in zip(arrays, blocks))
    )


def partial_attend(query_heads, keyval, lengths):
    count_req, positions, kv_width = keyval.shape
    kv_count = query_heads.shape[1]
    head_size = query_heads.shape[3]
    half_width = kv_count * head_size
    key_rows = keyval[:, :, :half_width].reshape(count_req, positions, kv_count, head_size)
    value_rows = keyval[:, :, half_width:].reshape(count_req, positions, kv_count, head_size)
    scores = jnp.einsum(
        "nkgh,ntkh->nkgt", query_heads, key_rows, preferred_element_type=jnp.float32
    ) * (1.0 / math.sqrt(head_size))
    valid = (jnp.arange(positions)[None, :] < lengths[:, None])[:, None, None, :]
    masked = jnp.where(valid, scores, -1e30)
    cache_max = jnp.max(masked, axis=3)
    expos = jnp.where(valid, jnp.exp(masked - cache_max[..., None]), 0.0)
    totals = jnp.sum(expos, axis=3)
    weights = expos.astype(jnp.bfloat16)
    mixture = jnp.einsum("nkgt,ntkh->nkgh", weights, value_rows, preferred_element_type=jnp.float32)
    return (cache_max, totals, mixture)


def finish(query_heads, fresh, cache_max, totals, mixture):
    count_req, kv_count, group_size, head_size = query_heads.shape
    half_width = kv_count * head_size
    own_key = fresh[:, :half_width].reshape(count_req, kv_count, head_size)
    own_value = fresh[:, half_width:].reshape(count_req, kv_count, head_size).astype(jnp.float32)
    own_score = jnp.einsum(
        "nkgh,nkh->nkg", query_heads, own_key, preferred_element_type=jnp.float32
    ) * (1.0 / math.sqrt(head_size))
    highest = jnp.maximum(cache_max, own_score)
    old_share = jnp.exp(cache_max - highest)
    new_share = jnp.exp(own_score - highest)
    weighted = old_share[..., None] * mixture + new_share[..., None] * own_value[:, :, None, :]
    output = weighted / (old_share * totals + new_share)[..., None]
    return output.reshape(count_req, kv_count * group_size * head_size).astype(jnp.bfloat16)


def body(
    queries,
    new_kv,
    cache_pool,
    cache_len,
    local_pages,
    anchor,
    push_pages,
    prefill_attn,
    residual,
    out_weight,
    norm_gain,
    router,
    routes,
    gate_up,
    down_proj,
):
    columns = lax.axis_size("gy")
    slot_count = (MOVED + columns - 2) // (columns - 1)
    group_size = HEADS // KV_HEADS
    kv_width = 2 * KV_HEADS * HEAD
    query_heads = queries.reshape(R_DEV, KV_HEADS, group_size, HEAD)
    local_kv = cache_pool[local_pages].reshape(LOCAL, MAXLEN, kv_width)
    matches = (anchor[:, None] == jnp.arange(columns, dtype=jnp.int32)[None, :]).astype(jnp.int32)
    earlier = jnp.sum((jnp.cumsum(matches, axis=0) - 1) * matches, axis=1)
    chosen = anchor * slot_count + earlier
    local_max, local_totals, local_mix = partial_attend(
        query_heads[:LOCAL], local_kv, cache_len[:LOCAL]
    )
    picker = chosen[:, None] == jnp.arange(columns * slot_count, dtype=jnp.int32)[None, :]
    sent_queries = jnp.einsum(
        "ms,md->sd",
        picker.astype(jnp.bfloat16),
        queries[LOCAL:],
        preferred_element_type=jnp.float32,
    )
    sent_lengths = jnp.sum(
        jnp.where(picker, cache_len[LOCAL:, None].astype(jnp.float32), 0.0), axis=0
    )
    got_queries, got_lengths = in_one_piece(
        (sent_queries.reshape(columns, slot_count, D), sent_lengths.reshape(columns, slot_count)),
        "gy",
        0,
        0,
        2,
    )
    far_heads = got_queries.astype(jnp.bfloat16).reshape(
        columns * slot_count, KV_HEADS, group_size, HEAD
    )
    far_kv = cache_pool[push_pages].reshape(columns * slot_count, MAXLEN, kv_width)
    far_max, far_totals, far_mix = partial_attend(
        far_heads, far_kv, got_lengths.reshape(columns * slot_count)
    )
    back_max, back_totals, back_mix = in_one_piece(
        (
            far_max.reshape(columns, slot_count, KV_HEADS, group_size),
            far_totals.reshape(columns, slot_count, KV_HEADS, group_size),
            far_mix.reshape(columns, slot_count, KV_HEADS, group_size, HEAD),
        ),
        "gy",
        0,
        0,
        4,
    )
    cache_max = jnp.concatenate(
        [local_max, back_max.reshape(columns * slot_count, KV_HEADS, group_size)[chosen]], axis=0
    )
    totals = jnp.concatenate(
        [local_totals, back_totals.reshape(columns * slot_count, KV_HEADS, group_size)[chosen]],
        axis=0,
    )
    mixture = jnp.concatenate(
        [local_mix, back_mix.reshape(columns * slot_count, KV_HEADS, group_size, HEAD)[chosen]],
        axis=0,
    )
    attended = finish(query_heads, new_kv, cache_max, totals, mixture)
    tokens = jnp.concatenate([attended, prefill_attn], axis=0)
    row_count = tokens.shape[0]
    full_out, full_pair, full_down = side_by_side((out_weight, gate_up, down_proj), "gx", 0, 1)
    stream = residual.astype(jnp.float32) + jnp.dot(
        tokens, full_out, preferred_element_type=jnp.float32
    )
    normed = (
        stream
        * lax.rsqrt(jnp.mean(stream * stream, axis=1, keepdims=True) + 1e-06)
        * norm_gain.astype(jnp.float32)
    ).astype(jnp.bfloat16)
    logits = jnp.dot(normed, router, preferred_element_type=jnp.float32)
    selector = routes[:, :, None] == jnp.arange(EXPERTS, dtype=jnp.int32)[None, None, :]
    gate_weights = jax.nn.softmax(
        jnp.sum(jnp.where(selector, logits[:, None, :], 0.0), axis=2), axis=1
    )
    flat_routes = routes.reshape(row_count * TOP)
    route_hits = (flat_routes[:, None] == jnp.arange(EXPERTS, dtype=jnp.int32)[None, :]).astype(
        jnp.int32
    )
    places = jnp.sum((jnp.cumsum(route_hits, axis=0) - 1) * route_hits, axis=1)
    targets = flat_routes * CAP + places
    repeated = jnp.repeat(normed, TOP, axis=0)
    experts_dev = full_pair.shape[1]
    outgoing_rows = (
        jnp.zeros((EXPERTS * CAP, D), jnp.bfloat16)
        .at[targets]
        .set(repeated)
        .reshape(columns, experts_dev, CAP, D)
    )
    arrived = lax.all_to_all(outgoing_rows, "gy", split_axis=0, concat_axis=0, tiled=True)
    gate_pair = jnp.einsum("secd,def->secf", arrived, full_pair, preferred_element_type=jnp.float32)
    hidden = (jax.nn.silu(gate_pair[..., :FF]) * gate_pair[..., FF:]).astype(jnp.bfloat16)
    expert_rows = jnp.einsum(
        "secf,def->secd", hidden, full_down, preferred_element_type=jnp.float32
    ).astype(jnp.bfloat16)
    returned = lax.all_to_all(expert_rows, "gy", split_axis=0, concat_axis=0, tiled=True).reshape(
        EXPERTS * CAP, D
    )
    picked = returned[targets].astype(jnp.float32).reshape(row_count, TOP, D)
    layer_out = stream + jnp.sum(gate_weights[:, :, None] * picked, axis=1)
    return (attended, layer_out)


def solution(mesh):
    placed = (
        P(("gx", "gy"), None),
        P(("gx", "gy"), None),
        P(("gx", "gy"), None, None),
        P(("gx", "gy")),
        P(("gx", "gy"), None),
        P(("gx", "gy")),
        P(("gx", "gy"), None),
        P(("gx", "gy"), None),
        P(("gx", "gy"), None),
        P("gx", None),
        P(),
        P(),
        P(("gx", "gy"), None),
        P("gx", "gy", None),
        P("gx", "gy", None),
    )
    return jax.shard_map(
        body,
        mesh=mesh,
        in_specs=placed,
        out_specs=(P(("gx", "gy"), None), P(("gx", "gy"), None)),
        check_vma=False,
    )
```

profile of v0, /device:TPU:96, one launch (start us, length us, event | category | flops | bytes accessed | tf_op | source)
XLA Modules:
  0.0 342.1 jit_solution(17967935271690350663)
XLA Ops:
  9.7 2.4 pad_maximum_fusion
  13.7 7.0 %all-to-all-start = ((f32[16,1,1537]{2,1,0:T(1,128)}), f32[16,1,1537]{2,1,0:T(1,128)S(1)}, u32[]{:S(2)}, u32[]{:S(2)}) async-start(f32[16,1,1537]{2,1,0:T(1,128)} %copy.120), calls=%async_computation | async-start | bytes 212992 | tf_op jit(solution)/shard_map/all_to_all | solution.py:26
  21.3 16.7 %gather_fusion.1 = bf16[512,16,1024]{2,1,0:T(8,128)(2,1)} fusion(bf16[128,16,1024]{2,1,0:T(8,128)(2,1)} %param.17, s32[1024]{0:T(1024)S(1)} %pad_clamp_fusion.1), kind=kCustom, calls=%fused_computation.1 | custom fusion | bytes 33556480 | tf_op jit(solution)/shard_map/gather | solution.py:134
  38.0 11.6 %fusion.58 = (bf16[16,512,512]{2,1,0:T(8,128)(2,1)}, bf16[16,512,512]{2,1,0:T(8,128)(2,1)}) fusion(bf16[16,512,1024]{2,1,0:T(8,128)(2,1)} %bitcast.81), kind=kLoop, calls=%fused_computation.106 | loop fusion | bytes 33554432 | tf_op jit(solution)/shard_map/slice | solution.py:54
  49.6 12.4 %copy.167 = bf16[16,512,512]{1,2,0:T(8,128)(2,1)} copy(bf16[16,512,512]{2,1,0:T(8,128)(2,1)} %get-tuple-element.8) | data formatting | bytes 16777216
  62.0 12.4 %copy.166 = bf16[16,512,512]{1,2,0:T(8,128)(2,1)} copy(bf16[16,512,512]{2,1,0:T(8,128)(2,1)} %get-tuple-element.7) | data formatting | bytes 16777216
  74.4 11.1 %gather_fusion = bf16[256,16,1024]{2,1,0:T(8,128)(2,1)} fusion(bf16[128,16,1024]{2,1,0:T(8,128)(2,1)} %param.17, s32[1024]{0:T(1024)S(1)} %pad_clamp_fusion.2), kind=kCustom, calls=%fused_computation | custom fusion | bytes 16778240 | tf_op jit(solution)/shard_map/gather | solution.py:107
  85.5 5.8 %fusion.59 = (bf16[8,512,512]{2,1,0:T(8,128)(2,1)}, bf16[8,512,512]{2,1,0:T(8,128)(2,1)}) fusion(bf16[8,512,1024]{2,1,0:T(8,128)(2,1)} %bitcast.83), kind=kLoop, calls=%fused_computation.107 | loop fusion | bytes 16777216 | tf_op jit(solution)/shard_map/slice | solution.py:55
  91.3 6.5 %copy.165 = bf16[8,512,512]{1,2,0:T(8,128)(2,1)} copy(bf16[8,512,512]{2,1,0:T(8,128)(2,1)} %get-tuple-element.10) | data formatting | bytes 8388608
  97.9 2.9 fusion.63
  102.1 6.5 %copy.169 = bf16[8,512,512]{1,2,0:T(8,128)(2,1)} copy(bf16[8,512,512]{2,1,0:T(8,128)(2,1)} %get-tuple-element.9) | data formatting | bytes 8388608
  108.6 3.4 %fusion.32 = f32[8,8,3,64]{3,2,1,0:T(4,128)S(1)} fusion(bf16[8,512,8,64]{1,3,2,0:T(8,128)(2,1)} %bitcast.86, f32[8,8,3,512]{3,2,1,0:T(4,128)S(1)} %get-tuple-element.20, f32[8,8,3]{2,1,0:T(8,128)S(1)} %get-tuple-element.19, pred[8,512]{1,0:T(8,128)(4,1)S(1)} %iota_compare_fusion.3), kind=kOutput, calls=%fused_computation.45 | convolution fusion | flops 12877824 | bytes 4641536 | tf_op jit(solution)/shard_map/nkgt,ntkh->nkgh/dot_general | solution.py:65
  112.4 9.2 %reduce-window.6 = s32[32,8,128]{2,1,0:T(8,128)S(1)} reduce-window(s32[32,8,128]{2,1,0:T(8,128)S(1)} %fusion.39, s32[]{:T(128)} %constant.14.clone.1), window={size=1x1x128 pad=0_0x0_0x127_0}, to_apply=%region_11.12 | reduce-window | flops 4161536 | bytes 262148 | tf_op jit(solution)/shard_map/reduce-window
  122.8 4.7 %fusion.62 = (f32[16,8,3]{2,1,0:T(8,128)S(1)}, f32[16,8,3,512]{3,2,1,0:T(4,128)S(1)}) fusion(bf16[16,8,3,64]{3,2,1,0:T(4,128)(2,1)S(1)} %reshape.235, bf16[16,512,8,64]{1,3,2,0:T(8,128)(2,1)} %bitcast.82, pred[16,512]{1,0:T(8,128)(4,1)S(1)} %broadcast_compare_fusion), kind=kOutput, calls=%fused_computation.110 | convolution fusion | flops 25755264 | bytes 9233920 | tf_op jit(solution)/shard_map/nkgh,ntkh->nkgt/dot_general | solution.py:56
  130.0 5.7 %convolution_bitcast_fusion.1 = f32[16,1,8,3,64]{4,3,2,0,1:T(4,128)S(1)} fusion(bf16[16,512,8,64]{1,3,2,0:T(8,128)(2,1)} %bitcast.84, f32[16,8,3,512]{3,2,1,0:T(4,128)S(1)} %get-tuple-element.18, f32[16,8,3]{2,1,0:T(8,128)S(1)} %get-tuple-element.17, pred[16,512]{1,0:T(8,128)(4,1)S(1)} %broadcast_compare_fusion), kind=kOutput, calls=%fused_computation.30 | convolution fusion | flops 25755648 | bytes 9283072 | tf_op jit(solution)/shard_map/nkgt,ntkh->nkgh/dot_general | solution.py:65
  136.8 7.2 %all-to-all-start.1 = ((f32[16,1,8,3,66]{4,2,3,1,0:T(8,128)}), f32[16,1,8,3,66]{4,2,3,1,0:T(8,128)S(1)}, u32[]{:S(2)}, u32[]{:S(2)}) async-start(f32[16,1,8,3,66]{4,2,3,1,0:T(8,128)} %copy.127), calls=%async_computation.1 | async-start | bytes 393216 | tf_op jit(solution)/shard_map/all_to_all | solution.py:26
  144.0 8.3 %all-to-all-done.1 = f32[16,1,8,3,66]{4,2,3,1,0:T(8,128)S(1)} async-done(((f32[16,1,8,3,66]{4,2,3,1,0:T(8,128)}), f32[16,1,8,3,66]{4,2,3,1,0:T(8,128)S(1)}, u32[]{:S(2)}, u32[]{:S(2)}) %all-to-all-start.1) | async-done | bytes 101408 | tf_op jit(solution)/shard_map/all_to_all | solution.py:26
  157.0 3.2 multiply_reduce_fusion
  161.3 8.4 %scatter_custom_fusion = bf16[1536,1536]{1,0:T(8,128)(2,1)} fusion(s32[1024]{0:T(1024)S(1)} %bitcast.101, bf16[]{:T(256)} %constant.24.clone.1, bf16[128,1536]{1,0:T(8,128)(2,1)S(1)} %multiply_convert_fusion), kind=kCustom, calls=%fused_computation.16 | custom fusion | bytes 5111810 | tf_op jit(solution)/shard_map/scatter | solution.py:188
  169.7 4.6 %all-to-all-start.2 = ((bf16[16,2,48,1536]{3,2,1,0:T(8,128)(2,1)}), bf16[16,2,48,1536]{3,2,1,0:T(8,128)(2,1)}, u32[]{:S(2)}, u32[]{:S(2)}) async-start(bf16[16,2,48,1536]{3,2,1,0:T(8,128)(2,1)} %bitcast.85), calls=%async_computation.2 | async-start | bytes 9437184 | tf_op jit(solution)/shard_map/all_to_all | solution.py:191
  176.1 3.0 copy.171
  179.1 6.6 %split.14 = bf16[1536,2048]{1,0:T(8,128)(2,1)} slice(bf16[1536,4608]{1,0:T(8,128)(2,1)} %all-gather.2.cloned.1.call-done), slice={[0:1536], [1536:3584]} | slice | bytes 12582912 | tf_op jit(solution)/shard_map/split | solution.py:43
  185.7 8.7 %copy.172 = bf16[1536,2048]{0,1:T(8,128)(2,1)} copy(bf16[1536,2048]{1,0:T(8,128)(2,1)} %split.14) | data formatting | bytes 12582912
  194.3 45.8 %all-to-all-done.2 = bf16[16,2,48,1536]{3,2,1,0:T(8,128)(2,1)} async-done(((bf16[16,2,48,1536]{3,2,1,0:T(8,128)(2,1)}), bf16[16,2,48,1536]{3,2,1,0:T(8,128)(2,1)}, u32[]{:S(2)}, u32[]{:S(2)}) %all-to-all-start.2) | async-done | bytes 4718624 | tf_op jit(solution)/shard_map/all_to_all | solution.py:191
  240.1 8.7 %fusion.8 = f32[16,2,48,1024]{3,2,0,1:T(8,128)S(1)} fusion(bf16[1536,2,1024,1]{0,2,3,1:T(8,128)(2,1)} %bitcast.87, bf16[16,2,48,1536]{3,2,1,0:T(8,128)(2,1)} %all-to-all-done.2), kind=kOutput, calls=%fused_computation.18 | convolution fusion | flops 4831838208 | bytes 17301504 | tf_op jit(solution)/shard_map/secd,def->secf/dot_general | solution.py:192
  248.9 2.8 convert_bitcast_fusion
  251.7 2.6 copy.152
  254.3 4.8 %all-to-all-start.3 = ((bf16[16,2,48,1536]{3,2,1,0:T(8,128)(2,1)}), bf16[16,2,48,1536]{3,2,1,0:T(8,128)(2,1)}, u32[]{:S(2)}, u32[]{:S(2)}) async-start(bf16[16,2,48,1536]{3,2,1,0:T(8,128)(2,1)} %copy.152), calls=%async_computation.3 | async-start | bytes 9437184 | tf_op jit(solution)/shard_map/all_to_all | solution.py:197
  259.5 61.2 %all-to-all-done.3 = bf16[16,2,48,1536]{3,2,1,0:T(8,128)(2,1)} async-done(((bf16[16,2,48,1536]{3,2,1,0:T(8,128)(2,1)}), bf16[16,2,48,1536]{3,2,1,0:T(8,128)(2,1)}, u32[]{:S(2)}, u32[]{:S(2)}) %all-to-all-start.3) | async-done | bytes 4718624 | tf_op jit(solution)/shard_map/all_to_all | solution.py:197
  320.7 9.6 %gather_fusion.5 = bf16[1024,1536]{1,0:T(8,128)(2,1)S(1)} fusion(bf16[1536,1536]{1,0:T(8,128)(2,1)} %bitcast.28, s32[1024]{0:T(1024)S(1)} %broadcast_clamp_fusion), kind=kCustom, calls=%fused_computation.5 | custom fusion | bytes 6295552 | tf_op jit(solution)/shard_map/gather | solution.py:200
  330.3 2.8 fusion
  333.1 2.1 add.87
  (129 shorter events, 19.2 us)
Async XLA Ops:
  7.2 251.9 %copy-start = (bf16[1536,32]{0,1:T(8,128)(2,1)S(1)}, bf16[1536,32]{0,1:T(8,128)(2,1)}, u32[]{:S(2)}) copy-start(bf16[1536,32]{0,1:T(8,128)(2,1)} %param.26) | copy-start | bytes 294916
  7.2 4.9 %copy-start.10 = (s32[8]{0:T(128)S(1)}, s32[8]{0:T(128)}, u32[]{:S(2)}) copy-start(s32[8]{0:T(128)} %param.20) | copy-start | bytes 100
  7.2 5.2 %copy-start.13 = (s32[16]{0:T(128)S(1)}, s32[16]{0:T(128)}, u32[]{:S(2)}) copy-start(s32[16]{0:T(128)} %param.18) | copy-start | bytes 196
  7.2 5.5 %copy-start.5 = (bf16[16,1536]{1,0:T(8,128)(2,1)S(1)}, bf16[16,1536]{1,0:T(8,128)(2,1)}, u32[]{:S(2)}) copy-start(bf16[16,1536]{1,0:T(8,128)(2,1)} %param.15) | copy-start | bytes 147460
  7.2 13.7 %copy-start.7 = (s32[128,8]{0,1:T(8,128)S(1)}, s32[128,8]{0,1:T(8,128)}, u32[]{:S(2)}) copy-start(s32[128,8]{0,1:T(8,128)} %param.27) | copy-start | bytes 12292
  7.2 14.0 %copy-start.9 = (s32[16,32]{1,0:T(8,128)S(1)}, s32[16,32]{1,0:T(8,128)}, u32[]{:S(2)}) copy-start(s32[16,32]{1,0:T(8,128)} %param.21) | copy-start | bytes 6148
  7.2 149.8 %all-gather.2.cloned.1.call-start = ((), (), s32[]{:S(2)}) async-start(), calls=%async_computation.4 | async-start | bytes 15925248 | tf_op jit(solution)/shard_map/all_gather | solution.py:42
  13.7 108.4 %all-to-all-start = ((f32[16,1,1537]{2,1,0:T(1,128)}), f32[16,1,1537]{2,1,0:T(1,128)S(1)}, u32[]{:S(2)}, u32[]{:S(2)}) async-start(f32[16,1,1537]{2,1,0:T(1,128)} %copy.120), calls=%async_computation | async-start | bytes 212992 | tf_op jit(solution)/shard_map/all_to_all | solution.py:26
  62.0 12.4 %copy-start.12 = (s32[8,32]{1,0:T(8,128)S(1)}, s32[8,32]{1,0:T(8,128)}, u32[]{:S(2)}) copy-start(s32[8,32]{1,0:T(8,128)} %param.19) | copy-start | bytes 3076
  91.3 6.5 %slice-start.1 = ((bf16[16,1536]{1,0:T(8,128)(2,1)}), bf16[8,1536]{1,0:T(8,128)(2,1)S(1)}, s32[]{:S(2)}) async-start(bf16[16,1536]{1,0:T(8,128)(2,1)} %param.15), calls=%async_computation.6 | async-start | bytes 49152 | tf_op jit(solution)/shard_map/slice | solution.py:112
  97.7 3.8 %copy-start.8 = (bf16[16,1024]{1,0:T(8,128)(2,1)S(1)}, bf16[16,1024]{1,0:T(8,128)(2,1)}, u32[]{:S(2)}) copy-start(bf16[16,1024]{1,0:T(8,128)(2,1)} %param.16) | copy-start | bytes 98308
  108.6 13.3 %copy-start.11 = (bf16[1536]{0:T(1024)(128)(2,1)S(1)}, bf16[1536]{0:T(1024)(128)(2,1)}, u32[]{:S(2)}) copy-start(bf16[1536]{0:T(1024)(128)(2,1)} %param.25) | copy-start | bytes 9220
  135.7 21.3 %copy-start.14 = (bf16[128,1536]{1,0:T(8,128)(2,1)S(1)}, bf16[128,1536]{1,0:T(8,128)(2,1)}, u32[]{:S(2)}) copy-start(bf16[128,1536]{1,0:T(8,128)(2,1)} %param.23) | copy-start | bytes 1179652
  135.7 21.3 %copy-start.15 = (bf16[112,1536]{1,0:T(8,128)(2,1)S(1)}, bf16[112,1536]{1,0:T(8,128)(2,1)}, u32[]{:S(2)}) copy-start(bf16[112,1536]{1,0:T(8,128)(2,1)} %param.22) | copy-start | bytes 1032196
  136.8 15.5 %all-to-all-start.1 = ((f32[16,1,8,3,66]{4,2,3,1,0:T(8,128)}), f32[16,1,8,3,66]{4,2,3,1,0:T(8,128)S(1)}, u32[]{:S(2)}, u32[]{:S(2)}) async-start(f32[16,1,8,3,66]{4,2,3,1,0:T(8,128)} %copy.127), calls=%async_computation.1 | async-start | bytes 393216 | tf_op jit(solution)/shard_map/all_to_all | solution.py:26
  157.0 12.7 %copy-start.6 = (bf16[16,1536]{1,0:T(8,128)(2,1)}, bf16[16,1536]{1,0:T(8,128)(2,1)S(1)}, u32[]{:S(2)}) copy-start(bf16[16,1536]{1,0:T(8,128)(2,1)S(1)} %fusion.43) | copy-start | bytes 147460
  160.3 0.9 copy-start.4
  161.3 8.4 %copy-start.1 = (bf16[128,1536]{1,0:T(8,128)(2,1)}, bf16[128,1536]{1,0:T(8,128)(2,1)S(1)}, u32[]{:S(2)}) copy-start(bf16[128,1536]{1,0:T(8,128)(2,1)S(1)} %multiply_convert_fusion) | copy-start | bytes 1179652
  169.7 70.5 %all-to-all-start.2 = ((bf16[16,2,48,1536]{3,2,1,0:T(8,128)(2,1)}), bf16[16,2,48,1536]{3,2,1,0:T(8,128)(2,1)}, u32[]{:S(2)}, u32[]{:S(2)}) async-start(bf16[16,2,48,1536]{3,2,1,0:T(8,128)(2,1)} %bitcast.85), calls=%async_computation.2 | async-start | bytes 9437184 | tf_op jit(solution)/shard_map/all_to_all | solution.py:191
  174.2 1.9 slice-start
  240.1 8.7 %copy-start.3 = (bf16[1536,1024]{0,1:T(8,128)(2,1)S(1)}, bf16[1536,1024]{0,1:T(8,128)(2,1)}, u32[]{:S(2)}) copy-start(bf16[1536,1024]{0,1:T(8,128)(2,1)} %copy.171) | copy-start | bytes 9437188
  254.3 4.8 %copy-start.2 = (bf16[128,1536]{1,0:T(8,128)(2,1)S(1)}, bf16[128,1536]{1,0:T(8,128)(2,1)}, u32[]{:S(2)}) copy-start(bf16[128,1536]{1,0:T(8,128)(2,1)} %copy-done.1) | copy-start | bytes 1179652
  254.3 66.4 %all-to-all-start.3 = ((bf16[16,2,48,1536]{3,2,1,0:T(8,128)(2,1)}), bf16[16,2,48,1536]{3,2,1,0:T(8,128)(2,1)}, u32[]{:S(2)}, u32[]{:S(2)}) async-start(bf16[16,2,48,1536]{3,2,1,0:T(8,128)(2,1)} %copy.152), calls=%async_computation.3 | async-start | bytes 9437184 | tf_op jit(solution)/shard_map/all_to_all | solution.py:197
Sparse Core Ops, SparseCore 0:
  12.2 73.2 all-gather.1
where the time goes:
time: 344 us; the launch traced here: 342 us
  local copies, waits for them, and re-layouts  137 us (40%)
  waiting for transfers between devices  115 us (33%)
  matrix products  32.3 us (9%)
  starting transfers between devices  23.6 us (7%)
  other arithmetic  19.4 us (6%)
  between operations  14.5 us (4%)
    all_to_all x1, waiting for transfers between devices, body(): lax.all_to_all(expert_rows, 'gy', split_axis=0, concat_axis=0, tiled=True)  61.2 us
    unnamed x43, local copies, waits for them, and re-layouts  53.1 us
    all_to_all x1, waiting for transfers between devices, body(): lax.all_to_all(outgoing_rows, 'gy', split_axis=0, concat_axis=0, tiled=True)  45.8 us
    gather x1, local copies, waits for them, and re-layouts, body(): cache_pool[push_pages].reshape(columns * slot_count, MAXLEN, kv_width)  16.7 us
    all_to_all x2, starting transfers between devices, in_one_piece(): lax.all_to_all(both, axis, split_axis=split_dim, concat_axis=concat_dim,...  14.2 us
    slice x1, local copies, waits for them, and re-layouts, partial_attend(): keyval[:, :, :half_width].reshape(count_req, positions, kv_count, head_size)  11.6 us
    gather x1, local copies, waits for them, and re-layouts, body(): local_kv = cache_pool[local_pages].reshape(LOCAL, MAXLEN, kv_width)  11.1 us
    gather x1, local copies, waits for them, and re-layouts, body(): picked = returned[targets].astype(jnp.float32).reshape(row_count, TOP, D)  9.6 us
  transfers between devices with their start and end apart: 5, of which 3 were waited for; matrix products, arithmetic and copies ran while one was open for 41% of the time, Pallas kernels for 0%

commit v1 on v0

--- a/solution.py
+++ b/solution.py
@@ -4,6 +4,8 @@
 import jax.numpy as jnp
 from jax import lax
 from jax.sharding import PartitionSpec as P
+from jax.experimental import pallas as pl
+from jax.experimental.pallas import tpu as pltpu
 
 D = 1536
 HEADS = 24
@@ -17,6 +19,102 @@
 LOCAL = 8
 MOVED = 8
 CAP = 48
+NPAGE = 32
+PAGE = 16
+
+
+def attend_kernel(tables, lengths, q_ref, pool_ref, max_ref, tot_ref, mix_ref, kvbuf, sems):
+    r = pl.program_id(0)
+    n = pl.num_programs(0)
+    half = KV_HEADS * HEAD
+
+    def start(req, slot):
+        def one(p, carry):
+            pltpu.make_async_copy(
+                pool_ref.at[tables[req, p]], kvbuf.at[slot, p], sems.at[slot]
+            ).start()
+            return carry
+
+        lax.fori_loop(0, NPAGE, one, 0, unroll=8)
+
+    @pl.when(r == 0)
+    def _():
+        start(0, 0)
+
+    slot = r % 2
+
+    @pl.when(r + 1 < n)
+    def _():
+        start(r + 1, 1 - slot)
+
+    pltpu.make_async_copy(pool_ref.at[pl.ds(0, NPAGE)], kvbuf.at[slot], sems.at[slot]).wait()
+    kv = kvbuf.at[slot]
+    keys = kv[:, :, :half].reshape(MAXLEN, half)
+    values = kv[:, :, half:].reshape(MAXLEN, half)
+    q = q_ref[0]
+    scores = lax.dot_general(
+        q, keys, (((1,), (1,)), ((), ())), preferred_element_type=jnp.float32
+    ) * (1.0 / math.sqrt(HEAD))
+    valid = lax.broadcasted_iota(jnp.int32, scores.shape, 1) < lengths[r]
+    masked = jnp.where(valid, scores, -1e30)
+    top = jnp.max(masked, axis=1, keepdims=True)
+    expos = jnp.where(valid, jnp.exp(masked - top), 0.0)
+    total = jnp.sum(expos, axis=1, keepdims=True)
+    mix = jnp.dot(expos.astype(jnp.bfloat16), values, preferred_element_type=jnp.float32)
+    max_ref[0] = jnp.broadcast_to(top, max_ref.shape[1:])
+    tot_ref[0] = jnp.broadcast_to(total, tot_ref.shape[1:])
+    mix_ref[0] = mix
+
+
+def paged_attend(query_rows, tables, lengths, pool):
+    count = query_rows.shape[0]
+    group_size = HEADS // KV_HEADS
+    half = KV_HEADS * HEAD
+    heads = query_rows.reshape(count, KV_HEADS, group_size, 1, HEAD)
+    mask = (jnp.arange(KV_HEADS)[:, None] == jnp.arange(KV_HEADS)[None, :])
+    spread = jnp.where(
+        mask[None, :, None, :, None], heads, jnp.zeros((), query_rows.dtype)
+    ).reshape(count, HEADS, half)
+    kv_width = pool.shape[2]
+    grid_spec = pltpu.PrefetchScalarGridSpec(
+        num_scalar_prefetch=2,
+        grid=(count,),
+        in_specs=[
+            pl.BlockSpec((1, HEADS, half), lambda r, t, l: (r, 0, 0)),
+            pl.BlockSpec(memory_space=pl.ANY),
+        ],
+        out_specs=[
+            pl.BlockSpec((1, HEADS, 128), lambda r, t, l: (r, 0, 0)),
+            pl.BlockSpec((1, HEADS, 128), lambda r, t, l: (r, 0, 0)),
+            pl.BlockSpec((1, HEADS, half), lambda r, t, l: (r, 0, 0)),
+        ],
+        scratch_shapes=[
+            pltpu.VMEM((2, NPAGE, PAGE, kv_width), pool.dtype),
+            pltpu.SemaphoreType.DMA((2,)),
+        ],
+    )
+    top, total, mix = pl.pallas_call(
+        attend_kernel,
+        grid_spec=grid_spec,
+        out_shape=[
+            jax.ShapeDtypeStruct((count, HEADS, 128), jnp.float32),
+            jax.ShapeDtypeStruct((count, HEADS, 128), jnp.float32),
+            jax.ShapeDtypeStruct((count, HEADS, half), jnp.float32),
+        ],
+        compiler_params=pltpu.CompilerParams(dimension_semantics=("arbitrary",)),
+        cost_estimate=pl.CostEstimate(
+            flops=count * 4 * HEADS * MAXLEN * half,
+            transcendentals=count * HEADS * MAXLEN,
+            bytes_accessed=count * MAXLEN * kv_width * 2,
+        ),
+    )(tables, lengths, spread, pool)
+    blocks = mix.reshape(count, KV_HEADS, group_size, KV_HEADS, HEAD)
+    mixture = jnp.sum(jnp.where(mask[None, :, None, :, None], blocks, 0.0), axis=3)
+    return (
+        top[:, :, 0].reshape(count, KV_HEADS, group_size),
+        total[:, :, 0].reshape(count, KV_HEADS, group_size),
+        mixture,
+    )
 
 
 def in_one_piece(arrays, axis, split_dim, concat_dim, along):
@@ -104,12 +202,11 @@
     group_size = HEADS // KV_HEADS
     kv_width = 2 * KV_HEADS * HEAD
     query_heads = queries.reshape(R_DEV, KV_HEADS, group_size, HEAD)
-    local_kv = cache_pool[local_pages].reshape(LOCAL, MAXLEN, kv_width)
     matches = (anchor[:, None] == jnp.arange(columns, dtype=jnp.int32)[None, :]).astype(jnp.int32)
     earlier = jnp.sum((jnp.cumsum(matches, axis=0) - 1) * matches, axis=1)
     chosen = anchor * slot_count + earlier
-    local_max, local_totals, local_mix = partial_attend(
-        query_heads[:LOCAL], local_kv, cache_len[:LOCAL]
+    local_max, local_totals, local_mix = paged_attend(
+        queries[:LOCAL], local_pages, cache_len[:LOCAL], cache_pool
     )
     picker = chosen[:, None] == jnp.arange(columns * slot_count, dtype=jnp.int32)[None, :]
     sent_queries = jnp.einsum(
@@ -128,12 +225,11 @@
         0,
         2,
     )
-    far_heads = got_queries.astype(jnp.bfloat16).reshape(
-        columns * slot_count, KV_HEADS, group_size, HEAD
-    )
-    far_kv = cache_pool[push_pages].reshape(columns * slot_count, MAXLEN, kv_width)
-    far_max, far_totals, far_mix = partial_attend(
-        far_heads, far_kv, got_lengths.reshape(columns * slot_count)
+    far_max, far_totals, far_mix = paged_attend(
+        got_queries.astype(jnp.bfloat16).reshape(columns * slot_count, D),
+        push_pages,
+        got_lengths.reshape(columns * slot_count).astype(jnp.int32),
+        cache_pool,
     )
     back_max, back_totals, back_mix = in_one_piece(
         (

time: 344 us -> 288 us (0.84)
  local copies, waits for them, and re-layouts: 137 us -> 61 us
  Pallas kernels: 0 us -> 28 us
  matrix products: 32.3 us -> 15.5 us
  waiting for transfers between devices: 115 us -> 120 us
    unnamed x43 -> x37, local copies, waits for them, and re-layouts: 53.1 us -> 15.5 us
    pallas_call x0 -> x2, Pallas kernels: none -> 28 us  [paged_attend(): pl.pallas_call(attend_kernel, grid_spec=grid_spec, out_shape=[jax.ShapeDt...]
    gather x2 -> x0, local copies, waits for them, and re-layouts: 27.8 us -> none  [the longest x1 16.7 us: body(): cache_pool[push_pages].reshape(columns * slot_count, MAXLEN, kv_width)]
    dot_general x4 -> x0, matrix products: 16.8 us -> none  [the longest x2 9.14 us: partial_attend(): jnp.einsum('nkgt,ntkh->nkgh', weights, value_rows, preferred_element_type...]
    slice x7 -> x8, local copies, waits for them, and re-layouts: 17.7 us -> 4.48 us  [the longest x2 2.13 us: paged_attend(): top[:, :, 0].reshape(count, KV_HEADS, group_size)]
  transfers between devices with their start and end apart: 5 -> 5, of which waited for: 3 -> 3; matrix products, arithmetic and copies ran while one was open for 41% -> 18% of each run, Pallas kernels for 0% -> 10%
where the time goes in v1:
time: 288 us; the launch traced here: 284 us
  waiting for transfers between devices  120 us (42%)
  local copies, waits for them, and re-layouts  61 us (21%)
  Pallas kernels  28 us (10%)
  starting transfers between devices  23.9 us (8%)
  other arithmetic  20.5 us (7%)
  matrix products  15.5 us (5%)
  between operations  14.6 us (5%)
    all_to_all x1, waiting for transfers between devices, body(): lax.all_to_all(expert_rows, 'gy', split_axis=0, concat_axis=0, tiled=True)  64.2 us
    all_to_all x1, waiting for transfers between devices, body(): lax.all_to_all(outgoing_rows, 'gy', split_axis=0, concat_axis=0, tiled=True)  47.8 us
    pallas_call x2, Pallas kernels, paged_attend(): pl.pallas_call(attend_kernel, grid_spec=grid_spec, out_shape=[jax.ShapeDt...  28 us
    unnamed x37, local copies, waits for them, and re-layouts  15.5 us
    all_to_all x2, starting transfers between devices, in_one_piece(): lax.all_to_all(both, axis, split_axis=split_dim, concat_axis=concat_dim,...  14.1 us
    gather x1, local copies, waits for them, and re-layouts, body(): picked = returned[targets].astype(jnp.float32).reshape(row_count, TOP, D)  9.6 us
    another operation x2, other arithmetic  9.04 us
    dot_general x1, matrix products, body(): jnp.einsum('secd,def->secf', arrived, full_pair, preferred_element_type=j...  8.73 us
  transfers between devices with their start and end apart: 5, of which 3 were waited for; matrix products, arithmetic and copies ran while one was open for 18% of the time, Pallas kernels for 10%

profile of v1, /device:TPU:96, one launch (start us, length us, event | category | flops | bytes accessed | tf_op | source)
XLA Modules:
  0.0 283.8 jit_solution(10306452981660409994)
XLA Ops:
  7.2 1.0 copy.164
  8.3 1.3 copy.163
  9.7 2.4 pad_maximum_fusion
  14.1 7.0 %all-to-all-start = ((f32[16,1,1537]{2,1,0:T(1,128)}), f32[16,1,1537]{2,1,0:T(1,128)S(1)}, u32[]{:S(2)}, u32[]{:S(2)}) async-start(f32[16,1,1537]{2,1,0:T(1,128)} %copy.115), calls=%async_computation | async-start | bytes 212992 | tf_op jit(solution)/shard_map/all_to_all | solution.py:124
  23.0 10.4 %shard_map.158 = (f32[8,24,128]{2,1,0:T(8,128)}, f32[8,24,128]{2,1,0:T(8,128)}, f32[8,24,512]{2,1,0:T(8,128)}) custom-call(s32[8,32]{1,0:T(8,128)} %tables.2, s32[8]{0:T(128)} %get-tuple-element.28.lengths, bf16[8,24,512]{2,1,0:T(8,128)(2,1)} %broadcast_select_fusion.1.q_ref, bf16[128,16,1024]{2,1,0:T(8,128)(2,1)} %pool_ref.3), custom_call_target="tpu_custom_call" | custom-call | flops 201326592 | bytes 8388608 | tf_op jit(solution)/shard_map/pallas_call | solution.py:96
  33.4 1.0 slice_reduce_fusion
  35.1 1.0 slice_reduce_fusion.1
  36.4 1.2 reshape.195
  37.8 9.0 %reduce-window.6 = s32[32,8,128]{2,1,0:T(8,128)S(1)} reduce-window(s32[32,8,128]{2,1,0:T(8,128)S(1)} %fusion.23, s32[]{:T(128)} %constant.13.clone.1), window={size=1x1x128 pad=0_0x0_0x127_0}, to_apply=%region_9.10 | reduce-window | flops 4161536 | bytes 262148 | tf_op jit(solution)/shard_map/reduce-window
  48.9 0.9 fusion.32.lengths
  50.6 17.6 %shard_map.159 = (f32[16,24,128]{2,1,0:T(8,128)}, f32[16,24,128]{2,1,0:T(8,128)}, f32[16,24,512]{2,1,0:T(8,128)}) custom-call(s32[16,32]{1,0:T(8,128)} %tables.3, s32[16]{0:T(128)} %fusion.32.lengths, bf16[16,24,512]{2,1,0:T(8,128)(2,1)} %broadcast_select_fusion.q_ref, bf16[128,16,1024]{2,1,0:T(8,128)(2,1)} %pool_ref.3), custom_call_target="tpu_custom_call" | custom-call | flops 402653184 | bytes 16777216 | tf_op jit(solution)/shard_map/pallas_call | solution.py:96
  68.2 1.5 reshape.191
  69.7 1.1 copy.117
  71.2 1.1 copy.116
  74.4 7.0 %all-to-all-start.1 = ((f32[16,1,8,3,66]{4,2,3,1,0:T(8,128)}), f32[16,1,8,3,66]{4,2,3,1,0:T(8,128)S(1)}, u32[]{:S(2)}, u32[]{:S(2)}) async-start(f32[16,1,8,3,66]{4,2,3,1,0:T(8,128)} %copy.120), calls=%async_computation.1 | async-start | bytes 393216 | tf_op jit(solution)/shard_map/all_to_all | solution.py:124
  81.4 8.3 %all-to-all-done.1 = f32[16,1,8,3,66]{4,2,3,1,0:T(8,128)S(1)} async-done(((f32[16,1,8,3,66]{4,2,3,1,0:T(8,128)}), f32[16,1,8,3,66]{4,2,3,1,0:T(8,128)S(1)}, u32[]{:S(2)}, u32[]{:S(2)}) %all-to-all-start.1) | async-done | bytes 101408 | tf_op jit(solution)/shard_map/all_to_all | solution.py:124
  94.5 3.2 %multiply_reduce_fusion = (f32[128]{0:T(128)S(1)}, f32[128,1536]{1,0:T(8,128)S(1)}) fusion(bf16[1536,4608]{1,0:T(8,128)(2,1)} %all-gather.2.cloned.1.call-done, bf16[112,1536]{1,0:T(8,128)(2,1)S(1)} %copy-done.14, bf16[16,1536]{1,0:T(8,128)(2,1)S(1)} %fusion.27, bf16[128,1536]{1,0:T(8,128)(2,1)S(1)} %copy-done.13), kind=kOutput, calls=%fused_computation.25 | convolution fusion | flops 605552512 | bytes 6291968 | tf_op jit(solution)/shard_map/dot_general | solution.py:260
  98.7 8.4 %scatter_custom_fusion = bf16[1536,1536]{1,0:T(8,128)(2,1)} fusion(s32[1024]{0:T(1024)S(1)} %bitcast.93, bf16[]{:T(256)} %constant.12.clone.1, bf16[128,1536]{1,0:T(8,128)(2,1)S(1)} %multiply_convert_fusion), kind=kCustom, calls=%fused_computation.14 | custom fusion | bytes 5111810 | tf_op jit(solution)/shard_map/scatter | solution.py:284
  107.1 4.8 %all-to-all-start.2 = ((bf16[16,2,48,1536]{3,2,1,0:T(8,128)(2,1)}), bf16[16,2,48,1536]{3,2,1,0:T(8,128)(2,1)}, u32[]{:S(2)}, u32[]{:S(2)}) async-start(bf16[16,2,48,1536]{3,2,1,0:T(8,128)(2,1)} %bitcast.75), calls=%async_computation.2 | async-start | bytes 9437184 | tf_op jit(solution)/shard_map/all_to_all | solution.py:287
  111.9 1.9 slice-done
  113.7 3.0 %copy.161 = bf16[1536,1024]{0,1:T(8,128)(2,1)} copy(bf16[1536,1024]{1,0:T(8,128)(2,1)S(1)} %slice-done) | data formatting | bytes 6291456
  116.7 6.5 %split.14 = bf16[1536,2048]{1,0:T(8,128)(2,1)} slice(bf16[1536,4608]{1,0:T(8,128)(2,1)} %all-gather.2.cloned.1.call-done), slice={[0:1536], [1536:3584]} | slice | bytes 12582912 | tf_op jit(solution)/shard_map/split | solution.py:141
  123.2 8.7 %copy.162 = bf16[1536,2048]{0,1:T(8,128)(2,1)} copy(bf16[1536,2048]{1,0:T(8,128)(2,1)} %split.14) | data formatting | bytes 12582912
  131.9 47.8 %all-to-all-done.2 = bf16[16,2,48,1536]{3,2,1,0:T(8,128)(2,1)} async-done(((bf16[16,2,48,1536]{3,2,1,0:T(8,128)(2,1)}), bf16[16,2,48,1536]{3,2,1,0:T(8,128)(2,1)}, u32[]{:S(2)}, u32[]{:S(2)}) %all-to-all-start.2) | async-done | bytes 4718624 | tf_op jit(solution)/shard_map/all_to_all | solution.py:287
  179.7 8.7 %fusion.8 = f32[16,2,48,1024]{3,2,0,1:T(8,128)S(1)} fusion(bf16[1536,2,1024,1]{0,2,3,1:T(8,128)(2,1)} %bitcast.76, bf16[16,2,48,1536]{3,2,1,0:T(8,128)(2,1)} %all-to-all-done.2), kind=kOutput, calls=%fused_computation.16 | convolution fusion | flops 4831838208 | bytes 17301504 | tf_op jit(solution)/shard_map/secd,def->secf/dot_general | solution.py:288
  188.4 2.8 %convert_bitcast_fusion = bf16[16,2,48,1536]{3,2,0,1:T(8,128)(2,1)S(1)} fusion(bf16[1536,2,512,1]{0,2,3,1:T(8,128)(2,1)S(1)} %bitcast.78, f32[16,2,48,1024]{3,2,0,1:T(8,128)S(1)} %fusion.8), kind=kOutput, calls=%fused_computation.11 | convolution fusion | flops 2422996992 | bytes 14155776 | tf_op jit(solution)/shard_map/secf,def->secd/dot_general | solution.py:290
  191.3 2.6 copy.146
  193.9 5.0 %all-to-all-start.3 = ((bf16[16,2,48,1536]{3,2,1,0:T(8,128)(2,1)}), bf16[16,2,48,1536]{3,2,1,0:T(8,128)(2,1)}, u32[]{:S(2)}, u32[]{:S(2)}) async-start(bf16[16,2,48,1536]{3,2,1,0:T(8,128)(2,1)} %copy.146), calls=%async_computation.3 | async-start | bytes 9437184 | tf_op jit(solution)/shard_map/all_to_all | solution.py:293
  199.4 64.2 %all-to-all-done.3 = bf16[16,2,48,1536]{3,2,1,0:T(8,128)(2,1)} async-done(((bf16[16,2,48,1536]{3,2,1,0:T(8,128)(2,1)}), bf16[16,2,48,1536]{3,2,1,0:T(8,128)(2,1)}, u32[]{:S(2)}, u32[]{:S(2)}) %all-to-all-start.3) | async-done | bytes 4718624 | tf_op jit(solution)/shard_map/all_to_all | solution.py:293
  263.6 9.6 %gather_fusion.3 = bf16[1024,1536]{1,0:T(8,128)(2,1)S(1)} fusion(bf16[1536,1536]{1,0:T(8,128)(2,1)} %bitcast.22, s32[1024]{0:T(1024)S(1)} %broadcast_clamp_fusion), kind=kCustom, calls=%fused_computation.3 | custom fusion | bytes 6295552 | tf_op jit(solution)/shard_map/gather | solution.py:296
  273.2 2.8 fusion
  276.0 1.0 add.71
  (125 shorter events, 16.3 us)
Async XLA Ops:
  7.2 191.8 %copy-start = (bf16[1536,32]{0,1:T(8,128)(2,1)S(1)}, bf16[1536,32]{0,1:T(8,128)(2,1)}, u32[]{:S(2)}) copy-start(bf16[1536,32]{0,1:T(8,128)(2,1)} %param.26) | copy-start | bytes 294916
  7.2 87.3 %all-gather.2.cloned.1.call-start = ((), (), s32[]{:S(2)}) async-start(), calls=%async_computation.4 | async-start | bytes 15925248 | tf_op jit(solution)/shard_map/all_gather | solution.py:140
  8.3 3.8 %copy-start.10 = (s32[8]{0:T(128)S(1)}, s32[8]{0:T(128)}, u32[]{:S(2)}) copy-start(s32[8]{0:T(128)} %param.20) | copy-start | bytes 100
  8.3 4.1 %copy-start.12 = (s32[16]{0:T(128)S(1)}, s32[16]{0:T(128)}, u32[]{:S(2)}) copy-start(s32[16]{0:T(128)} %param.18) | copy-start | bytes 196
  8.3 4.8 %copy-start.6 = (bf16[16,1536]{1,0:T(8,128)(2,1)S(1)}, bf16[16,1536]{1,0:T(8,128)(2,1)}, u32[]{:S(2)}) copy-start(bf16[16,1536]{1,0:T(8,128)(2,1)} %param.15) | copy-start | bytes 147460
  9.7 11.7 %copy-start.8 = (s32[128,8]{0,1:T(8,128)S(1)}, s32[128,8]{0,1:T(8,128)}, u32[]{:S(2)}) copy-start(s32[128,8]{0,1:T(8,128)} %param.27) | copy-start | bytes 12292
  9.7 12.2 %slice-start.1 = ((bf16[16,1536]{1,0:T(8,128)(2,1)}), bf16[8,1536]{1,0:T(8,128)(2,1)S(1)}, s32[]{:S(2)}) async-start(bf16[16,1536]{1,0:T(8,128)(2,1)} %param.15), calls=%async_computation.6 | async-start | bytes 49152 | tf_op jit(solution)/shard_map/slice | solution.py:209
  13.4 21.2 %copy-start.9 = (bf16[16,1024]{1,0:T(8,128)(2,1)S(1)}, bf16[16,1024]{1,0:T(8,128)(2,1)}, u32[]{:S(2)}) copy-start(bf16[16,1024]{1,0:T(8,128)(2,1)} %param.16) | copy-start | bytes 98308
  14.1 33.7 %all-to-all-start = ((f32[16,1,1537]{2,1,0:T(1,128)}), f32[16,1,1537]{2,1,0:T(1,128)S(1)}, u32[]{:S(2)}, u32[]{:S(2)}) async-start(f32[16,1,1537]{2,1,0:T(1,128)} %copy.115), calls=%async_computation | async-start | bytes 212992 | tf_op jit(solution)/shard_map/all_to_all | solution.py:124
  33.4 14.5 %copy-start.11 = (bf16[1536]{0:T(1024)(128)(2,1)S(1)}, bf16[1536]{0:T(1024)(128)(2,1)}, u32[]{:S(2)}) copy-start(bf16[1536]{0:T(1024)(128)(2,1)} %param.25) | copy-start | bytes 9220
  73.3 21.1 %copy-start.13 = (bf16[128,1536]{1,0:T(8,128)(2,1)S(1)}, bf16[128,1536]{1,0:T(8,128)(2,1)}, u32[]{:S(2)}) copy-start(bf16[128,1536]{1,0:T(8,128)(2,1)} %param.23) | copy-start | bytes 1179652
  73.3 21.1 %copy-start.14 = (bf16[112,1536]{1,0:T(8,128)(2,1)S(1)}, bf16[112,1536]{1,0:T(8,128)(2,1)}, u32[]{:S(2)}) copy-start(bf16[112,1536]{1,0:T(8,128)(2,1)} %param.22) | copy-start | bytes 1032196
  74.4 15.4 %all-to-all-start.1 = ((f32[16,1,8,3,66]{4,2,3,1,0:T(8,128)}), f32[16,1,8,3,66]{4,2,3,1,0:T(8,128)S(1)}, u32[]{:S(2)}, u32[]{:S(2)}) async-start(f32[16,1,8,3,66]{4,2,3,1,0:T(8,128)} %copy.120), calls=%async_computation.1 | async-start | bytes 393216 | tf_op jit(solution)/shard_map/all_to_all | solution.py:124
  94.4 3.3 %copy-start.7 = (bf16[16,1536]{1,0:T(8,128)(2,1)}, bf16[16,1536]{1,0:T(8,128)(2,1)S(1)}, u32[]{:S(2)}) copy-start(bf16[16,1536]{1,0:T(8,128)(2,1)S(1)} %fusion.27) | copy-start | bytes 147460
  97.7 0.9 copy-start.4
  98.7 8.4 %copy-start.1 = (bf16[128,1536]{1,0:T(8,128)(2,1)}, bf16[128,1536]{1,0:T(8,128)(2,1)S(1)}, u32[]{:S(2)}) copy-start(bf16[128,1536]{1,0:T(8,128)(2,1)S(1)} %multiply_convert_fusion) | copy-start | bytes 1179652
  107.1 72.6 %all-to-all-start.2 = ((bf16[16,2,48,1536]{3,2,1,0:T(8,128)(2,1)}), bf16[16,2,48,1536]{3,2,1,0:T(8,128)(2,1)}, u32[]{:S(2)}, u32[]{:S(2)}) async-start(bf16[16,2,48,1536]{3,2,1,0:T(8,128)(2,1)} %bitcast.75), calls=%async_computation.2 | async-start | bytes 9437184 | tf_op jit(solution)/shard_map/all_to_all | solution.py:287
  111.9 1.9 slice-start
  179.7 8.7 %copy-start.3 = (bf16[1536,1024]{0,1:T(8,128)(2,1)S(1)}, bf16[1536,1024]{0,1:T(8,128)(2,1)}, u32[]{:S(2)}) copy-start(bf16[1536,1024]{0,1:T(8,128)(2,1)} %copy.161) | copy-start | bytes 9437188
  193.9 5.1 %copy-start.2 = (bf16[128,1536]{1,0:T(8,128)(2,1)S(1)}, bf16[128,1536]{1,0:T(8,128)(2,1)}, u32[]{:S(2)}) copy-start(bf16[128,1536]{1,0:T(8,128)(2,1)} %copy-done.1) | copy-start | bytes 1179652
  193.9 69.7 %all-to-all-start.3 = ((bf16[16,2,48,1536]{3,2,1,0:T(8,128)(2,1)}), bf16[16,2,48,1536]{3,2,1,0:T(8,128)(2,1)}, u32[]{:S(2)}, u32[]{:S(2)}) async-start(bf16[16,2,48,1536]{3,2,1,0:T(8,128)(2,1)} %copy.146), calls=%async_computation.3 | async-start | bytes 9437184 | tf_op jit(solution)/shard_map/all_to_all | solution.py:293
  273.2 2.8 copy-start.5
Sparse Core Ops, SparseCore 0:
  12.2 73.3 all-gather.1

commit v2 on v1

--- a/solution.py
+++ b/solution.py
@@ -256,7 +256,9 @@
     attended = finish(query_heads, new_kv, cache_max, totals, mixture)
     tokens = jnp.concatenate([attended, prefill_attn], axis=0)
     row_count = tokens.shape[0]
-    full_out, full_pair, full_down = side_by_side((out_weight, gate_up, down_proj), "gx", 0, 1)
+    full_out = lax.all_gather(out_weight, "gx", axis=0, tiled=True)
+    full_pair = lax.all_gather(gate_up, "gx", axis=0, tiled=True)
+    full_down = lax.all_gather(down_proj, "gx", axis=0, tiled=True)
     stream = residual.astype(jnp.float32) + jnp.dot(
         tokens, full_out, preferred_element_type=jnp.float32
     )
@@ -270,31 +272,28 @@
     gate_weights = jax.nn.softmax(
         jnp.sum(jnp.where(selector, logits[:, None, :], 0.0), axis=2), axis=1
     )
-    flat_routes = routes.reshape(row_count * TOP)
-    route_hits = (flat_routes[:, None] == jnp.arange(EXPERTS, dtype=jnp.int32)[None, :]).astype(
-        jnp.int32
-    )
-    places = jnp.sum((jnp.cumsum(route_hits, axis=0) - 1) * route_hits, axis=1)
-    targets = flat_routes * CAP + places
-    repeated = jnp.repeat(normed, TOP, axis=0)
+    dense_gates = jnp.where(
+        jnp.any(selector, axis=1),
+        jnp.sum(jnp.where(selector, gate_weights[:, :, None], 0.0), axis=1),
+        -1.0,
+    )
     experts_dev = full_pair.shape[1]
-    outgoing_rows = (
-        jnp.zeros((EXPERTS * CAP, D), jnp.bfloat16)
-        .at[targets]
-        .set(repeated)
-        .reshape(columns, experts_dev, CAP, D)
-    )
-    arrived = lax.all_to_all(outgoing_rows, "gy", split_axis=0, concat_axis=0, tiled=True)
-    gate_pair = jnp.einsum("secd,def->secf", arrived, full_pair, preferred_element_type=jnp.float32)
+    all_normed = lax.all_gather(normed, "gy", axis=0, tiled=True)
+    all_gates = lax.all_gather(dense_gates, "gy", axis=0, tiled=True)
+    first = lax.axis_index("gy") * experts_dev
+    my_gates = lax.dynamic_slice_in_dim(all_gates, first, experts_dev, axis=1)
+    my_routed = my_gates >= 0.0
+    gate_pair = jnp.einsum("rd,def->ref", all_normed, full_pair, preferred_element_type=jnp.float32)
     hidden = (jax.nn.silu(gate_pair[..., :FF]) * gate_pair[..., FF:]).astype(jnp.bfloat16)
     expert_rows = jnp.einsum(
-        "secf,def->secd", hidden, full_down, preferred_element_type=jnp.float32
+        "ref,def->red", hidden, full_down, preferred_element_type=jnp.float32
     ).astype(jnp.bfloat16)
-    returned = lax.all_to_all(expert_rows, "gy", split_axis=0, concat_axis=0, tiled=True).reshape(
-        EXPERTS * CAP, D
-    )
-    picked = returned[targets].astype(jnp.float32).reshape(row_count, TOP, D)
-    layer_out = stream + jnp.sum(gate_weights[:, :, None] * picked, axis=1)
+    partial = jnp.sum(
+        jnp.where(my_routed[..., None], my_gates[..., None] * expert_rows.astype(jnp.float32), 0.0),
+        axis=1,
+    )
+    mixed = lax.psum_scatter(partial, "gy", scatter_dimension=0, tiled=True)
+    layer_out = stream + mixed
     return (attended, layer_out)
 
 

time: 288 us -> 308 us (1.069)
  local copies, waits for them, and re-layouts: 61 us -> 20.9 us
  waiting for transfers between devices: 120 us -> 149 us
  matrix products: 15.5 us -> 43.6 us
  blocking collectives: 0 us -> 22.3 us
  starting transfers between devices: 23.9 us -> 13.8 us
  other arithmetic: 20.5 us -> 11.6 us
    all_to_all x2 -> x0, waiting for transfers between devices: 112 us -> none  [the longest x1 64.2 us: body(): lax.all_to_all(expert_rows, 'gy', split_axis=0, concat_axis=0, tiled=True)]
    reduce_scatter x0 -> x1, waiting for transfers between devices: none -> 95.6 us  [body(): mixed = lax.psum_scatter(partial, 'gy', scatter_dimension=0, tiled=True)]
    all_gather x1 -> x4, waiting for transfers between devices: 0.02 us -> 43.9 us  [the longest x1 35.4 us: body(): all_normed = lax.all_gather(normed, 'gy', axis=0, tiled=True)]
    dot_general x2, matrix products: 11.6 us -> 37.9 us  [the longest x1 19.4 us: body(): jnp.einsum('rd,def->ref', all_normed, full_pair, preferred_element_type=j...]
    all_gather x0 -> x1, blocking collectives: none -> 22.3 us  [body(): all_gates = lax.all_gather(dense_gates, 'gy', axis=0, tiled=True)]
    unnamed x37 -> x18, local copies, waits for them, and re-layouts: 15.5 us -> 3.52 us
    all_to_all x2 -> x0, starting transfers between devices: 9.8 us -> none  [the longest x1 5.03 us: body(): lax.all_to_all(expert_rows, 'gy', split_axis=0, concat_axis=0, tiled=True)]
    gather x1 -> x0, local copies, waits for them, and re-layouts: 9.6 us -> none  [body(): picked = returned[targets].astype(jnp.float32).reshape(row_count, TOP, D)]
  transfers between devices with their start and end apart: 5 -> 7, of which waited for: 3 -> 4; matrix products, arithmetic and copies ran while one was open for 18% -> 18% of each run, Pallas kernels for 10% -> 9%
where the time goes in v2:
time: 308 us; the launch traced here: 303 us
  waiting for transfers between devices  149 us (48%)
  matrix products  43.6 us (14%)
  Pallas kernels  28.1 us (9%)
  blocking collectives  22.3 us (7%)
  local copies, waits for them, and re-layouts  20.9 us (7%)
  between operations  14.2 us (5%)
  starting transfers between devices  13.8 us (4%)
  other arithmetic  11.6 us (4%)
    reduce_scatter x1, waiting for transfers between devices, body(): mixed = lax.psum_scatter(partial, 'gy', scatter_dimension=0, tiled=True)  95.6 us
    all_gather x1, waiting for transfers between devices, body(): all_normed = lax.all_gather(normed, 'gy', axis=0, tiled=True)  35.4 us
    pallas_call x2, Pallas kernels, paged_attend(): pl.pallas_call(attend_kernel, grid_spec=grid_spec, out_shape=[jax.ShapeDt...  28.1 us
    all_gather x1, blocking collectives, body(): all_gates = lax.all_gather(dense_gates, 'gy', axis=0, tiled=True)  22.3 us
    dot_general x1, matrix products, body(): jnp.einsum('rd,def->ref', all_normed, full_pair, preferred_element_type=j...  19.4 us
    dot_general x1, matrix products, body(): jnp.einsum('ref,def->red', hidden, full_down, preferred_element_type=jnp....  18.5 us
    all_to_all x2, starting transfers between devices, in_one_piece(): lax.all_to_all(both, axis, split_axis=split_dim, concat_axis=concat_dim,...  13.6 us
    all_gather x1, waiting for transfers between devices, body(): full_down = lax.all_gather(down_proj, 'gx', axis=0, tiled=True)  8.53 us
  transfers between devices with their start and end apart: 7, of which 4 were waited for; matrix products, arithmetic and copies ran while one was open for 18% of the time, Pallas kernels for 9%

profile of v2, /device:TPU:96, one launch (start us, length us, event | category | flops | bytes accessed | tf_op | source)
XLA Modules:
  0.0 302.9 jit_solution(15682517844773992493)
XLA Ops:
  8.0 2.2 copy.108
  11.0 0.8 select_reduce_fusion.5
  11.8 1.2 compare_select_fusion
  13.2 1.0 convolution_bitcast_fusion
  14.2 0.7 copy.88
  15.0 7.0 %all-to-all-start = ((f32[16,1,1537]{2,1,0:T(1,128)}), f32[16,1,1537]{2,1,0:T(1,128)S(1)}, u32[]{:S(2)}, u32[]{:S(2)}) async-start(f32[16,1,1537]{2,1,0:T(1,128)} %copy.88), calls=%async_computation | async-start | bytes 212992 | tf_op jit(solution)/shard_map/all_to_all | solution.py:124
  22.0 0.7 slice.53
  22.8 1.0 reshape.122
  24.8 0.7 slice_convert_fusion.1
  27.1 10.2 %shard_map.158 = (f32[8,24,128]{2,1,0:T(8,128)}, f32[8,24,128]{2,1,0:T(8,128)}, f32[8,24,512]{2,1,0:T(8,128)}) custom-call(s32[8,32]{1,0:T(8,128)} %tables.2, s32[8]{0:T(128)} %get-tuple-element.30.lengths, bf16[8,24,512]{2,1,0:T(8,128)(2,1)} %broadcast_select_fusion.1.q_ref, bf16[128,16,1024]{2,1,0:T(8,128)(2,1)} %pool_ref.3), custom_call_target="tpu_custom_call" | custom-call | flops 201326592 | bytes 8388608 | tf_op jit(solution)/shard_map/pallas_call | solution.py:96
  37.4 1.0 slice_reduce_fusion
  38.6 1.0 slice_reduce_fusion.1
  39.8 1.2 reshape.124
  42.5 0.9 fusion.19.lengths
  43.4 0.8 broadcast_select_fusion.q_ref
  44.2 17.9 %shard_map.159 = (f32[16,24,128]{2,1,0:T(8,128)}, f32[16,24,128]{2,1,0:T(8,128)}, f32[16,24,512]{2,1,0:T(8,128)}) custom-call(s32[16,32]{1,0:T(8,128)} %tables.3, s32[16]{0:T(128)} %fusion.19.lengths, bf16[16,24,512]{2,1,0:T(8,128)(2,1)} %broadcast_select_fusion.q_ref, bf16[128,16,1024]{2,1,0:T(8,128)(2,1)} %pool_ref.3), custom_call_target="tpu_custom_call" | custom-call | flops 402653184 | bytes 16777216 | tf_op jit(solution)/shard_map/pallas_call | solution.py:96
  62.2 1.2 copy.89
  63.4 1.1 copy.90
  65.2 1.5 reshape.120
  68.4 6.6 %all-to-all-start.1 = ((f32[16,1,8,3,66]{4,2,3,1,0:T(8,128)}), f32[16,1,8,3,66]{4,2,3,1,0:T(8,128)S(1)}, u32[]{:S(2)}, u32[]{:S(2)}) async-start(f32[16,1,8,3,66]{4,2,3,1,0:T(8,128)} %copy.93), calls=%async_computation.1 | async-start | bytes 393216 | tf_op jit(solution)/shard_map/all_to_all | solution.py:124
  75.0 8.3 %all-to-all-done.1 = f32[16,1,8,3,66]{4,2,3,1,0:T(8,128)S(1)} async-done(((f32[16,1,8,3,66]{4,2,3,1,0:T(8,128)}), f32[16,1,8,3,66]{4,2,3,1,0:T(8,128)S(1)}, u32[]{:S(2)}, u32[]{:S(2)}) %all-to-all-start.1) | async-done | bytes 101408 | tf_op jit(solution)/shard_map/all_to_all | solution.py:124
  88.1 3.2 %multiply_reduce_fusion = (f32[128]{0:T(128)S(1)}, f32[128,1536]{1,0:T(8,128)S(1)}) fusion(bf16[1536,1536]{1,0:T(8,128)(2,1)} %all-gather.5.cloned.1.call-done, bf16[112,1536]{1,0:T(8,128)(2,1)S(1)} %copy-done.4, bf16[16,1536]{1,0:T(8,128)(2,1)S(1)} %fusion.14, bf16[128,1536]{1,0:T(8,128)(2,1)S(1)} %copy-done.2), kind=kOutput, calls=%fused_computation.15 | convolution fusion | flops 605552512 | bytes 6291968 | tf_op jit(solution)/shard_map/dot_general | solution.py:262
  91.3 0.9 multiply_convert_fusion
  92.3 0.8 copy.109
  93.2 1.2 fusion.31
  94.6 22.3 %all_gather.16 = f32[2048,32]{0,1:T(8,128)S(1)} all-gather(f32[128,32]{0,1:T(8,128)S(1)} %broadcast_select_fusion.2), channel_id=1, replica_groups=mesh['gx'=8,'gy'=16] {'gy'}, dimensions={0}, use_global_device_ids=true | all-gather | bytes 278528 | tf_op jit(solution)/shard_map/all_gather | solution.py:282
  116.9 35.4 %all-gather.7.cloned.1.call-done = bf16[2048,1536]{1,0:T(8,128)(2,1)} async-done(((bf16[128,1536]{1,0:T(8,128)(2,1)}), bf16[2048,1536]{1,0:T(8,128)(2,1)}) %all-gather.7.cloned.1.call-update) | async-done | bytes 6291472 | tf_op jit(solution)/shard_map/all_gather | solution.py:281
  152.3 19.4 %fusion.3 = f32[2048,2,1024]{2,0,1:T(8,128)} fusion(bf16[1536,2,1024]{2,0,1:T(8,128)(2,1)} %all-gather.9.cloned.1.call-done, bf16[2048,1536]{1,0:T(8,128)(2,1)} %all-gather.7.cloned.1.call-done), kind=kOutput, calls=%fused_computation.8 | convolution fusion | flops 12884901888 | bytes 29360128 | tf_op jit(solution)/shard_map/rd,def->ref/dot_general | solution.py:286
  171.7 8.5 %all-gather.11.cloned.1.call-done = bf16[1536,2,512]{2,0,1:T(8,128)(2,1)} async-done(((bf16[192,2,512]{2,0,1:T(8,128)(2,1)}), bf16[1536,2,512]{2,0,1:T(8,128)(2,1)}) %all-gather.11.cloned.1.call-update) | async-done | bytes 3145744 | tf_op jit(solution)/shard_map/all_gather | solution.py:261
  180.2 18.5 %fusion.1 = f32[2048,1536]{1,0:T(8,128)} fusion(f32[2048,2]{0,1:T(2,128)S(1)} %get-tuple-element.15, pred[2048,2]{0,1:T(4,128)(4,1)S(1)} %get-tuple-element.14, bf16[1536,2,512]{2,0,1:T(8,128)(2,1)} %all-gather.11.cloned.1.call-done, f32[2048,2,1024]{2,0,1:T(8,128)} %fusion.3), kind=kOutput, calls=%fused_computation.5 | convolution fusion | flops 6483345408 | bytes 32526336 | tf_op jit(solution)/shard_map/ref,def->red/dot_general | solution.py:288
  198.7 95.6 %reduce-scatter.2.cloned.1.call-done = f32[128,1536]{1,0:T(8,128)} async-done(((f32[2048,1536]{1,0:T(8,128)}), f32[128,1536]{1,0:T(8,128)}) %reduce-scatter.2.cloned.1.call-update) | async-done | bytes 786448 | tf_op jit(solution)/shard_map/reduce_scatter | solution.py:295
  294.3 2.1 add.51
  (93 shorter events, 13.7 us)
Async XLA Ops:
  7.2 86.0 %copy-start = (bf16[1536,32]{0,1:T(8,128)(2,1)S(1)}, bf16[1536,32]{0,1:T(8,128)(2,1)}, u32[]{:S(2)}) copy-start(bf16[1536,32]{0,1:T(8,128)(2,1)} %param.26) | copy-start | bytes 294916
  7.2 80.9 %all-gather.5.cloned.1.call-start = ((), (), s32[]{:S(2)}) async-start(), calls=%async_computation.3 | async-start | bytes 5308416 | tf_op jit(solution)/shard_map/all_gather | solution.py:259
  7.9 109.0 %all-gather.9.cloned.1.call-start = ((), (), s32[]{:S(2)}) async-start(), calls=%async_computation.5 | async-start | bytes 7077888 | tf_op jit(solution)/shard_map/all_gather | solution.py:260
  15.0 26.5 %all-to-all-start = ((f32[16,1,1537]{2,1,0:T(1,128)}), f32[16,1,1537]{2,1,0:T(1,128)S(1)}, u32[]{:S(2)}, u32[]{:S(2)}) async-start(f32[16,1,1537]{2,1,0:T(1,128)} %copy.88), calls=%async_computation | async-start | bytes 212992 | tf_op jit(solution)/shard_map/all_to_all | solution.py:124
  62.1 25.9 %copy-start.2 = (bf16[128,1536]{1,0:T(8,128)(2,1)S(1)}, bf16[128,1536]{1,0:T(8,128)(2,1)}, u32[]{:S(2)}) copy-start(bf16[128,1536]{1,0:T(8,128)(2,1)} %param.23) | copy-start | bytes 1179652
  62.2 25.9 %copy-start.4 = (bf16[112,1536]{1,0:T(8,128)(2,1)S(1)}, bf16[112,1536]{1,0:T(8,128)(2,1)}, u32[]{:S(2)}) copy-start(bf16[112,1536]{1,0:T(8,128)(2,1)} %param.22) | copy-start | bytes 1032196
  68.4 14.9 %all-to-all-start.1 = ((f32[16,1,8,3,66]{4,2,3,1,0:T(8,128)}), f32[16,1,8,3,66]{4,2,3,1,0:T(8,128)S(1)}, u32[]{:S(2)}, u32[]{:S(2)}) async-start(f32[16,1,8,3,66]{4,2,3,1,0:T(8,128)} %copy.93), calls=%async_computation.1 | async-start | bytes 393216 | tf_op jit(solution)/shard_map/all_to_all | solution.py:124
  75.0 77.3 %all-gather.7.cloned.1.call-start = ((), (), s32[]{:S(2)}) async-start(), calls=%async_computation.4 | async-start | bytes 6684672 | tf_op jit(solution)/shard_map/all_gather | solution.py:281
  84.0 8.3 %copy-start.3 = (bf16[192,2,512]{2,1,0:T(2,128)(2,1)S(1)}, bf16[192,2,512]{2,1,0:T(2,128)(2,1)}, u32[]{:S(2)}) copy-start(bf16[192,2,512]{2,1,0:T(2,128)(2,1)} %param.29) | copy-start | bytes 1179652
  84.5 8.6 %copy-start.6 = (s32[128,8]{0,1:T(8,128)S(1)}, s32[128,8]{0,1:T(8,128)}, u32[]{:S(2)}) copy-start(s32[128,8]{0,1:T(8,128)} %param.27) | copy-start | bytes 12292
  88.0 83.7 %copy-start.5 = (bf16[16,1536]{1,0:T(8,128)(2,1)}, bf16[16,1536]{1,0:T(8,128)(2,1)S(1)}, u32[]{:S(2)}) copy-start(bf16[16,1536]{1,0:T(8,128)(2,1)S(1)} %fusion.14) | copy-start | bytes 147460
  92.2 88.0 %all-gather.11.cloned.1.call-start = ((), (), s32[]{:S(2)}) async-start(), calls=%async_computation.6 | async-start | bytes 3538944 | tf_op jit(solution)/shard_map/all_gather | solution.py:261
  93.1 201.2 %reduce-scatter.2.cloned.1.call-start = ((), (), s32[]{:S(2)}) async-start(), calls=%async_computation.7 | async-start | bytes 13369344 | tf_op jit(solution)/shard_map/reduce_scatter | solution.py:295
  198.7 97.7 %copy-start.1 = (bf16[1536,32]{0,1:T(8,128)(2,1)S(1)}, bf16[1536,32]{0,1:T(8,128)(2,1)}, u32[]{:S(2)}) copy-start(bf16[1536,32]{0,1:T(8,128)(2,1)} %param.26) | copy-start | bytes 294916
Sparse Core Ops, SparseCore 0:
  9.7 33.6 all-gather.4
  45.1 41.0 all-gather.8
  92.3 59.8 all-gather.6
  153.8 26.3 all-gather.10
  198.8 95.3 reduce-scatter.1

commit v3 on v1

--- a/solution.py
+++ b/solution.py
@@ -256,7 +256,9 @@
     attended = finish(query_heads, new_kv, cache_max, totals, mixture)
     tokens = jnp.concatenate([attended, prefill_attn], axis=0)
     row_count = tokens.shape[0]
-    full_out, full_pair, full_down = side_by_side((out_weight, gate_up, down_proj), "gx", 0, 1)
+    full_out = lax.all_gather(out_weight, "gx", axis=0, tiled=True)
+    full_pair = lax.all_gather(gate_up, "gx", axis=0, tiled=True)
+    full_down = lax.all_gather(down_proj, "gx", axis=0, tiled=True)
     stream = residual.astype(jnp.float32) + jnp.dot(
         tokens, full_out, preferred_element_type=jnp.float32
     )
@@ -270,18 +272,28 @@
     gate_weights = jax.nn.softmax(
         jnp.sum(jnp.where(selector, logits[:, None, :], 0.0), axis=2), axis=1
     )
-    flat_routes = routes.reshape(row_count * TOP)
-    route_hits = (flat_routes[:, None] == jnp.arange(EXPERTS, dtype=jnp.int32)[None, :]).astype(
-        jnp.int32
-    )
-    places = jnp.sum((jnp.cumsum(route_hits, axis=0) - 1) * route_hits, axis=1)
-    targets = flat_routes * CAP + places
-    repeated = jnp.repeat(normed, TOP, axis=0)
+    row_hits = jnp.any(selector, axis=1)
+    earlier_rows = (
+        lax.broadcasted_iota(jnp.int32, (row_count, row_count), 1)
+        < lax.broadcasted_iota(jnp.int32, (row_count, row_count), 0)
+    ).astype(jnp.bfloat16)
+    counts = jnp.dot(
+        earlier_rows, row_hits.astype(jnp.bfloat16), preferred_element_type=jnp.float32
+    ).astype(jnp.int32)
+    place_of = jnp.sum(jnp.where(selector, counts[:, None, :], 0), axis=2)
+    targets = (routes * CAP + place_of).reshape(row_count * TOP)
     experts_dev = full_pair.shape[1]
+    slot_hits = row_hits.T[:, None, :] & (
+        counts.T[:, None, :] == jnp.arange(CAP, dtype=jnp.int32)[None, :, None]
+    )
     outgoing_rows = (
-        jnp.zeros((EXPERTS * CAP, D), jnp.bfloat16)
-        .at[targets]
-        .set(repeated)
+        jnp.einsum(
+            "ecr,rd->ecd",
+            slot_hits.astype(jnp.bfloat16),
+            normed,
+            preferred_element_type=jnp.float32,
+        )
+        .astype(jnp.bfloat16)
         .reshape(columns, experts_dev, CAP, D)
     )
     arrived = lax.all_to_all(outgoing_rows, "gy", split_axis=0, concat_axis=0, tiled=True)

time: 288 us -> 282 us (0.979)
  local copies, waits for them, and re-layouts: 61 us -> 33.9 us
  waiting for transfers between devices: 120 us -> 140 us
  matrix products: 15.5 us -> 25.2 us
  other arithmetic: 20.5 us -> 12.8 us
    all_to_all x1, waiting for transfers between devices: 47.8 us -> 67 us  [body(): lax.all_to_all(outgoing_rows, 'gy', split_axis=0, concat_axis=0, tiled=True)]
    unnamed x37 -> x20, local copies, waits for them, and re-layouts: 15.5 us -> 3.5 us
    another operation x2 -> x0, other arithmetic: 9.04 us -> none
    split x3 -> x0, local copies, waits for them, and re-layouts: 8.37 us -> none  [side_by_side(): jnp.split(result, [sum(widths[:k]) for k in range(1, len(widths))], axis=...]
    scatter x1 -> x0, local copies, waits for them, and re-layouts: 8.36 us -> none  [body(): outgoing_rows = jnp.zeros((EXPERTS * CAP, D), jnp.bfloat16).at[targets].s...]
    dot_general x0 -> x2, matrix products: none -> 3.83 us  [the longest x1 3.69 us: body(): jnp.einsum('ecr,rd->ecd', slot_hits.astype(jnp.bfloat16), normed, preferr...]
    dot_general x1, matrix products: 2.85 us -> 6.4 us  [body(): jnp.einsum('secf,def->secd', hidden, full_down, preferred_element_type=jn...]
  transfers between devices with their start and end apart: 5 -> 7, of which waited for: 3 -> 3; matrix products, arithmetic and copies ran while one was open for 18% -> 17% of each run, Pallas kernels for 10% -> 10%
where the time goes in v3:
time: 282 us; the launch traced here: 278 us
  waiting for transfers between devices  140 us (50%)
  local copies, waits for them, and re-layouts  33.9 us (12%)
  Pallas kernels  27.7 us (10%)
  matrix products  25.2 us (9%)
  starting transfers between devices  24 us (9%)
  between operations  14.2 us (5%)
  other arithmetic  12.8 us (5%)
    all_to_all x1, waiting for transfers between devices, body(): lax.all_to_all(outgoing_rows, 'gy', split_axis=0, concat_axis=0, tiled=True)  67 us
    all_to_all x1, waiting for transfers between devices, body(): lax.all_to_all(expert_rows, 'gy', split_axis=0, concat_axis=0, tiled=True)  63.9 us
    pallas_call x2, Pallas kernels, paged_attend(): pl.pallas_call(attend_kernel, grid_spec=grid_spec, out_shape=[jax.ShapeDt...  27.7 us
    all_to_all x2, starting transfers between devices, in_one_piece(): lax.all_to_all(both, axis, split_axis=split_dim, concat_axis=concat_dim,...  14.1 us
    gather x1, local copies, waits for them, and re-layouts, body(): picked = returned[targets].astype(jnp.float32).reshape(row_count, TOP, D)  10.2 us
    dot_general x1, matrix products, body(): jnp.einsum('secd,def->secf', arrived, full_pair, preferred_element_type=j...  10.2 us
    all_to_all x2, waiting for transfers between devices, in_one_piece(): lax.all_to_all(both, axis, split_axis=split_dim, concat_axis=concat_dim,...  8.33 us
    dot_general x1, matrix products, body(): jnp.einsum('secf,def->secd', hidden, full_down, preferred_element_type=jn...  6.4 us
  transfers between devices with their start and end apart: 7, of which 3 were waited for; matrix products, arithmetic and copies ran while one was open for 17% of the time, Pallas kernels for 10%

profile of v3, /device:TPU:96, one launch (start us, length us, event | category | flops | bytes accessed | tf_op | source)
XLA Modules:
  0.0 277.8 jit_solution(17793556507387675782)
XLA Ops:
  8.0 2.2 copy.123
  11.0 0.8 select_reduce_fusion.5
  11.8 1.2 compare_select_fusion.1
  13.3 1.0 convolution_bitcast_fusion
  14.3 0.8 copy.102
  15.0 7.0 %all-to-all-start = ((f32[16,1,1537]{2,1,0:T(1,128)}), f32[16,1,1537]{2,1,0:T(1,128)S(1)}, u32[]{:S(2)}, u32[]{:S(2)}) async-start(f32[16,1,1537]{2,1,0:T(1,128)} %copy.102), calls=%async_computation | async-start | bytes 212992 | tf_op jit(solution)/shard_map/all_to_all | solution.py:124
  22.8 1.0 reshape.164
  25.2 10.3 %shard_map.158 = (f32[8,24,128]{2,1,0:T(8,128)}, f32[8,24,128]{2,1,0:T(8,128)}, f32[8,24,512]{2,1,0:T(8,128)}) custom-call(s32[8,32]{1,0:T(8,128)} %tables.2, s32[8]{0:T(128)} %get-tuple-element.28.lengths, bf16[8,24,512]{2,1,0:T(8,128)(2,1)} %broadcast_select_fusion.1.q_ref, bf16[128,16,1024]{2,1,0:T(8,128)(2,1)} %pool_ref.3), custom_call_target="tpu_custom_call" | custom-call | flops 201326592 | bytes 8388608 | tf_op jit(solution)/shard_map/pallas_call | solution.py:96
  35.4 1.0 slice_reduce_fusion.1
  36.6 1.0 slice_reduce_fusion
  38.5 1.2 reshape.166
  41.4 0.9 fusion.30.lengths
  42.3 0.8 broadcast_select_fusion.q_ref
  43.1 17.5 %shard_map.159 = (f32[16,24,128]{2,1,0:T(8,128)}, f32[16,24,128]{2,1,0:T(8,128)}, f32[16,24,512]{2,1,0:T(8,128)}) custom-call(s32[16,32]{1,0:T(8,128)} %tables.3, s32[16]{0:T(128)} %fusion.30.lengths, bf16[16,24,512]{2,1,0:T(8,128)(2,1)} %broadcast_select_fusion.q_ref, bf16[128,16,1024]{2,1,0:T(8,128)(2,1)} %pool_ref.3), custom_call_target="tpu_custom_call" | custom-call | flops 402653184 | bytes 16777216 | tf_op jit(solution)/shard_map/pallas_call | solution.py:96
  60.5 1.5 reshape.162
  62.1 1.1 copy.103
  63.6 1.1 copy.104
  66.7 7.0 %all-to-all-start.1 = ((f32[16,1,8,3,66]{4,2,3,1,0:T(8,128)}), f32[16,1,8,3,66]{4,2,3,1,0:T(8,128)S(1)}, u32[]{:S(2)}, u32[]{:S(2)}) async-start(f32[16,1,8,3,66]{4,2,3,1,0:T(8,128)} %copy.107), calls=%async_computation.1 | async-start | bytes 393216 | tf_op jit(solution)/shard_map/all_to_all | solution.py:124
  73.7 8.3 %all-to-all-done.1 = f32[16,1,8,3,66]{4,2,3,1,0:T(8,128)S(1)} async-done(((f32[16,1,8,3,66]{4,2,3,1,0:T(8,128)}), f32[16,1,8,3,66]{4,2,3,1,0:T(8,128)S(1)}, u32[]{:S(2)}, u32[]{:S(2)}) %all-to-all-start.1) | async-done | bytes 101408 | tf_op jit(solution)/shard_map/all_to_all | solution.py:124
  86.8 3.2 %multiply_reduce_fusion = (f32[128]{0:T(128)S(1)}, f32[128,1536]{1,0:T(8,128)S(1)}) fusion(bf16[1536,1536]{1,0:T(8,128)(2,1)} %all-gather.4.cloned.1.call-done, bf16[112,1536]{1,0:T(8,128)(2,1)S(1)} %copy-done.3, bf16[16,1536]{1,0:T(8,128)(2,1)S(1)} %fusion.25, bf16[128,1536]{1,0:T(8,128)(2,1)S(1)} %copy-done.1), kind=kOutput, calls=%fused_computation.22 | convolution fusion | flops 605552512 | bytes 6291968 | tf_op jit(solution)/shard_map/dot_general | solution.py:262
  90.0 3.7 %convolution_convert_fusion = bf16[32,48,1536]{2,1,0:T(8,128)(2,1)} fusion(s32[32,128]{1,0:T(8,128)S(1)} %bitcast.64, pred[32,128]{1,0:T(8,128)(4,1)S(1)} %bitcast.69, f32[128,1536]{1,0:T(8,128)S(1)} %get-tuple-element.26, f32[1536]{0:T(1024)S(1)} %convert_element_type.73, f32[128]{0:T(128)S(1)} %add_rsqrt_fusion), kind=kOutput, calls=%fused_computation.10 | convolution fusion | flops 607322112 | bytes 5532160 | tf_op jit(solution)/shard_map/ecr,rd->ecd/dot_general | solution.py:290
  93.7 4.7 %all-to-all-start.2 = ((bf16[16,2,48,1536]{3,2,1,0:T(8,128)(2,1)}), bf16[16,2,48,1536]{3,2,1,0:T(8,128)(2,1)}, u32[]{:S(2)}, u32[]{:S(2)}) async-start(bf16[16,2,48,1536]{3,2,1,0:T(8,128)(2,1)} %bitcast.59), calls=%async_computation.2 | async-start | bytes 9437184 | tf_op jit(solution)/shard_map/all_to_all | solution.py:299
  98.7 0.8 copy.125
  99.5 67.0 %all-to-all-done.2 = bf16[16,2,48,1536]{3,2,1,0:T(8,128)(2,1)} async-done(((bf16[16,2,48,1536]{3,2,1,0:T(8,128)(2,1)}), bf16[16,2,48,1536]{3,2,1,0:T(8,128)(2,1)}, u32[]{:S(2)}, u32[]{:S(2)}) %all-to-all-start.2) | async-done | bytes 4718624 | tf_op jit(solution)/shard_map/all_to_all | solution.py:299
  166.5 10.2 %fusion.6 = f32[16,2,48,1024]{3,2,0,1:T(8,128)} fusion(bf16[1536,2,1024]{2,0,1:T(8,128)(2,1)} %all-gather.6.cloned.1.call-done, bf16[16,2,48,1536]{3,2,1,0:T(8,128)(2,1)} %all-to-all-done.2), kind=kOutput, calls=%fused_computation.14 | convolution fusion | flops 4831838208 | bytes 17301504 | tf_op jit(solution)/shard_map/secd,def->secf/dot_general | solution.py:300
  176.7 6.4 %convert_bitcast_fusion = bf16[16,2,48,1536]{3,2,0,1:T(8,128)(2,1)S(1)} fusion(bf16[1536,2,512]{2,0,1:T(8,128)(2,1)} %all-gather.8.cloned.1.call-done, f32[16,2,48,1024]{3,2,0,1:T(8,128)} %fusion.6), kind=kOutput, calls=%fused_computation.9 | convolution fusion | flops 2422996992 | bytes 14155776 | tf_op jit(solution)/shard_map/secf,def->secd/dot_general | solution.py:302
  183.1 2.6 copy.126
  185.7 4.9 %all-to-all-start.3 = ((bf16[16,2,48,1536]{3,2,1,0:T(8,128)(2,1)}), bf16[16,2,48,1536]{3,2,1,0:T(8,128)(2,1)}, u32[]{:S(2)}, u32[]{:S(2)}) async-start(bf16[16,2,48,1536]{3,2,1,0:T(8,128)(2,1)} %copy.126), calls=%async_computation.3 | async-start | bytes 9437184 | tf_op jit(solution)/shard_map/all_to_all | solution.py:305
  191.4 63.9 %all-to-all-done.3 = bf16[16,2,48,1536]{3,2,1,0:T(8,128)(2,1)} async-done(((bf16[16,2,48,1536]{3,2,1,0:T(8,128)(2,1)}), bf16[16,2,48,1536]{3,2,1,0:T(8,128)(2,1)}, u32[]{:S(2)}, u32[]{:S(2)}) %all-to-all-start.3) | async-done | bytes 4718624 | tf_op jit(solution)/shard_map/all_to_all | solution.py:305
  255.3 10.2 %gather_fusion.3 = bf16[1024,1536]{1,0:T(8,128)(2,1)} fusion(bf16[1536,1536]{1,0:T(8,128)(2,1)} %bitcast.20, s32[1024]{0:T(1024)S(1)} %broadcast_clamp_fusion), kind=kCustom, calls=%fused_computation.3 | custom fusion | bytes 6295552 | tf_op jit(solution)/shard_map/gather | solution.py:308
  265.6 4.7 %fusion = f32[128,1536]{1,0:T(8,128)S(1)} fusion(bf16[1024,1536]{1,0:T(8,128)(2,1)} %gather_fusion.3, f32[128,8]{1,0:T(8,128)S(1)} %copy.122), kind=kLoop, calls=%fused_computation.5 | loop fusion | flops 4521984 | bytes 3936256 | tf_op jit(solution)/shard_map/reduce_sum | solution.py:309
  270.3 1.0 add.64
  (100 shorter events, 14.5 us)
Async XLA Ops:
  7.2 183.7 %copy-start = (bf16[1536,32]{0,1:T(8,128)(2,1)S(1)}, bf16[1536,32]{0,1:T(8,128)(2,1)}, u32[]{:S(2)}) copy-start(bf16[1536,32]{0,1:T(8,128)(2,1)} %param.26) | copy-start | bytes 294916
  7.2 79.6 %all-gather.4.cloned.1.call-start = ((), (), s32[]{:S(2)}) async-start(), calls=%async_computation.4 | async-start | bytes 5308416 | tf_op jit(solution)/shard_map/all_gather | solution.py:259
  7.9 29.9 %copy-start.6 = (bf16[16,1024]{1,0:T(8,128)(2,1)S(1)}, bf16[16,1024]{1,0:T(8,128)(2,1)}, u32[]{:S(2)}) copy-start(bf16[16,1024]{1,0:T(8,128)(2,1)} %param.16) | copy-start | bytes 98308
  7.9 91.6 %all-gather.6.cloned.1.call-start = ((), (), s32[]{:S(2)}) async-start(), calls=%async_computation.5 | async-start | bytes 7077888 | tf_op jit(solution)/shard_map/all_gather | solution.py:260
  10.2 29.4 %copy-start.5 = (s32[128,8]{0,1:T(8,128)S(1)}, s32[128,8]{0,1:T(8,128)}, u32[]{:S(2)}) copy-start(s32[128,8]{0,1:T(8,128)} %param.27) | copy-start | bytes 12292
  15.0 25.3 %all-to-all-start = ((f32[16,1,1537]{2,1,0:T(1,128)}), f32[16,1,1537]{2,1,0:T(1,128)S(1)}, u32[]{:S(2)}, u32[]{:S(2)}) async-start(f32[16,1,1537]{2,1,0:T(1,128)} %copy.102), calls=%async_computation | async-start | bytes 212992 | tf_op jit(solution)/shard_map/all_to_all | solution.py:124
  24.0 16.3 %copy-start.7 = (bf16[1536]{0:T(1024)(128)(2,1)S(1)}, bf16[1536]{0:T(1024)(128)(2,1)}, u32[]{:S(2)}) copy-start(bf16[1536]{0:T(1024)(128)(2,1)} %param.25) | copy-start | bytes 9220
  64.7 22.1 %copy-start.1 = (bf16[128,1536]{1,0:T(8,128)(2,1)S(1)}, bf16[128,1536]{1,0:T(8,128)(2,1)}, u32[]{:S(2)}) copy-start(bf16[128,1536]{1,0:T(8,128)(2,1)} %param.23) | copy-start | bytes 1179652
  64.7 22.1 %copy-start.3 = (bf16[112,1536]{1,0:T(8,128)(2,1)S(1)}, bf16[112,1536]{1,0:T(8,128)(2,1)}, u32[]{:S(2)}) copy-start(bf16[112,1536]{1,0:T(8,128)(2,1)} %param.22) | copy-start | bytes 1032196
  66.7 15.4 %all-to-all-start.1 = ((f32[16,1,8,3,66]{4,2,3,1,0:T(8,128)}), f32[16,1,8,3,66]{4,2,3,1,0:T(8,128)S(1)}, u32[]{:S(2)}, u32[]{:S(2)}) async-start(f32[16,1,8,3,66]{4,2,3,1,0:T(8,128)} %copy.107), calls=%async_computation.1 | async-start | bytes 393216 | tf_op jit(solution)/shard_map/all_to_all | solution.py:124
  86.7 7.0 %copy-start.4 = (bf16[16,1536]{1,0:T(8,128)(2,1)}, bf16[16,1536]{1,0:T(8,128)(2,1)S(1)}, u32[]{:S(2)}) copy-start(bf16[16,1536]{1,0:T(8,128)(2,1)S(1)} %fusion.25) | copy-start | bytes 147460
  93.7 4.9 %copy-start.2 = (bf16[192,2,512]{2,1,0:T(2,128)(2,1)S(1)}, bf16[192,2,512]{2,1,0:T(2,128)(2,1)}, u32[]{:S(2)}) copy-start(bf16[192,2,512]{2,1,0:T(2,128)(2,1)} %param.29) | copy-start | bytes 1179652
  93.7 72.8 %all-to-all-start.2 = ((bf16[16,2,48,1536]{3,2,1,0:T(8,128)(2,1)}), bf16[16,2,48,1536]{3,2,1,0:T(8,128)(2,1)}, u32[]{:S(2)}, u32[]{:S(2)}) async-start(bf16[16,2,48,1536]{3,2,1,0:T(8,128)(2,1)} %bitcast.59), calls=%async_computation.2 | async-start | bytes 9437184 | tf_op jit(solution)/shard_map/all_to_all | solution.py:299
  98.4 78.3 %all-gather.8.cloned.1.call-start = ((), (), s32[]{:S(2)}) async-start(), calls=%async_computation.6 | async-start | bytes 3538944 | tf_op jit(solution)/shard_map/all_gather | solution.py:261
  185.7 69.6 %all-to-all-start.3 = ((bf16[16,2,48,1536]{3,2,1,0:T(8,128)(2,1)}), bf16[16,2,48,1536]{3,2,1,0:T(8,128)(2,1)}, u32[]{:S(2)}, u32[]{:S(2)}) async-start(bf16[16,2,48,1536]{3,2,1,0:T(8,128)(2,1)} %copy.126), calls=%async_computation.3 | async-start | bytes 9437184 | tf_op jit(solution)/shard_map/all_to_all | solution.py:305
Sparse Core Ops, SparseCore 0:
  9.7 33.6 all-gather.3
  45.1 40.9 all-gather.5
  101.5 27.9 all-gather.7

commit v4 on v3

--- a/solution.py
+++ b/solution.py
@@ -64,6 +64,67 @@
     max_ref[0] = jnp.broadcast_to(top, max_ref.shape[1:])
     tot_ref[0] = jnp.broadcast_to(total, tot_ref.shape[1:])
     mix_ref[0] = mix
+
+
+def exchange_kernel(x_ref, y_ref, send_sems, recv_sems, own_sem):
+    n = x_ref.shape[0]
+    me = lax.axis_index("gy")
+    row = lax.axis_index("gx")
+    mesh_ids = pl.DeviceIdType.MESH
+    barrier = pltpu.get_barrier_semaphore()
+    for k in range(1, n):
+        pl.semaphore_signal(
+            barrier, inc=1, device_id=(row, lax.rem(me + k, n)), device_id_type=mesh_ids
+        )
+    pl.semaphore_wait(barrier, n - 1)
+    own = pltpu.make_async_copy(x_ref.at[me], y_ref.at[me], own_sem)
+    own.start()
+    copies = []
+    for k in range(1, n):
+        dest = lax.rem(me + k, n)
+        copy = pltpu.make_async_remote_copy(
+            src_ref=x_ref.at[dest],
+            dst_ref=y_ref.at[me],
+            send_sem=send_sems.at[k],
+            recv_sem=recv_sems.at[k],
+            device_id=(row, dest),
+            device_id_type=mesh_ids,
+        )
+        copy.start()
+        copies.append(copy)
+    for k in range(1, n):
+        source = lax.rem(me + n - k, n)
+        pltpu.make_async_remote_copy(
+            src_ref=x_ref.at[source],
+            dst_ref=y_ref.at[source],
+            send_sem=send_sems.at[k],
+            recv_sem=recv_sems.at[k],
+            device_id=(row, source),
+            device_id_type=mesh_ids,
+        ).wait_recv()
+    for copy in copies:
+        copy.wait_send()
+    own.wait()
+
+
+def exchange(x, tag):
+    n = x.shape[0]
+    block = x.size // n * x.dtype.itemsize
+    return pl.pallas_call(
+        exchange_kernel,
+        out_shape=jax.ShapeDtypeStruct(x.shape, x.dtype),
+        in_specs=[pl.BlockSpec(memory_space=pl.ANY)],
+        out_specs=pl.BlockSpec(memory_space=pl.ANY),
+        scratch_shapes=[
+            pltpu.SemaphoreType.DMA((n,)),
+            pltpu.SemaphoreType.DMA((n,)),
+            pltpu.SemaphoreType.DMA,
+        ],
+        compiler_params=pltpu.CompilerParams(collective_id=tag, has_side_effects=True),
+        cost_estimate=pl.CostEstimate(
+            flops=0, transcendentals=0, bytes_accessed=2 * n * block
+        ),
+    )(x)
 
 
 def paged_attend(query_rows, tables, lengths, pool):
@@ -296,13 +357,13 @@
         .astype(jnp.bfloat16)
         .reshape(columns, experts_dev, CAP, D)
     )
-    arrived = lax.all_to_all(outgoing_rows, "gy", split_axis=0, concat_axis=0, tiled=True)
+    arrived = exchange(outgoing_rows, 1)
     gate_pair = jnp.einsum("secd,def->secf", arrived, full_pair, preferred_element_type=jnp.float32)
     hidden = (jax.nn.silu(gate_pair[..., :FF]) * gate_pair[..., FF:]).astype(jnp.bfloat16)
     expert_rows = jnp.einsum(
         "secf,def->secd", hidden, full_down, preferred_element_type=jnp.float32
     ).astype(jnp.bfloat16)
-    returned = lax.all_to_all(expert_rows, "gy", split_axis=0, concat_axis=0, tiled=True).reshape(
+    returned = exchange(expert_rows, 2).reshape(
         EXPERTS * CAP, D
     )
     picked = returned[targets].astype(jnp.float32).reshape(row_count, TOP, D)

time: 282 us -> 294 us (1.043)
  the two profiles are of different devices: /device:TPU:96 before, /device:TPU:64 now
where the time goes in v4:
time: 294 us; the launch traced here: 291 us
  Pallas kernels  183 us (62%)
  local copies, waits for them, and re-layouts  30.8 us (10%)
  matrix products  27.3 us (9%)
  between operations  14.2 us (5%)
  starting transfers between devices  14 us (5%)
  other arithmetic  12.8 us (4%)
  waiting for transfers between devices  9.08 us (3%)
    pallas_call x2, Pallas kernels, exchange(): pl.pallas_call(exchange_kernel, out_shape=jax.ShapeDtypeStruct(x.shape, x...  155 us
    pallas_call x2, Pallas kernels, paged_attend(): pl.pallas_call(attend_kernel, grid_spec=grid_spec, out_shape=[jax.ShapeDt...  27.9 us
    all_to_all x2, starting transfers between devices, in_one_piece(): lax.all_to_all(both, axis, split_axis=split_dim, concat_axis=concat_dim,...  13.8 us
    gather x1, local copies, waits for them, and re-layouts, body(): picked = returned[targets].astype(jnp.float32).reshape(row_count, TOP, D)  10.2 us
    dot_general x1, matrix products, body(): jnp.einsum('secd,def->secf', arrived, full_pair, preferred_element_type=j...  10.2 us
    dot_general x1, matrix products, body(): jnp.einsum('secf,def->secd', hidden, full_down, preferred_element_type=jn...  8.53 us
    all_to_all x2, waiting for transfers between devices, in_one_piece(): lax.all_to_all(both, axis, split_axis=split_dim, concat_axis=concat_dim,...  8.32 us
  transfers between devices with their start and end apart: 5, of which 1 were waited for; matrix products, arithmetic and copies ran while one was open for 16% of the time, Pallas kernels for 33%

profile of v4, /device:TPU:64, one launch (start us, length us, event | category | flops | bytes accessed | tf_op | source)
XLA Modules:
  0.0 291.0 jit_solution(8910692626870205355)
XLA Ops:
  7.2 0.7 all-gather.4.cloned.1.call-update
  8.0 2.2 copy.124
  10.2 0.7 fusion.30
  11.0 0.8 select_reduce_fusion.5
  11.8 1.2 compare_select_fusion.1
  13.3 1.0 convolution_bitcast_fusion
  14.3 0.8 copy.103
  15.0 7.0 %all-to-all-start = ((f32[16,1,1537]{2,1,0:T(1,128)}), f32[16,1,1537]{2,1,0:T(1,128)S(1)}, u32[]{:S(2)}, u32[]{:S(2)}) async-start(f32[16,1,1537]{2,1,0:T(1,128)} %copy.103), calls=%async_computation | async-start | bytes 212992 | tf_op jit(solution)/shard_map/all_to_all | solution.py:185
  22.1 1.8 copy.126
  24.8 0.7 broadcast_select_fusion.1.q_ref
  25.5 10.2 %shard_map.158 = (f32[8,24,128]{2,1,0:T(8,128)}, f32[8,24,128]{2,1,0:T(8,128)}, f32[8,24,512]{2,1,0:T(8,128)}) custom-call(s32[8,32]{1,0:T(8,128)} %tables.2, s32[8]{0:T(128)} %get-tuple-element.28.lengths, bf16[8,24,512]{2,1,0:T(8,128)(2,1)} %broadcast_select_fusion.1.q_ref, bf16[128,16,1024]{2,1,0:T(8,128)(2,1)} %pool_ref.3), custom_call_target="tpu_custom_call" | custom-call | flops 201326592 | bytes 8388608 | tf_op jit(solution)/shard_map/pallas_call | solution.py:157
  35.7 1.0 slice_reduce_fusion.1
  37.6 1.0 slice_reduce_fusion
  39.2 1.2 reshape.166
  42.0 0.9 fusion.29.lengths
  42.9 0.8 broadcast_select_fusion.q_ref
  43.7 17.7 %shard_map.159 = (f32[16,24,128]{2,1,0:T(8,128)}, f32[16,24,128]{2,1,0:T(8,128)}, f32[16,24,512]{2,1,0:T(8,128)}) custom-call(s32[16,32]{1,0:T(8,128)} %tables.3, s32[16]{0:T(128)} %fusion.29.lengths, bf16[16,24,512]{2,1,0:T(8,128)(2,1)} %broadcast_select_fusion.q_ref, bf16[128,16,1024]{2,1,0:T(8,128)(2,1)} %pool_ref.3), custom_call_target="tpu_custom_call" | custom-call | flops 402653184 | bytes 16777216 | tf_op jit(solution)/shard_map/pallas_call | solution.py:157
  61.4 1.5 reshape.162
  62.9 1.1 copy.104
  64.4 1.1 copy.105
  66.9 0.7 copy.108
  67.6 6.8 %all-to-all-start.1 = ((f32[16,1,8,3,66]{4,2,3,1,0:T(8,128)}), f32[16,1,8,3,66]{4,2,3,1,0:T(8,128)S(1)}, u32[]{:S(2)}, u32[]{:S(2)}) async-start(f32[16,1,8,3,66]{4,2,3,1,0:T(8,128)} %copy.108), calls=%async_computation.1 | async-start | bytes 393216 | tf_op jit(solution)/shard_map/all_to_all | solution.py:185
  74.4 8.3 %all-to-all-done.1 = f32[16,1,8,3,66]{4,2,3,1,0:T(8,128)S(1)} async-done(((f32[16,1,8,3,66]{4,2,3,1,0:T(8,128)}), f32[16,1,8,3,66]{4,2,3,1,0:T(8,128)S(1)}, u32[]{:S(2)}, u32[]{:S(2)}) %all-to-all-start.1) | async-done | bytes 101408 | tf_op jit(solution)/shard_map/all_to_all | solution.py:185
  87.4 3.2 %multiply_reduce_fusion = (f32[128]{0:T(128)S(1)}, f32[128,1536]{1,0:T(8,128)S(1)}) fusion(bf16[1536,1536]{1,0:T(8,128)(2,1)} %all-gather.4.cloned.1.call-done, bf16[112,1536]{1,0:T(8,128)(2,1)S(1)} %copy-done.2, bf16[16,1536]{1,0:T(8,128)(2,1)S(1)} %fusion.24, bf16[128,1536]{1,0:T(8,128)(2,1)S(1)} %copy-done.1), kind=kOutput, calls=%fused_computation.22 | convolution fusion | flops 605552512 | bytes 6291968 | tf_op jit(solution)/shard_map/dot_general | solution.py:323
  91.2 3.7 %convolution_convert_fusion = bf16[32,48,1536]{2,1,0:T(8,128)(2,1)} fusion(s32[32,128]{1,0:T(8,128)S(1)} %bitcast.63, pred[32,128]{1,0:T(8,128)(4,1)S(1)} %bitcast.68, f32[128,1536]{1,0:T(8,128)S(1)} %get-tuple-element.26, f32[1536]{0:T(1024)S(1)} %convert_element_type.72, f32[128]{0:T(128)S(1)} %add_rsqrt_fusion), kind=kOutput, calls=%fused_computation.10 | convolution fusion | flops 607322112 | bytes 5532160 | tf_op jit(solution)/shard_map/ecr,rd->ecd/dot_general | solution.py:351
  94.9 69.4 %shard_map.160 = bf16[16,2,48,1536]{3,2,1,0:T(8,128)(2,1)} custom-call(bf16[16,2,48,1536]{3,2,1,0:T(8,128)(2,1)} %bitcast.58), custom_call_target="tpu_custom_call" | custom-call | bytes 9437184 | tf_op jit(solution)/shard_map/pallas_call | solution.py:113
  164.3 10.2 %fusion.6 = f32[16,2,48,1024]{3,2,0,1:T(8,128)} fusion(bf16[1536,2,1024]{2,0,1:T(8,128)(2,1)} %all-gather.6.cloned.1.call-done, bf16[16,2,48,1536]{3,2,1,0:T(8,128)(2,1)} %shard_map.160), kind=kOutput, calls=%fused_computation.14 | convolution fusion | flops 4831838208 | bytes 17301504 | tf_op jit(solution)/shard_map/secd,def->secf/dot_general | solution.py:361
  174.5 8.5 %convert_bitcast_fusion.x_ref = bf16[16,2,48,1536]{3,2,1,0:T(8,128)(2,1)} fusion(bf16[1536,2,512]{2,0,1:T(8,128)(2,1)} %all-gather.8.cloned.1.call-done, f32[16,2,48,1024]{3,2,0,1:T(8,128)} %fusion.6), kind=kOutput, calls=%fused_computation.9 | convolution fusion | flops 2422996992 | bytes 14155776 | tf_op jit(solution)/shard_map/secf,def->secd/dot_general | solution.py:363
  183.0 85.5 %shard_map.161 = bf16[16,2,48,1536]{3,2,1,0:T(8,128)(2,1)} custom-call(bf16[16,2,48,1536]{3,2,1,0:T(8,128)(2,1)} %convert_bitcast_fusion.x_ref), custom_call_target="tpu_custom_call" | custom-call | bytes 9437184 | tf_op jit(solution)/shard_map/pallas_call | solution.py:113
  268.5 10.2 %gather_fusion.3 = bf16[1024,1536]{1,0:T(8,128)(2,1)} fusion(bf16[1536,1536]{1,0:T(8,128)(2,1)} %bitcast.57, s32[1024]{0:T(1024)S(1)} %broadcast_clamp_fusion), kind=kCustom, calls=%fused_computation.3 | custom fusion | bytes 6295552 | tf_op jit(solution)/shard_map/gather | solution.py:369
  278.8 4.7 %fusion = f32[128,1536]{1,0:T(8,128)S(1)} fusion(bf16[1024,1536]{1,0:T(8,128)(2,1)} %gather_fusion.3, f32[128,8]{1,0:T(8,128)S(1)} %copy.123), kind=kLoop, calls=%fused_computation.5 | loop fusion | flops 4521984 | bytes 3936256 | tf_op jit(solution)/shard_map/reduce_sum | solution.py:370
  283.5 1.0 add.64
  (98 shorter events, 11.0 us)
Async XLA Ops:
  7.2 83.5 %copy-start = (bf16[1536,32]{0,1:T(8,128)(2,1)S(1)}, bf16[1536,32]{0,1:T(8,128)(2,1)}, u32[]{:S(2)}) copy-start(bf16[1536,32]{0,1:T(8,128)(2,1)} %param.26) | copy-start | bytes 294916
  7.2 16.8 %copy-start.4 = (bf16[16,1536]{1,0:T(8,128)(2,1)S(1)}, bf16[16,1536]{1,0:T(8,128)(2,1)}, u32[]{:S(2)}) copy-start(bf16[16,1536]{1,0:T(8,128)(2,1)} %param.15) | copy-start | bytes 147460
  7.2 17.2 %slice-start = ((bf16[16,1536]{1,0:T(8,128)(2,1)}), bf16[8,1536]{1,0:T(8,128)(2,1)S(1)}, s32[]{:S(2)}) async-start(bf16[16,1536]{1,0:T(8,128)(2,1)} %param.15), calls=%async_computation.5 | async-start | bytes 49152 | tf_op jit(solution)/shard_map/slice | solution.py:270
  7.2 80.2 %all-gather.4.cloned.1.call-start = ((), (), s32[]{:S(2)}) async-start(), calls=%async_computation.2 | async-start | bytes 5308416 | tf_op jit(solution)/shard_map/all_gather | solution.py:320
  7.9 156.4 %all-gather.6.cloned.1.call-start = ((), (), s32[]{:S(2)}) async-start(), calls=%async_computation.3 | async-start | bytes 7077888 | tf_op jit(solution)/shard_map/all_gather | solution.py:321
  10.2 26.5 %copy-start.6 = (bf16[16,1024]{1,0:T(8,128)(2,1)S(1)}, bf16[16,1024]{1,0:T(8,128)(2,1)}, u32[]{:S(2)}) copy-start(bf16[16,1024]{1,0:T(8,128)(2,1)} %param.16) | copy-start | bytes 98308
  10.2 26.7 %copy-start.5 = (s32[128,8]{0,1:T(8,128)S(1)}, s32[128,8]{0,1:T(8,128)}, u32[]{:S(2)}) copy-start(s32[128,8]{0,1:T(8,128)} %param.27) | copy-start | bytes 12292
  15.0 25.9 %all-to-all-start = ((f32[16,1,1537]{2,1,0:T(1,128)}), f32[16,1,1537]{2,1,0:T(1,128)S(1)}, u32[]{:S(2)}, u32[]{:S(2)}) async-start(f32[16,1,1537]{2,1,0:T(1,128)} %copy.103), calls=%async_computation | async-start | bytes 212992 | tf_op jit(solution)/shard_map/all_to_all | solution.py:185
  22.1 152.4 %all-gather.8.cloned.1.call-start = ((), (), s32[]{:S(2)}) async-start(), calls=%async_computation.4 | async-start | bytes 3538944 | tf_op jit(solution)/shard_map/all_gather | solution.py:322
  24.5 16.5 %copy-start.7 = (bf16[1536]{0:T(1024)(128)(2,1)S(1)}, bf16[1536]{0:T(1024)(128)(2,1)}, u32[]{:S(2)}) copy-start(bf16[1536]{0:T(1024)(128)(2,1)} %param.25) | copy-start | bytes 9220
  65.6 21.9 %copy-start.1 = (bf16[128,1536]{1,0:T(8,128)(2,1)S(1)}, bf16[128,1536]{1,0:T(8,128)(2,1)}, u32[]{:S(2)}) copy-start(bf16[128,1536]{1,0:T(8,128)(2,1)} %param.23) | copy-start | bytes 1179652
  65.6 21.9 %copy-start.2 = (bf16[112,1536]{1,0:T(8,128)(2,1)S(1)}, bf16[112,1536]{1,0:T(8,128)(2,1)}, u32[]{:S(2)}) copy-start(bf16[112,1536]{1,0:T(8,128)(2,1)} %param.22) | copy-start | bytes 1032196
  67.6 15.1 %all-to-all-start.1 = ((f32[16,1,8,3,66]{4,2,3,1,0:T(8,128)}), f32[16,1,8,3,66]{4,2,3,1,0:T(8,128)S(1)}, u32[]{:S(2)}, u32[]{:S(2)}) async-start(f32[16,1,8,3,66]{4,2,3,1,0:T(8,128)} %copy.108), calls=%async_computation.1 | async-start | bytes 393216 | tf_op jit(solution)/shard_map/all_to_all | solution.py:185
  87.4 7.5 %copy-start.3 = (bf16[16,1536]{1,0:T(8,128)(2,1)}, bf16[16,1536]{1,0:T(8,128)(2,1)S(1)}, u32[]{:S(2)}) copy-start(bf16[16,1536]{1,0:T(8,128)(2,1)S(1)} %fusion.24) | copy-start | bytes 147460
Sparse Core Ops, SparseCore 0:
  9.7 34.7 all-gather.3
  46.2 41.0 all-gather.5
  89.0 27.8 all-gather.7

commit v5 on v3

--- a/solution.py
+++ b/solution.py
@@ -286,25 +286,27 @@
     slot_hits = row_hits.T[:, None, :] & (
         counts.T[:, None, :] == jnp.arange(CAP, dtype=jnp.int32)[None, :, None]
     )
-    outgoing_rows = (
-        jnp.einsum(
-            "ecr,rd->ecd",
-            slot_hits.astype(jnp.bfloat16),
+    chunk_hits = slot_hits.reshape(columns, experts_dev, CAP, row_count)
+    returned_parts = []
+    for local in range(experts_dev):
+        outgoing = jnp.einsum(
+            "scr,rd->scd",
+            chunk_hits[:, local].astype(jnp.bfloat16),
             normed,
             preferred_element_type=jnp.float32,
+        ).astype(jnp.bfloat16)
+        arrived = lax.all_to_all(outgoing, "gy", split_axis=0, concat_axis=0, tiled=True)
+        gate_pair = jnp.einsum(
+            "scd,df->scf", arrived, full_pair[:, local], preferred_element_type=jnp.float32
         )
-        .astype(jnp.bfloat16)
-        .reshape(columns, experts_dev, CAP, D)
-    )
-    arrived = lax.all_to_all(outgoing_rows, "gy", split_axis=0, concat_axis=0, tiled=True)
-    gate_pair = jnp.einsum("secd,def->secf", arrived, full_pair, preferred_element_type=jnp.float32)
-    hidden = (jax.nn.silu(gate_pair[..., :FF]) * gate_pair[..., FF:]).astype(jnp.bfloat16)
-    expert_rows = jnp.einsum(
-        "secf,def->secd", hidden, full_down, preferred_element_type=jnp.float32
-    ).astype(jnp.bfloat16)
-    returned = lax.all_to_all(expert_rows, "gy", split_axis=0, concat_axis=0, tiled=True).reshape(
-        EXPERTS * CAP, D
-    )
+        hidden = (jax.nn.silu(gate_pair[..., :FF]) * gate_pair[..., FF:]).astype(jnp.bfloat16)
+        expert_rows = jnp.einsum(
+            "scf,df->scd", hidden, full_down[:, local], preferred_element_type=jnp.float32
+        ).astype(jnp.bfloat16)
+        returned_parts.append(
+            lax.all_to_all(expert_rows, "gy", split_axis=0, concat_axis=0, tiled=True)
+        )
+    returned = jnp.stack(returned_parts, axis=1).reshape(EXPERTS * CAP, D)
     picked = returned[targets].astype(jnp.float32).reshape(row_count, TOP, D)
     layer_out = stream + jnp.sum(gate_weights[:, :, None] * picked, axis=1)
     return (attended, layer_out)

time: 282 us -> 270 us (0.957)
  waiting for transfers between devices: 140 us -> 118 us
  starting transfers between devices: 24 us -> 30.6 us
  matrix products: 25.2 us -> 28.7 us
    all_to_all x1 -> x2, waiting for transfers between devices: 67 us -> 51.3 us  [body(): lax.all_to_all(outgoing, 'gy', split_axis=0, concat_axis=0, tiled=True)]
    all_to_all x1 -> x2, waiting for transfers between devices: 63.9 us -> 57.8 us  [body(): lax.all_to_all(expert_rows, 'gy', split_axis=0, concat_axis=0, tiled=True)]
    dot_general x3 -> x6, matrix products: 20.3 us -> 24.6 us  [the longest x2 12.2 us: body(): jnp.einsum('scd,df->scf', arrived, full_pair[:, local], preferred_element...]
    unnamed x20 -> x36, local copies, waits for them, and re-layouts: 3.5 us -> 7.16 us
    all_to_all x1 -> x2, starting transfers between devices: 4.91 us -> 8.17 us  [body(): lax.all_to_all(expert_rows, 'gy', split_axis=0, concat_axis=0, tiled=True)]
    all_to_all x1 -> x2, starting transfers between devices: 4.7 us -> 7.63 us  [body(): lax.all_to_all(outgoing, 'gy', split_axis=0, concat_axis=0, tiled=True)]
  transfers between devices with their start and end apart: 7 -> 9, of which waited for: 3 -> 5; matrix products, arithmetic and copies ran while one was open for 17% -> 20% of each run, Pallas kernels for 10% -> 10%
where the time goes in v5:
time: 270 us; the launch traced here: 266 us
  waiting for transfers between devices  118 us (44%)
  local copies, waits for them, and re-layouts  35.3 us (13%)
  starting transfers between devices  30.6 us (11%)
  matrix products  28.7 us (11%)
  Pallas kernels  27.7 us (10%)
  between operations  14.4 us (5%)
  other arithmetic  11.2 us (4%)
    all_to_all x2, waiting for transfers between devices, body(): lax.all_to_all(expert_rows, 'gy', split_axis=0, concat_axis=0, tiled=True)  57.8 us
    all_to_all x2, waiting for transfers between devices, body(): lax.all_to_all(outgoing, 'gy', split_axis=0, concat_axis=0, tiled=True)  51.3 us
    pallas_call x2, Pallas kernels, paged_attend(): pl.pallas_call(attend_kernel, grid_spec=grid_spec, out_shape=[jax.ShapeDt...  27.7 us
    all_to_all x2, starting transfers between devices, in_one_piece(): lax.all_to_all(both, axis, split_axis=split_dim, concat_axis=concat_dim,...  14.7 us
    dot_general x2, matrix products, body(): jnp.einsum('scd,df->scf', arrived, full_pair[:, local], preferred_element...  12.2 us
    gather x1, local copies, waits for them, and re-layouts, body(): picked = returned[targets].astype(jnp.float32).reshape(row_count, TOP, D)  9.6 us
    all_to_all x2, waiting for transfers between devices, in_one_piece(): lax.all_to_all(both, axis, split_axis=split_dim, concat_axis=concat_dim,...  8.33 us
    all_to_all x2, starting transfers between devices, body(): lax.all_to_all(expert_rows, 'gy', split_axis=0, concat_axis=0, tiled=True)  8.17 us
  transfers between devices with their start and end apart: 9, of which 5 were waited for; matrix products, arithmetic and copies ran while one was open for 20% of the time, Pallas kernels for 10%

profile of v5, /device:TPU:96, one launch (start us, length us, event | category | flops | bytes accessed | tf_op | source)
XLA Modules:
  0.0 266.1 jit_solution(1026968962386927519)
XLA Ops:
  8.0 2.2 copy.126
  12.3 7.0 %all-to-all-start = ((f32[16,1,1537]{2,1,0:T(1,128)}), f32[16,1,1537]{2,1,0:T(1,128)S(1)}, u32[]{:S(2)}, u32[]{:S(2)}) async-start(f32[16,1,1537]{2,1,0:T(1,128)} %copy.103), calls=%async_computation | async-start | bytes 212992 | tf_op jit(solution)/shard_map/all_to_all | solution.py:124
  22.6 10.1 %shard_map.158 = (f32[8,24,128]{2,1,0:T(8,128)}, f32[8,24,128]{2,1,0:T(8,128)}, f32[8,24,512]{2,1,0:T(8,128)}) custom-call(s32[8,32]{1,0:T(8,128)} %tables.2, s32[8]{0:T(128)} %get-tuple-element.28.lengths, bf16[8,24,512]{2,1,0:T(8,128)(2,1)} %broadcast_select_fusion.1.q_ref, bf16[128,16,1024]{2,1,0:T(8,128)(2,1)} %pool_ref.3), custom_call_target="tpu_custom_call" | custom-call | flops 201326592 | bytes 8388608 | tf_op jit(solution)/shard_map/pallas_call | solution.py:96
  33.7 1.0 slice_reduce_fusion
  35.2 1.2 reshape.168
  39.8 17.6 %shard_map.159 = (f32[16,24,128]{2,1,0:T(8,128)}, f32[16,24,128]{2,1,0:T(8,128)}, f32[16,24,512]{2,1,0:T(8,128)}) custom-call(s32[16,32]{1,0:T(8,128)} %tables.3, s32[16]{0:T(128)} %fusion.24.lengths, bf16[16,24,512]{2,1,0:T(8,128)(2,1)} %broadcast_select_fusion.q_ref, bf16[128,16,1024]{2,1,0:T(8,128)(2,1)} %pool_ref.3), custom_call_target="tpu_custom_call" | custom-call | flops 402653184 | bytes 16777216 | tf_op jit(solution)/shard_map/pallas_call | solution.py:96
  57.3 1.2 copy.104
  58.5 1.2 copy.105
  60.3 1.5 reshape.164
  63.5 7.7 %all-to-all-start.1 = ((f32[16,1,8,3,66]{4,2,3,1,0:T(8,128)}), f32[16,1,8,3,66]{4,2,3,1,0:T(8,128)S(1)}, u32[]{:S(2)}, u32[]{:S(2)}) async-start(f32[16,1,8,3,66]{4,2,3,1,0:T(8,128)} %copy.108), calls=%async_computation.1 | async-start | bytes 393216 | tf_op jit(solution)/shard_map/all_to_all | solution.py:124
  71.2 8.3 %all-to-all-done.1 = f32[16,1,8,3,66]{4,2,3,1,0:T(8,128)S(1)} async-done(((f32[16,1,8,3,66]{4,2,3,1,0:T(8,128)}), f32[16,1,8,3,66]{4,2,3,1,0:T(8,128)S(1)}, u32[]{:S(2)}, u32[]{:S(2)}) %all-to-all-start.1) | async-done | bytes 101408 | tf_op jit(solution)/shard_map/all_to_all | solution.py:124
  84.3 3.3 %multiply_reduce_fusion = (f32[128]{0:T(128)S(1)}, f32[128,1536]{1,0:T(8,128)S(1)}) fusion(bf16[1536,1536]{1,0:T(8,128)(2,1)} %all-gather.4.cloned.1.call-done, bf16[112,1536]{1,0:T(8,128)(2,1)S(1)} %copy-done.7, bf16[16,1536]{1,0:T(8,128)(2,1)S(1)} %fusion.19, bf16[128,1536]{1,0:T(8,128)(2,1)S(1)} %copy-done.5), kind=kOutput, calls=%fused_computation.29 | convolution fusion | flops 605552512 | bytes 6291968 | tf_op jit(solution)/shard_map/dot_general | solution.py:262
  88.6 2.2 convolution_convert_fusion.1
  90.7 3.7 %all-to-all-start.4 = ((bf16[16,48,1536]{2,1,0:T(8,128)(2,1)}), bf16[16,48,1536]{2,1,0:T(8,128)(2,1)S(1)}, u32[]{:S(2)}, u32[]{:S(2)}) async-start(bf16[16,48,1536]{2,1,0:T(8,128)(2,1)} %convolution_convert_fusion.1), calls=%async_computation.4 | async-start | bytes 4718592 | tf_op jit(solution)/shard_map/all_to_all | solution.py:298
  94.5 2.2 convolution_convert_fusion.3
  96.7 29.3 %all-to-all-done.4 = bf16[16,48,1536]{2,1,0:T(8,128)(2,1)S(1)} async-done(((bf16[16,48,1536]{2,1,0:T(8,128)(2,1)}), bf16[16,48,1536]{2,1,0:T(8,128)(2,1)S(1)}, u32[]{:S(2)}, u32[]{:S(2)}) %all-to-all-start.4) | async-done | bytes 2359328 | tf_op jit(solution)/shard_map/all_to_all | solution.py:298
  125.9 1.4 copy-done.4
  127.3 3.9 %all-to-all-start.2 = ((bf16[16,48,1536]{2,1,0:T(8,128)(2,1)}), bf16[16,48,1536]{2,1,0:T(8,128)(2,1)S(1)}, u32[]{:S(2)}, u32[]{:S(2)}) async-start(bf16[16,48,1536]{2,1,0:T(8,128)(2,1)} %convolution_convert_fusion.3), calls=%async_computation.2 | async-start | bytes 4718592 | tf_op jit(solution)/shard_map/all_to_all | solution.py:298
  131.3 6.8 %fusion.1 = f32[16,48,1024]{2,1,0:T(8,128)} fusion(bf16[16,48,1536]{2,1,0:T(8,128)(2,1)} %copy-done.4, bf16[1536,2,1024]{2,0,1:T(8,128)(2,1)} %all-gather.6.cloned.1.call-done), kind=kOutput, calls=%fused_computation.12 | convolution fusion | flops 2415919104 | bytes 8650752 | tf_op jit(solution)/shard_map/scd,df->scf/dot_general | solution.py:299
  138.1 5.2 %convolution_convert_fusion = bf16[16,48,1536]{2,1,0:T(8,128)(2,1)} fusion(bf16[1536,2,512]{2,0,1:T(8,128)(2,1)} %all-gather.8.cloned.1.call-done, f32[16,48,1024]{2,1,0:T(8,128)} %fusion.1), kind=kOutput, calls=%fused_computation.7 | convolution fusion | flops 1211498496 | bytes 7077888 | tf_op jit(solution)/shard_map/scf,df->scd/dot_general | solution.py:303
  143.3 22.0 %all-to-all-done.2 = bf16[16,48,1536]{2,1,0:T(8,128)(2,1)S(1)} async-done(((bf16[16,48,1536]{2,1,0:T(8,128)(2,1)}), bf16[16,48,1536]{2,1,0:T(8,128)(2,1)S(1)}, u32[]{:S(2)}, u32[]{:S(2)}) %all-to-all-start.2) | async-done | bytes 2359328 | tf_op jit(solution)/shard_map/all_to_all | solution.py:298
  165.3 1.4 copy-done.3
  166.7 3.7 %all-to-all-start.5 = ((bf16[16,48,1536]{2,1,0:T(8,128)(2,1)}), bf16[16,48,1536]{2,1,0:T(8,128)(2,1)S(1)}, u32[]{:S(2)}, u32[]{:S(2)}) async-start(bf16[16,48,1536]{2,1,0:T(8,128)(2,1)} %convolution_convert_fusion), calls=%async_computation.5 | async-start | bytes 4718592 | tf_op jit(solution)/shard_map/all_to_all | solution.py:307
  170.4 5.3 %fusion.2 = f32[16,48,1024]{2,1,0:T(8,128)S(1)} fusion(bf16[16,48,1536]{2,1,0:T(8,128)(2,1)} %copy-done.3, bf16[1536,2,1024]{2,0,1:T(8,128)(2,1)} %all-gather.6.cloned.1.call-done), kind=kOutput, calls=%fused_computation.14 | convolution fusion | flops 2415919104 | bytes 8650752 | tf_op jit(solution)/shard_map/scd,df->scf/dot_general | solution.py:299
  175.8 2.8 %convolution_convert_fusion.2 = bf16[16,48,1536]{2,1,0:T(8,128)(2,1)} fusion(bf16[1536,2,512]{2,0,1:T(8,128)(2,1)S(1)} %copy-done.15, f32[16,48,1024]{2,1,0:T(8,128)S(1)} %fusion.2), kind=kOutput, calls=%fused_computation.9 | convolution fusion | flops 1211498496 | bytes 7077888 | tf_op jit(solution)/shard_map/scf,df->scd/dot_general | solution.py:303
  178.6 25.8 %all-to-all-done.5 = bf16[16,48,1536]{2,1,0:T(8,128)(2,1)S(1)} async-done(((bf16[16,48,1536]{2,1,0:T(8,128)(2,1)}), bf16[16,48,1536]{2,1,0:T(8,128)(2,1)S(1)}, u32[]{:S(2)}, u32[]{:S(2)}) %all-to-all-start.5) | async-done | bytes 2359328 | tf_op jit(solution)/shard_map/all_to_all | solution.py:307
  204.4 4.4 %all-to-all-start.3 = ((bf16[16,48,1536]{2,1,0:T(8,128)(2,1)}), bf16[16,48,1536]{2,1,0:T(8,128)(2,1)}, u32[]{:S(2)}, u32[]{:S(2)}) async-start(bf16[16,48,1536]{2,1,0:T(8,128)(2,1)} %convolution_convert_fusion.2), calls=%async_computation.3 | async-start | bytes 4718592 | tf_op jit(solution)/shard_map/all_to_all | solution.py:307
  209.6 32.0 %all-to-all-done.3 = bf16[16,48,1536]{2,1,0:T(8,128)(2,1)} async-done(((bf16[16,48,1536]{2,1,0:T(8,128)(2,1)}), bf16[16,48,1536]{2,1,0:T(8,128)(2,1)}, u32[]{:S(2)}, u32[]{:S(2)}) %all-to-all-start.3) | async-done | bytes 2359328 | tf_op jit(solution)/shard_map/all_to_all | solution.py:307
  241.6 2.1 pad_maximum_fusion
  243.7 2.4 copy.128
  246.1 9.6 %gather_fusion.3 = bf16[1024,1536]{1,0:T(8,128)(2,1)S(1)} fusion(bf16[1536,1536]{1,0:T(8,128)(2,1)} %bitcast.73, s32[1024]{0:T(1024)S(1)} %broadcast_clamp_fusion), kind=kCustom, calls=%fused_computation.3 | custom fusion | bytes 6295552 | tf_op jit(solution)/shard_map/gather | solution.py:310
  255.8 2.8 %fusion = f32[128,1536]{1,0:T(8,128)S(1)} fusion(bf16[1024,1536]{1,0:T(8,128)(2,1)S(1)} %gather_fusion.3, f32[128,8]{1,0:T(8,128)S(1)} %copy.123), kind=kLoop, calls=%fused_computation.5 | loop fusion | flops 4521984 | bytes 3936256 | tf_op jit(solution)/shard_map/reduce_sum | solution.py:311
  (130 shorter events, 20.4 us)
Async XLA Ops:
  7.2 202.0 %copy-start = (bf16[1536,32]{0,1:T(8,128)(2,1)S(1)}, bf16[1536,32]{0,1:T(8,128)(2,1)}, u32[]{:S(2)}) copy-start(bf16[1536,32]{0,1:T(8,128)(2,1)} %param.26) | copy-start | bytes 294916
  7.2 3.1 %copy-start.12 = (s32[8]{0:T(128)S(1)}, s32[8]{0:T(128)}, u32[]{:S(2)}) copy-start(s32[8]{0:T(128)} %param.20) | copy-start | bytes 100
  7.2 3.4 %copy-start.14 = (s32[16]{0:T(128)S(1)}, s32[16]{0:T(128)}, u32[]{:S(2)}) copy-start(s32[16]{0:T(128)} %param.18) | copy-start | bytes 196
  7.2 4.1 %copy-start.9 = (bf16[16,1536]{1,0:T(8,128)(2,1)S(1)}, bf16[16,1536]{1,0:T(8,128)(2,1)}, u32[]{:S(2)}) copy-start(bf16[16,1536]{1,0:T(8,128)(2,1)} %param.15) | copy-start | bytes 147460
  7.2 12.2 %copy-start.6 = (bf16[192,2,512]{2,1,0:T(2,128)(2,1)S(1)}, bf16[192,2,512]{2,1,0:T(2,128)(2,1)}, u32[]{:S(2)}) copy-start(bf16[192,2,512]{2,1,0:T(2,128)(2,1)} %param.29) | copy-start | bytes 1179652
  7.2 77.0 %all-gather.4.cloned.1.call-start = ((), (), s32[]{:S(2)}) async-start(), calls=%async_computation.6 | async-start | bytes 5308416 | tf_op jit(solution)/shard_map/all_gather | solution.py:259
  8.0 12.4 %copy-start.10 = (s32[128,8]{0,1:T(8,128)S(1)}, s32[128,8]{0,1:T(8,128)}, u32[]{:S(2)}) copy-start(s32[128,8]{0,1:T(8,128)} %param.27) | copy-start | bytes 12292
  8.0 12.7 %copy-start.13 = (bf16[1536]{0:T(1024)(128)(2,1)S(1)}, bf16[1536]{0:T(1024)(128)(2,1)}, u32[]{:S(2)}) copy-start(bf16[1536]{0:T(1024)(128)(2,1)} %param.25) | copy-start | bytes 9220
  8.0 12.9 %slice-start = ((bf16[16,1536]{1,0:T(8,128)(2,1)}), bf16[8,1536]{1,0:T(8,128)(2,1)S(1)}, s32[]{:S(2)}) async-start(bf16[16,1536]{1,0:T(8,128)(2,1)} %param.15), calls=%async_computation.9 | async-start | bytes 49152 | tf_op jit(solution)/shard_map/slice | solution.py:209
  8.0 13.0 %copy-start.11 = (bf16[16,1024]{1,0:T(8,128)(2,1)S(1)}, bf16[16,1024]{1,0:T(8,128)(2,1)}, u32[]{:S(2)}) copy-start(bf16[16,1024]{1,0:T(8,128)(2,1)} %param.16) | copy-start | bytes 98308
  8.0 123.3 %all-gather.6.cloned.1.call-start = ((), (), s32[]{:S(2)}) async-start(), calls=%async_computation.7 | async-start | bytes 7077888 | tf_op jit(solution)/shard_map/all_gather | solution.py:260
  12.3 24.7 %all-to-all-start = ((f32[16,1,1537]{2,1,0:T(1,128)}), f32[16,1,1537]{2,1,0:T(1,128)S(1)}, u32[]{:S(2)}, u32[]{:S(2)}) async-start(f32[16,1,1537]{2,1,0:T(1,128)} %copy.103), calls=%async_computation | async-start | bytes 212992 | tf_op jit(solution)/shard_map/all_to_all | solution.py:124
  19.4 118.8 %all-gather.8.cloned.1.call-start = ((), (), s32[]{:S(2)}) async-start(), calls=%async_computation.8 | async-start | bytes 3538944 | tf_op jit(solution)/shard_map/all_gather | solution.py:261
  63.5 16.0 %all-to-all-start.1 = ((f32[16,1,8,3,66]{4,2,3,1,0:T(8,128)}), f32[16,1,8,3,66]{4,2,3,1,0:T(8,128)S(1)}, u32[]{:S(2)}, u32[]{:S(2)}) async-start(f32[16,1,8,3,66]{4,2,3,1,0:T(8,128)} %copy.108), calls=%async_computation.1 | async-start | bytes 393216 | tf_op jit(solution)/shard_map/all_to_all | solution.py:124
  80.2 4.0 %copy-start.5 = (bf16[128,1536]{1,0:T(8,128)(2,1)S(1)}, bf16[128,1536]{1,0:T(8,128)(2,1)}, u32[]{:S(2)}) copy-start(bf16[128,1536]{1,0:T(8,128)(2,1)} %param.23) | copy-start | bytes 1179652
  80.2 4.0 %copy-start.7 = (bf16[112,1536]{1,0:T(8,128)(2,1)S(1)}, bf16[112,1536]{1,0:T(8,128)(2,1)}, u32[]{:S(2)}) copy-start(bf16[112,1536]{1,0:T(8,128)(2,1)} %param.22) | copy-start | bytes 1032196
  84.2 3.3 %copy-start.8 = (bf16[16,1536]{1,0:T(8,128)(2,1)}, bf16[16,1536]{1,0:T(8,128)(2,1)S(1)}, u32[]{:S(2)}) copy-start(bf16[16,1536]{1,0:T(8,128)(2,1)S(1)} %fusion.19) | copy-start | bytes 147460
  87.5 0.9 copy-start.1
  90.7 35.2 %all-to-all-start.4 = ((bf16[16,48,1536]{2,1,0:T(8,128)(2,1)}), bf16[16,48,1536]{2,1,0:T(8,128)(2,1)S(1)}, u32[]{:S(2)}, u32[]{:S(2)}) async-start(bf16[16,48,1536]{2,1,0:T(8,128)(2,1)} %convolution_convert_fusion.1), calls=%async_computation.4 | async-start | bytes 4718592 | tf_op jit(solution)/shard_map/all_to_all | solution.py:298
  125.9 1.4 copy-start.4
  127.3 38.0 %all-to-all-start.2 = ((bf16[16,48,1536]{2,1,0:T(8,128)(2,1)}), bf16[16,48,1536]{2,1,0:T(8,128)(2,1)S(1)}, u32[]{:S(2)}, u32[]{:S(2)}) async-start(bf16[16,48,1536]{2,1,0:T(8,128)(2,1)} %convolution_convert_fusion.3), calls=%async_computation.2 | async-start | bytes 4718592 | tf_op jit(solution)/shard_map/all_to_all | solution.py:298
  165.3 1.4 copy-start.3
  166.7 37.7 %all-to-all-start.5 = ((bf16[16,48,1536]{2,1,0:T(8,128)(2,1)}), bf16[16,48,1536]{2,1,0:T(8,128)(2,1)S(1)}, u32[]{:S(2)}, u32[]{:S(2)}) async-start(bf16[16,48,1536]{2,1,0:T(8,128)(2,1)} %convolution_convert_fusion), calls=%async_computation.5 | async-start | bytes 4718592 | tf_op jit(solution)/shard_map/all_to_all | solution.py:307
  170.4 5.4 %copy-start.15 = (bf16[1536,2,512]{2,0,1:T(8,128)(2,1)S(1)}, bf16[1536,2,512]{2,0,1:T(8,128)(2,1)}, u32[]{:S(2)}) copy-start(bf16[1536,2,512]{2,0,1:T(8,128)(2,1)} %all-gather.8.cloned.1.call-done) | copy-start | bytes 9437188
  204.4 37.2 %all-to-all-start.3 = ((bf16[16,48,1536]{2,1,0:T(8,128)(2,1)}), bf16[16,48,1536]{2,1,0:T(8,128)(2,1)}, u32[]{:S(2)}, u32[]{:S(2)}) async-start(bf16[16,48,1536]{2,1,0:T(8,128)(2,1)} %convolution_convert_fusion.2), calls=%async_computation.3 | async-start | bytes 4718592 | tf_op jit(solution)/shard_map/all_to_all | solution.py:307
  255.8 2.8 %copy-start.2 = (f32[128,1536]{1,0:T(8,128)S(1)}, f32[128,1536]{1,0:T(8,128)}, u32[]{:S(2)}) copy-start(f32[128,1536]{1,0:T(8,128)} %copy-done.1) | copy-start | bytes 2359300
Sparse Core Ops, SparseCore 0:
  9.7 33.6 all-gather.3
  45.1 41.0 all-gather.5
  87.9 28.7 all-gather.7

commit v6 on v5

--- a/solution.py
+++ b/solution.py
@@ -28,17 +28,24 @@
     n = pl.num_programs(0)
     half = KV_HEADS * HEAD
 
+    def pages_of(req):
+        return (lengths[req] + PAGE - 1) // PAGE
+
+    def page_copy(req, slot, p):
+        return pltpu.make_async_copy(
+            pool_ref.at[tables[req, p]], kvbuf.at[slot, p], sems.at[slot, p]
+        )
+
     def start(req, slot):
         def one(p, carry):
-            pltpu.make_async_copy(
-                pool_ref.at[tables[req, p]], kvbuf.at[slot, p], sems.at[slot]
-            ).start()
+            page_copy(req, slot, p).start()
             return carry
 
-        lax.fori_loop(0, NPAGE, one, 0, unroll=8)
+        lax.fori_loop(0, pages_of(req), one, 0)
 
     @pl.when(r == 0)
     def _():
+        kvbuf[...] = jnp.zeros(kvbuf.shape, kvbuf.dtype)
         start(0, 0)
 
     slot = r % 2
@@ -47,7 +54,11 @@
     def _():
         start(r + 1, 1 - slot)
 
-    pltpu.make_async_copy(pool_ref.at[pl.ds(0, NPAGE)], kvbuf.at[slot], sems.at[slot]).wait()
+    def wait_one(p, carry):
+        page_copy(r, slot, p).wait()
+        return carry
+
+    lax.fori_loop(0, pages_of(r), wait_one, 0)
     kv = kvbuf.at[slot]
     keys = kv[:, :, :half].reshape(MAXLEN, half)
     values = kv[:, :, half:].reshape(MAXLEN, half)
@@ -90,7 +101,7 @@
         ],
         scratch_shapes=[
             pltpu.VMEM((2, NPAGE, PAGE, kv_width), pool.dtype),
-            pltpu.SemaphoreType.DMA((2,)),
+            pltpu.SemaphoreType.DMA((2, NPAGE)),
         ],
     )
     top, total, mix = pl.pallas_call(
@@ -281,7 +292,6 @@
         earlier_rows, row_hits.astype(jnp.bfloat16), preferred_element_type=jnp.float32
     ).astype(jnp.int32)
     place_of = jnp.sum(jnp.where(selector, counts[:, None, :], 0), axis=2)
-    targets = (routes * CAP + place_of).reshape(row_count * TOP)
     experts_dev = full_pair.shape[1]
     slot_hits = row_hits.T[:, None, :] & (
         counts.T[:, None, :] == jnp.arange(CAP, dtype=jnp.int32)[None, :, None]
@@ -306,8 +316,21 @@
         returned_parts.append(
             lax.all_to_all(expert_rows, "gy", split_axis=0, concat_axis=0, tiled=True)
         )
-    returned = jnp.stack(returned_parts, axis=1).reshape(EXPERTS * CAP, D)
-    picked = returned[targets].astype(jnp.float32).reshape(row_count, TOP, D)
+    flat_place = place_of.reshape(row_count * TOP)
+    flat_expert = routes.reshape(row_count * TOP)
+    picked = None
+    for local, part in enumerate(returned_parts):
+        spot = jnp.where(
+            flat_expert % experts_dev == local, flat_expert // experts_dev * CAP + flat_place, -1
+        )
+        one_hot = (spot[:, None] == jnp.arange(columns * CAP, dtype=jnp.int32)[None, :]).astype(
+            jnp.bfloat16
+        )
+        share = jnp.dot(
+            one_hot, part.reshape(columns * CAP, D), preferred_element_type=jnp.float32
+        )
+        picked = share if picked is None else picked + share
+    picked = picked.reshape(row_count, TOP, D)
     layer_out = stream + jnp.sum(gate_weights[:, :, None] * picked, axis=1)
     return (attended, layer_out)
 

time: 270 us -> 253 us (0.937)
  local copies, waits for them, and re-layouts: 35.3 us -> 19.9 us
  matrix products: 28.7 us -> 41.7 us
  waiting for transfers between devices: 118 us -> 110 us
  other arithmetic: 11.2 us -> 6.35 us
  Pallas kernels: 27.7 us -> 24.2 us
    dot_general x0 -> x2, matrix products: none -> 13.1 us  [body(): jnp.dot(one_hot, part.reshape(columns * CAP, D), preferred_element_type=j...]
    gather x1 -> x0, local copies, waits for them, and re-layouts: 9.6 us -> none  [body(): picked = returned[targets].astype(jnp.float32).reshape(row_count, TOP, D)]
    all_to_all x2, waiting for transfers between devices: 57.8 us -> 49.7 us  [body(): lax.all_to_all(expert_rows, 'gy', split_axis=0, concat_axis=0, tiled=True)]
    unnamed x36 -> x29, local copies, waits for them, and re-layouts: 7.16 us -> 3.6 us
    pallas_call x2, Pallas kernels: 27.7 us -> 24.2 us  [paged_attend(): pl.pallas_call(attend_kernel, grid_spec=grid_spec, out_shape=[jax.ShapeDt...]
    reduce_sum x1 -> x0, other arithmetic: 2.79 us -> none  [body(): layer_out = stream + jnp.sum(gate_weights[:, :, None] * picked, axis=1)]
  transfers between devices with their start and end apart: 9 -> 9, of which waited for: 5 -> 5; matrix products, arithmetic and copies ran while one was open for 20% -> 24% of each run, Pallas kernels for 10% -> 10%
where the time goes in v6:
time: 253 us; the launch traced here: 250 us
  waiting for transfers between devices  110 us (43%)
  matrix products  41.7 us (16%)
  starting transfers between devices  33 us (13%)
  Pallas kernels  24.2 us (10%)
  local copies, waits for them, and re-layouts  19.9 us (8%)
  between operations  14.3 us (6%)
  other arithmetic  6.35 us (3%)
    all_to_all x2, waiting for transfers between devices, body(): lax.all_to_all(outgoing, 'gy', split_axis=0, concat_axis=0, tiled=True)  51.2 us
    all_to_all x2, waiting for transfers between devices, body(): lax.all_to_all(expert_rows, 'gy', split_axis=0, concat_axis=0, tiled=True)  49.7 us
    pallas_call x2, Pallas kernels, paged_attend(): pl.pallas_call(attend_kernel, grid_spec=grid_spec, out_shape=[jax.ShapeDt...  24.2 us
    all_to_all x2, starting transfers between devices, in_one_piece(): lax.all_to_all(both, axis, split_axis=split_dim, concat_axis=concat_dim,...  15 us
    dot_general x2, matrix products, body(): jnp.dot(one_hot, part.reshape(columns * CAP, D), preferred_element_type=j...  13.1 us
    dot_general x2, matrix products, body(): jnp.einsum('scd,df->scf', arrived, full_pair[:, local], preferred_element...  12.2 us
    all_to_all x2, starting transfers between devices, body(): lax.all_to_all(outgoing, 'gy', split_axis=0, concat_axis=0, tiled=True)  9.08 us
    all_to_all x2, starting transfers between devices, body(): lax.all_to_all(expert_rows, 'gy', split_axis=0, concat_axis=0, tiled=True)  8.89 us
  transfers between devices with their start and end apart: 9, of which 5 were waited for; matrix products, arithmetic and copies ran while one was open for 24% of the time, Pallas kernels for 10%

profile of v6, /device:TPU:96, one launch (start us, length us, event | category | flops | bytes accessed | tf_op | source)
XLA Modules:
  0.0 249.5 jit_solution(8696608811959806178)
XLA Ops:
  8.0 2.2 copy.125
  12.3 7.0 %all-to-all-start = ((f32[16,1,1537]{2,1,0:T(1,128)}), f32[16,1,1537]{2,1,0:T(1,128)S(1)}, u32[]{:S(2)}, u32[]{:S(2)}) async-start(f32[16,1,1537]{2,1,0:T(1,128)} %copy.100), calls=%async_computation | async-start | bytes 212992 | tf_op jit(solution)/shard_map/all_to_all | solution.py:135
  22.6 9.5 %shard_map.158 = (f32[8,24,128]{2,1,0:T(8,128)}, f32[8,24,128]{2,1,0:T(8,128)}, f32[8,24,512]{2,1,0:T(8,128)}) custom-call(s32[8,32]{1,0:T(8,128)} %tables.2, s32[8]{0:T(128)} %get-tuple-element.30.lengths, bf16[8,24,512]{2,1,0:T(8,128)(2,1)} %broadcast_select_fusion.1.q_ref, bf16[128,16,1024]{2,1,0:T(8,128)(2,1)} %pool_ref.3), custom_call_target="tpu_custom_call" | custom-call | flops 201326592 | bytes 8388608 | tf_op jit(solution)/shard_map/pallas_call | solution.py:107
  32.1 1.0 slice_reduce_fusion.1
  33.1 1.0 slice_reduce_fusion
  34.5 1.2 reshape.221
  37.5 0.8 broadcast_select_fusion.q_ref
  38.3 0.9 fusion.27.lengths
  39.2 14.7 %shard_map.159 = (f32[16,24,128]{2,1,0:T(8,128)}, f32[16,24,128]{2,1,0:T(8,128)}, f32[16,24,512]{2,1,0:T(8,128)}) custom-call(s32[16,32]{1,0:T(8,128)} %tables.3, s32[16]{0:T(128)} %fusion.27.lengths, bf16[16,24,512]{2,1,0:T(8,128)(2,1)} %broadcast_select_fusion.q_ref, bf16[128,16,1024]{2,1,0:T(8,128)(2,1)} %pool_ref.3), custom_call_target="tpu_custom_call" | custom-call | flops 402653184 | bytes 16777216 | tf_op jit(solution)/shard_map/pallas_call | solution.py:107
  53.9 1.1 copy.101
  55.0 1.2 copy.102
  56.9 1.6 reshape.217
  60.1 7.9 %all-to-all-start.1 = ((f32[16,1,8,3,66]{4,2,3,1,0:T(8,128)}), f32[16,1,8,3,66]{4,2,3,1,0:T(8,128)S(1)}, u32[]{:S(2)}, u32[]{:S(2)}) async-start(f32[16,1,8,3,66]{4,2,3,1,0:T(8,128)} %copy.105), calls=%async_computation.1 | async-start | bytes 393216 | tf_op jit(solution)/shard_map/all_to_all | solution.py:135
  68.1 8.3 %all-to-all-done.1 = f32[16,1,8,3,66]{4,2,3,1,0:T(8,128)S(1)} async-done(((f32[16,1,8,3,66]{4,2,3,1,0:T(8,128)}), f32[16,1,8,3,66]{4,2,3,1,0:T(8,128)S(1)}, u32[]{:S(2)}, u32[]{:S(2)}) %all-to-all-start.1) | async-done | bytes 101408 | tf_op jit(solution)/shard_map/all_to_all | solution.py:135
  81.1 3.2 %multiply_reduce_fusion = (f32[128]{0:T(128)S(1)}, f32[128,1536]{1,0:T(8,128)S(1)}) fusion(bf16[1536,1536]{1,0:T(8,128)(2,1)} %all-gather.4.cloned.1.call-done, bf16[112,1536]{1,0:T(8,128)(2,1)S(1)} %copy-done.3, bf16[16,1536]{1,0:T(8,128)(2,1)S(1)} %fusion.22, bf16[128,1536]{1,0:T(8,128)(2,1)S(1)} %copy-done.1), kind=kOutput, calls=%fused_computation.32 | convolution fusion | flops 605552512 | bytes 6291968 | tf_op jit(solution)/shard_map/dot_general | solution.py:273
  84.5 2.2 convolution_convert_fusion.3
  86.7 4.4 %all-to-all-start.2 = ((bf16[16,48,1536]{2,1,0:T(8,128)(2,1)}), bf16[16,48,1536]{2,1,0:T(8,128)(2,1)}, u32[]{:S(2)}, u32[]{:S(2)}) async-start(bf16[16,48,1536]{2,1,0:T(8,128)(2,1)} %convolution_convert_fusion.3), calls=%async_computation.2 | async-start | bytes 4718592 | tf_op jit(solution)/shard_map/all_to_all | solution.py:308
  91.2 2.2 convolution_convert_fusion.1
  93.3 30.8 %all-to-all-done.2 = bf16[16,48,1536]{2,1,0:T(8,128)(2,1)} async-done(((bf16[16,48,1536]{2,1,0:T(8,128)(2,1)}), bf16[16,48,1536]{2,1,0:T(8,128)(2,1)}, u32[]{:S(2)}, u32[]{:S(2)}) %all-to-all-start.2) | async-done | bytes 2359328 | tf_op jit(solution)/shard_map/all_to_all | solution.py:308
  124.1 4.6 %all-to-all-start.4 = ((bf16[16,48,1536]{2,1,0:T(8,128)(2,1)}), bf16[16,48,1536]{2,1,0:T(8,128)(2,1)}, u32[]{:S(2)}, u32[]{:S(2)}) async-start(bf16[16,48,1536]{2,1,0:T(8,128)(2,1)} %convolution_convert_fusion.1), calls=%async_computation.4 | async-start | bytes 4718592 | tf_op jit(solution)/shard_map/all_to_all | solution.py:308
  128.7 6.8 %fusion.2 = f32[16,48,1024]{2,1,0:T(8,128)} fusion(bf16[16,48,1536]{2,1,0:T(8,128)(2,1)} %all-to-all-done.2, bf16[1536,2,1024]{2,0,1:T(8,128)(2,1)} %all-gather.6.cloned.1.call-done), kind=kOutput, calls=%fused_computation.12 | convolution fusion | flops 2415919104 | bytes 8650752 | tf_op jit(solution)/shard_map/scd,df->scf/dot_general | solution.py:309
  135.6 5.2 %convolution_convert_fusion.2 = bf16[16,48,1536]{2,1,0:T(8,128)(2,1)} fusion(bf16[1536,2,512]{2,0,1:T(8,128)(2,1)} %all-gather.8.cloned.1.call-done, f32[16,48,1024]{2,1,0:T(8,128)} %fusion.2), kind=kOutput, calls=%fused_computation.7 | convolution fusion | flops 1211498496 | bytes 7077888 | tf_op jit(solution)/shard_map/scf,df->scd/dot_general | solution.py:313
  140.8 20.5 %all-to-all-done.4 = bf16[16,48,1536]{2,1,0:T(8,128)(2,1)} async-done(((bf16[16,48,1536]{2,1,0:T(8,128)(2,1)}), bf16[16,48,1536]{2,1,0:T(8,128)(2,1)}, u32[]{:S(2)}, u32[]{:S(2)}) %all-to-all-start.4) | async-done | bytes 2359328 | tf_op jit(solution)/shard_map/all_to_all | solution.py:308
  161.2 4.5 %all-to-all-start.3 = ((bf16[16,48,1536]{2,1,0:T(8,128)(2,1)}), bf16[16,48,1536]{2,1,0:T(8,128)(2,1)}, u32[]{:S(2)}, u32[]{:S(2)}) async-start(bf16[16,48,1536]{2,1,0:T(8,128)(2,1)} %convolution_convert_fusion.2), calls=%async_computation.3 | async-start | bytes 4718592 | tf_op jit(solution)/shard_map/all_to_all | solution.py:317
  165.7 5.3 %fusion.1 = f32[16,48,1024]{2,1,0:T(8,128)S(1)} fusion(bf16[16,48,1536]{2,1,0:T(8,128)(2,1)} %all-to-all-done.4, bf16[1536,2,1024]{2,0,1:T(8,128)(2,1)} %all-gather.6.cloned.1.call-done), kind=kOutput, calls=%fused_computation.10 | convolution fusion | flops 2415919104 | bytes 8650752 | tf_op jit(solution)/shard_map/scd,df->scf/dot_general | solution.py:309
  171.1 2.9 %convolution_convert_fusion = bf16[16,48,1536]{2,1,0:T(8,128)(2,1)} fusion(bf16[1536,2,512]{2,0,1:T(8,128)(2,1)S(1)} %copy-done.11, f32[16,48,1024]{2,1,0:T(8,128)S(1)} %fusion.1), kind=kOutput, calls=%fused_computation.5 | convolution fusion | flops 1211498496 | bytes 7077888 | tf_op jit(solution)/shard_map/scf,df->scd/dot_general | solution.py:313
  173.9 24.4 %all-to-all-done.3 = bf16[16,48,1536]{2,1,0:T(8,128)(2,1)} async-done(((bf16[16,48,1536]{2,1,0:T(8,128)(2,1)}), bf16[16,48,1536]{2,1,0:T(8,128)(2,1)}, u32[]{:S(2)}, u32[]{:S(2)}) %all-to-all-start.3) | async-done | bytes 2359328 | tf_op jit(solution)/shard_map/all_to_all | solution.py:317
  198.3 4.4 %all-to-all-start.5 = ((bf16[16,48,1536]{2,1,0:T(8,128)(2,1)}), bf16[16,48,1536]{2,1,0:T(8,128)(2,1)}, u32[]{:S(2)}, u32[]{:S(2)}) async-start(bf16[16,48,1536]{2,1,0:T(8,128)(2,1)} %convolution_convert_fusion), calls=%async_computation.5 | async-start | bytes 4718592 | tf_op jit(solution)/shard_map/all_to_all | solution.py:317
  203.6 6.3 %fusion.3 = f32[1024,1536]{1,0:T(8,128)} fusion(bf16[768,1536]{1,0:T(8,128)(2,1)} %bitcast.19, s32[1024]{0:T(1024)S(1)} %get-tuple-element.24), kind=kOutput, calls=%fused_computation.15 | convolution fusion | flops 2416705536 | bytes 8654848 | tf_op jit(solution)/shard_map/dot_general | solution.py:329
  209.9 25.3 %all-to-all-done.5 = bf16[16,48,1536]{2,1,0:T(8,128)(2,1)} async-done(((bf16[16,48,1536]{2,1,0:T(8,128)(2,1)}), bf16[16,48,1536]{2,1,0:T(8,128)(2,1)}, u32[]{:S(2)}, u32[]{:S(2)}) %all-to-all-start.5) | async-done | bytes 2359328 | tf_op jit(solution)/shard_map/all_to_all | solution.py:317
  235.3 6.7 %fusion = f32[128,1536]{1,0:T(8,128)S(1)} fusion(f32[1024,1536]{1,0:T(8,128)} %fusion.3, bf16[768,1536]{1,0:T(8,128)(2,1)} %bitcast.25, f32[128,8]{1,0:T(8,128)S(1)} %copy.120, s32[1024]{0:T(1024)S(1)} %get-tuple-element.23), kind=kOutput, calls=%fused_computation.4 | convolution fusion | flops 2421227520 | bytes 9445376 | tf_op jit(solution)/shard_map/dot_general | solution.py:329
  242.0 1.0 add.89
  (120 shorter events, 16.0 us)
Async XLA Ops:
  7.2 196.0 %copy-start = (bf16[1536,32]{0,1:T(8,128)(2,1)S(1)}, bf16[1536,32]{0,1:T(8,128)(2,1)}, u32[]{:S(2)}) copy-start(bf16[1536,32]{0,1:T(8,128)(2,1)} %param.26) | copy-start | bytes 294916
  7.2 3.1 %copy-start.8 = (s32[8]{0:T(128)S(1)}, s32[8]{0:T(128)}, u32[]{:S(2)}) copy-start(s32[8]{0:T(128)} %param.20) | copy-start | bytes 100
  7.2 3.4 %copy-start.10 = (s32[16]{0:T(128)S(1)}, s32[16]{0:T(128)}, u32[]{:S(2)}) copy-start(s32[16]{0:T(128)} %param.18) | copy-start | bytes 196
  7.2 4.1 %copy-start.5 = (bf16[16,1536]{1,0:T(8,128)(2,1)S(1)}, bf16[16,1536]{1,0:T(8,128)(2,1)}, u32[]{:S(2)}) copy-start(bf16[16,1536]{1,0:T(8,128)(2,1)} %param.15) | copy-start | bytes 147460
  7.2 12.2 %copy-start.2 = (bf16[192,2,512]{2,1,0:T(2,128)(2,1)S(1)}, bf16[192,2,512]{2,1,0:T(2,128)(2,1)}, u32[]{:S(2)}) copy-start(bf16[192,2,512]{2,1,0:T(2,128)(2,1)} %param.29) | copy-start | bytes 1179652
  7.2 73.9 %all-gather.4.cloned.1.call-start = ((), (), s32[]{:S(2)}) async-start(), calls=%async_computation.6 | async-start | bytes 5308416 | tf_op jit(solution)/shard_map/all_gather | solution.py:270
  8.0 12.5 %copy-start.6 = (s32[128,8]{0,1:T(8,128)S(1)}, s32[128,8]{0,1:T(8,128)}, u32[]{:S(2)}) copy-start(s32[128,8]{0,1:T(8,128)} %param.27) | copy-start | bytes 12292
  8.0 12.7 %copy-start.9 = (bf16[1536]{0:T(1024)(128)(2,1)S(1)}, bf16[1536]{0:T(1024)(128)(2,1)}, u32[]{:S(2)}) copy-start(bf16[1536]{0:T(1024)(128)(2,1)} %param.25) | copy-start | bytes 9220
  8.0 12.9 %slice-start = ((bf16[16,1536]{1,0:T(8,128)(2,1)}), bf16[8,1536]{1,0:T(8,128)(2,1)S(1)}, s32[]{:S(2)}) async-start(bf16[16,1536]{1,0:T(8,128)(2,1)} %param.15), calls=%async_computation.9 | async-start | bytes 49152 | tf_op jit(solution)/shard_map/slice | solution.py:220
  8.0 13.0 %copy-start.7 = (bf16[16,1024]{1,0:T(8,128)(2,1)S(1)}, bf16[16,1024]{1,0:T(8,128)(2,1)}, u32[]{:S(2)}) copy-start(bf16[16,1024]{1,0:T(8,128)(2,1)} %param.16) | copy-start | bytes 98308
  8.0 120.7 %all-gather.6.cloned.1.call-start = ((), (), s32[]{:S(2)}) async-start(), calls=%async_computation.7 | async-start | bytes 7077888 | tf_op jit(solution)/shard_map/all_gather | solution.py:271
  12.3 24.1 %all-to-all-start = ((f32[16,1,1537]{2,1,0:T(1,128)}), f32[16,1,1537]{2,1,0:T(1,128)S(1)}, u32[]{:S(2)}, u32[]{:S(2)}) async-start(f32[16,1,1537]{2,1,0:T(1,128)} %copy.100), calls=%async_computation | async-start | bytes 212992 | tf_op jit(solution)/shard_map/all_to_all | solution.py:135
  19.4 116.2 %all-gather.8.cloned.1.call-start = ((), (), s32[]{:S(2)}) async-start(), calls=%async_computation.8 | async-start | bytes 3538944 | tf_op jit(solution)/shard_map/all_gather | solution.py:272
  60.1 16.3 %all-to-all-start.1 = ((f32[16,1,8,3,66]{4,2,3,1,0:T(8,128)}), f32[16,1,8,3,66]{4,2,3,1,0:T(8,128)S(1)}, u32[]{:S(2)}, u32[]{:S(2)}) async-start(f32[16,1,8,3,66]{4,2,3,1,0:T(8,128)} %copy.105), calls=%async_computation.1 | async-start | bytes 393216 | tf_op jit(solution)/shard_map/all_to_all | solution.py:135
  77.1 4.0 %copy-start.1 = (bf16[128,1536]{1,0:T(8,128)(2,1)S(1)}, bf16[128,1536]{1,0:T(8,128)(2,1)}, u32[]{:S(2)}) copy-start(bf16[128,1536]{1,0:T(8,128)(2,1)} %param.23) | copy-start | bytes 1179652
  77.1 4.0 %copy-start.3 = (bf16[112,1536]{1,0:T(8,128)(2,1)S(1)}, bf16[112,1536]{1,0:T(8,128)(2,1)}, u32[]{:S(2)}) copy-start(bf16[112,1536]{1,0:T(8,128)(2,1)} %param.22) | copy-start | bytes 1032196
  81.1 3.3 %copy-start.4 = (bf16[16,1536]{1,0:T(8,128)(2,1)}, bf16[16,1536]{1,0:T(8,128)(2,1)S(1)}, u32[]{:S(2)}) copy-start(bf16[16,1536]{1,0:T(8,128)(2,1)S(1)} %fusion.22) | copy-start | bytes 147460
  86.7 37.4 %all-to-all-start.2 = ((bf16[16,48,1536]{2,1,0:T(8,128)(2,1)}), bf16[16,48,1536]{2,1,0:T(8,128)(2,1)}, u32[]{:S(2)}, u32[]{:S(2)}) async-start(bf16[16,48,1536]{2,1,0:T(8,128)(2,1)} %convolution_convert_fusion.3), calls=%async_computation.2 | async-start | bytes 4718592 | tf_op jit(solution)/shard_map/all_to_all | solution.py:308
  124.1 37.2 %all-to-all-start.4 = ((bf16[16,48,1536]{2,1,0:T(8,128)(2,1)}), bf16[16,48,1536]{2,1,0:T(8,128)(2,1)}, u32[]{:S(2)}, u32[]{:S(2)}) async-start(bf16[16,48,1536]{2,1,0:T(8,128)(2,1)} %convolution_convert_fusion.1), calls=%async_computation.4 | async-start | bytes 4718592 | tf_op jit(solution)/shard_map/all_to_all | solution.py:308
  161.2 37.0 %all-to-all-start.3 = ((bf16[16,48,1536]{2,1,0:T(8,128)(2,1)}), bf16[16,48,1536]{2,1,0:T(8,128)(2,1)}, u32[]{:S(2)}, u32[]{:S(2)}) async-start(bf16[16,48,1536]{2,1,0:T(8,128)(2,1)} %convolution_convert_fusion.2), calls=%async_computation.3 | async-start | bytes 4718592 | tf_op jit(solution)/shard_map/all_to_all | solution.py:317
  165.7 5.4 %copy-start.11 = (bf16[1536,2,512]{2,0,1:T(8,128)(2,1)S(1)}, bf16[1536,2,512]{2,0,1:T(8,128)(2,1)}, u32[]{:S(2)}) copy-start(bf16[1536,2,512]{2,0,1:T(8,128)(2,1)} %all-gather.8.cloned.1.call-done) | copy-start | bytes 9437188
  198.3 37.0 %all-to-all-start.5 = ((bf16[16,48,1536]{2,1,0:T(8,128)(2,1)}), bf16[16,48,1536]{2,1,0:T(8,128)(2,1)}, u32[]{:S(2)}, u32[]{:S(2)}) async-start(bf16[16,48,1536]{2,1,0:T(8,128)(2,1)} %convolution_convert_fusion), calls=%async_computation.5 | async-start | bytes 4718592 | tf_op jit(solution)/shard_map/all_to_all | solution.py:317
Sparse Core Ops, SparseCore 0:
  9.7 33.6 all-gather.3
  45.1 40.9 all-gather.5
  87.9 28.7 all-gather.7

commit v7 on v6

--- a/solution.py
+++ b/solution.py
@@ -75,6 +75,67 @@
     max_ref[0] = jnp.broadcast_to(top, max_ref.shape[1:])
     tot_ref[0] = jnp.broadcast_to(total, tot_ref.shape[1:])
     mix_ref[0] = mix
+
+
+def exchange_kernel(x_ref, y_ref, send_sems, recv_sems, own_sem):
+    n = x_ref.shape[0]
+    me = lax.axis_index("gy")
+    row = lax.axis_index("gx")
+    mesh_ids = pl.DeviceIdType.MESH
+    barrier = pltpu.get_barrier_semaphore()
+    for k in range(1, n):
+        pl.semaphore_signal(
+            barrier, inc=1, device_id=(row, lax.rem(me + k, n)), device_id_type=mesh_ids
+        )
+    pl.semaphore_wait(barrier, n - 1)
+    own = pltpu.make_async_copy(x_ref.at[me], y_ref.at[me], own_sem)
+    own.start()
+    copies = []
+    for k in range(1, n):
+        dest = lax.rem(me + k, n)
+        copy = pltpu.make_async_remote_copy(
+            src_ref=x_ref.at[dest],
+            dst_ref=y_ref.at[me],
+            send_sem=send_sems.at[k],
+            recv_sem=recv_sems.at[k],
+            device_id=(row, dest),
+            device_id_type=mesh_ids,
+        )
+        copy.start()
+        copies.append(copy)
+    for k in range(1, n):
+        source = lax.rem(me + n - k, n)
+        pltpu.make_async_remote_copy(
+            src_ref=x_ref.at[source],
+            dst_ref=y_ref.at[source],
+            send_sem=send_sems.at[k],
+            recv_sem=recv_sems.at[k],
+            device_id=(row, source),
+            device_id_type=mesh_ids,
+        ).wait_recv()
+    for copy in copies:
+        copy.wait_send()
+    own.wait()
+
+
+def exchange(x, tag):
+    n = x.shape[0]
+    block = x.size // n * x.dtype.itemsize
+    return pl.pallas_call(
+        exchange_kernel,
+        out_shape=jax.ShapeDtypeStruct(x.shape, x.dtype),
+        in_specs=[pl.BlockSpec(memory_space=pl.ANY)],
+        out_specs=pl.BlockSpec(memory_space=pl.ANY),
+        scratch_shapes=[
+            pltpu.SemaphoreType.DMA((n,)),
+            pltpu.SemaphoreType.DMA((n,)),
+            pltpu.SemaphoreType.DMA,
+        ],
+        compiler_params=pltpu.CompilerParams(collective_id=tag, has_side_effects=True),
+        cost_estimate=pl.CostEstimate(
+            flops=0, transcendentals=0, bytes_accessed=2 * n * block
+        ),
+    )(x)
 
 
 def paged_attend(query_rows, tables, lengths, pool):
@@ -128,14 +189,10 @@
     )
 
 
-def in_one_piece(arrays, axis, split_dim, concat_dim, along):
+def in_one_piece(arrays, tag, along):
     columns = [a.reshape(*a.shape[:along], -1) for a in arrays]
     both = jnp.concatenate(columns, axis=along)
-    result, at, gathered = (
-        lax.all_to_all(both, axis, split_axis=split_dim, concat_axis=concat_dim, tiled=True),
-        0,
-        [],
-    )
+    result, at, gathered = (exchange(both, tag), 0, [])
     for a, column in zip(arrays, columns):
         share = result[..., at : at + column.shape[along]]
         gathered.append(share.reshape(*share.shape[:along], *a.shape[along:]))
@@ -231,9 +288,7 @@
     )
     got_queries, got_lengths = in_one_piece(
         (sent_queries.reshape(columns, slot_count, D), sent_lengths.reshape(columns, slot_count)),
-        "gy",
-        0,
-        0,
+        3,
         2,
     )
     far_max, far_totals, far_mix = paged_attend(
@@ -248,9 +303,7 @@
             far_totals.reshape(columns, slot_count, KV_HEADS, group_size),
             far_mix.reshape(columns, slot_count, KV_HEADS, group_size, HEAD),
         ),
-        "gy",
-        0,
-        0,
+        4,
         4,
     )
     cache_max = jnp.concatenate(

time: 253 us -> 252 us (level)
  Pallas kernels: 24.2 us -> 43.9 us
  starting transfers between devices: 33 us -> 19.6 us
  waiting for transfers between devices: 110 us -> 98.9 us
    pallas_call x0 -> x2, Pallas kernels: none -> 19.1 us  [exchange(): pl.pallas_call(exchange_kernel, out_shape=jax.ShapeDtypeStruct(x.shape, x...]
    all_to_all x2 -> x0, starting transfers between devices: 15 us -> none  [in_one_piece(): lax.all_to_all(both, axis, split_axis=split_dim, concat_axis=concat_dim,...]
    all_to_all x2 -> x0, waiting for transfers between devices: 8.33 us -> none  [in_one_piece(): lax.all_to_all(both, axis, split_axis=split_dim, concat_axis=concat_dim,...]
    all_to_all x2, waiting for transfers between devices: 51.2 us -> 47.7 us  [body(): lax.all_to_all(outgoing, 'gy', split_axis=0, concat_axis=0, tiled=True)]
  transfers between devices with their start and end apart: 9 -> 7, of which waited for: 5 -> 4; matrix products, arithmetic and copies ran while one was open for 24% -> 26% of each run, Pallas kernels for 10% -> 18%
where the time goes in v7:
time: 252 us; the launch traced here: 248 us
  waiting for transfers between devices  98.9 us (39%)
  Pallas kernels  43.9 us (17%)
  matrix products  41.7 us (17%)
  local copies, waits for them, and re-layouts  21.5 us (9%)
  starting transfers between devices  19.6 us (8%)
  between operations  14.3 us (6%)
  other arithmetic  8.45 us (3%)
    all_to_all x2, waiting for transfers between devices, body(): lax.all_to_all(expert_rows, 'gy', split_axis=0, concat_axis=0, tiled=True)  50.4 us
    all_to_all x2, waiting for transfers between devices, body(): lax.all_to_all(outgoing, 'gy', split_axis=0, concat_axis=0, tiled=True)  47.7 us
    pallas_call x2, Pallas kernels, paged_attend(): pl.pallas_call(attend_kernel, grid_spec=grid_spec, out_shape=[jax.ShapeDt...  24.9 us
    pallas_call x2, Pallas kernels, exchange(): pl.pallas_call(exchange_kernel, out_shape=jax.ShapeDtypeStruct(x.shape, x...  19.1 us
    dot_general x2, matrix products, body(): jnp.dot(one_hot, part.reshape(columns * CAP, D), preferred_element_type=j...  13.1 us
    dot_general x2, matrix products, body(): jnp.einsum('scd,df->scf', arrived, full_pair[:, local], preferred_element...  12.2 us
    all_to_all x2, starting transfers between devices, body(): lax.all_to_all(outgoing, 'gy', split_axis=0, concat_axis=0, tiled=True)  10.6 us
    all_to_all x2, starting transfers between devices, body(): lax.all_to_all(expert_rows, 'gy', split_axis=0, concat_axis=0, tiled=True)  8.89 us
  transfers between devices with their start and end apart: 7, of which 4 were waited for; matrix products, arithmetic and copies ran while one was open for 26% of the time, Pallas kernels for 18%

profile of v7, /device:TPU:96, one launch (start us, length us, event | category | flops | bytes accessed | tf_op | source)
XLA Modules:
  0.0 248.4 jit_solution(9072380447064327862)
XLA Ops:
  8.0 2.2 copy.115
  13.2 10.1 %shard_map.159 = f32[16,1,1537]{2,1,0:T(1,128)} custom-call(f32[16,1,1537]{2,1,0:T(1,128)} %pad_maximum_fusion.1.x_ref), custom_call_target="tpu_custom_call" | custom-call | bytes 196736 | tf_op jit(solution)/shard_map/pallas_call | solution.py:124
  23.2 1.6 convert_reduce_fusion.lengths
  24.8 1.1 fusion.19
  27.9 15.0 %shard_map.160 = (f32[16,24,128]{2,1,0:T(8,128)}, f32[16,24,128]{2,1,0:T(8,128)}, f32[16,24,512]{2,1,0:T(8,128)}) custom-call(s32[16,32]{1,0:T(8,128)} %tables.3, s32[16]{0:T(128)} %convert_reduce_fusion.lengths, bf16[16,24,512]{2,1,0:T(8,128)(2,1)} %broadcast_select_fusion.q_ref, bf16[128,16,1024]{2,1,0:T(8,128)(2,1)} %pool_ref.3), custom_call_target="tpu_custom_call" | custom-call | flops 402653184 | bytes 16777216 | tf_op jit(solution)/shard_map/pallas_call | solution.py:168
  43.0 1.1 copy.94
  44.1 1.1 copy.95
  45.9 1.5 reshape.217
  48.1 1.0 pad_maximum_fusion.x_ref
  49.2 9.0 %shard_map.161 = f32[16,1,8,3,66]{4,3,2,1,0:T(4,128)} custom-call(f32[16,1,8,3,66]{4,3,2,1,0:T(4,128)} %pad_maximum_fusion.x_ref), custom_call_target="tpu_custom_call" | custom-call | bytes 202752 | tf_op jit(solution)/shard_map/pallas_call | solution.py:124
  58.2 1.2 slice_bitcast_fusion.12
  59.3 1.2 fusion.41
  62.6 9.9 %shard_map.158 = (f32[8,24,128]{2,1,0:T(8,128)}, f32[8,24,128]{2,1,0:T(8,128)}, f32[8,24,512]{2,1,0:T(8,128)}) custom-call(s32[8,32]{1,0:T(8,128)} %tables.2, s32[8]{0:T(128)} %get-tuple-element.30.lengths, bf16[8,24,512]{2,1,0:T(8,128)(2,1)} %broadcast_select_fusion.1.q_ref, bf16[128,16,1024]{2,1,0:T(8,128)(2,1)} %pool_ref.3), custom_call_target="tpu_custom_call" | custom-call | flops 201326592 | bytes 8388608 | tf_op jit(solution)/shard_map/pallas_call | solution.py:168
  72.5 1.0 slice_reduce_fusion.1
  74.9 1.2 reshape.221
  81.3 3.2 %multiply_reduce_fusion = (f32[128]{0:T(128)S(1)}, f32[128,1536]{1,0:T(8,128)S(1)}) fusion(bf16[1536,1536]{1,0:T(8,128)(2,1)} %all-gather.4.cloned.1.call-done, bf16[112,1536]{1,0:T(8,128)(2,1)S(1)} %copy-done.3, bf16[16,1536]{1,0:T(8,128)(2,1)S(1)} %fusion.22, bf16[128,1536]{1,0:T(8,128)(2,1)S(1)} %copy-done.1), kind=kOutput, calls=%fused_computation.31 | convolution fusion | flops 605552512 | bytes 6291968 | tf_op jit(solution)/shard_map/dot_general | solution.py:326
  84.7 2.2 convolution_convert_fusion.3
  86.9 6.1 %all-to-all-start = ((bf16[16,48,1536]{2,1,0:T(8,128)(2,1)}), bf16[16,48,1536]{2,1,0:T(8,128)(2,1)}, u32[]{:S(2)}, u32[]{:S(2)}) async-start(bf16[16,48,1536]{2,1,0:T(8,128)(2,1)} %convolution_convert_fusion.3), calls=%async_computation | async-start | bytes 4718592 | tf_op jit(solution)/shard_map/all_to_all | solution.py:361
  93.0 2.2 convolution_convert_fusion.1
  95.2 28.0 %all-to-all-done = bf16[16,48,1536]{2,1,0:T(8,128)(2,1)} async-done(((bf16[16,48,1536]{2,1,0:T(8,128)(2,1)}), bf16[16,48,1536]{2,1,0:T(8,128)(2,1)}, u32[]{:S(2)}, u32[]{:S(2)}) %all-to-all-start) | async-done | bytes 2359328 | tf_op jit(solution)/shard_map/all_to_all | solution.py:361
  123.2 4.5 %all-to-all-start.2 = ((bf16[16,48,1536]{2,1,0:T(8,128)(2,1)}), bf16[16,48,1536]{2,1,0:T(8,128)(2,1)}, u32[]{:S(2)}, u32[]{:S(2)}) async-start(bf16[16,48,1536]{2,1,0:T(8,128)(2,1)} %convolution_convert_fusion.1), calls=%async_computation.2 | async-start | bytes 4718592 | tf_op jit(solution)/shard_map/all_to_all | solution.py:361
  127.7 6.8 %fusion.2 = f32[16,48,1024]{2,1,0:T(8,128)} fusion(bf16[16,48,1536]{2,1,0:T(8,128)(2,1)} %all-to-all-done, bf16[1536,2,1024]{2,0,1:T(8,128)(2,1)} %all-gather.6.cloned.1.call-done), kind=kOutput, calls=%fused_computation.12 | convolution fusion | flops 2415919104 | bytes 8650752 | tf_op jit(solution)/shard_map/scd,df->scf/dot_general | solution.py:362
  134.6 5.2 %convolution_convert_fusion.2 = bf16[16,48,1536]{2,1,0:T(8,128)(2,1)} fusion(bf16[1536,2,512]{2,0,1:T(8,128)(2,1)} %all-gather.8.cloned.1.call-done, f32[16,48,1024]{2,1,0:T(8,128)} %fusion.2), kind=kOutput, calls=%fused_computation.7 | convolution fusion | flops 1211498496 | bytes 7077888 | tf_op jit(solution)/shard_map/scf,df->scd/dot_general | solution.py:366
  139.7 19.6 %all-to-all-done.2 = bf16[16,48,1536]{2,1,0:T(8,128)(2,1)} async-done(((bf16[16,48,1536]{2,1,0:T(8,128)(2,1)}), bf16[16,48,1536]{2,1,0:T(8,128)(2,1)}, u32[]{:S(2)}, u32[]{:S(2)}) %all-to-all-start.2) | async-done | bytes 2359328 | tf_op jit(solution)/shard_map/all_to_all | solution.py:361
  159.4 4.5 %all-to-all-start.1 = ((bf16[16,48,1536]{2,1,0:T(8,128)(2,1)}), bf16[16,48,1536]{2,1,0:T(8,128)(2,1)}, u32[]{:S(2)}, u32[]{:S(2)}) async-start(bf16[16,48,1536]{2,1,0:T(8,128)(2,1)} %convolution_convert_fusion.2), calls=%async_computation.1 | async-start | bytes 4718592 | tf_op jit(solution)/shard_map/all_to_all | solution.py:370
  163.9 5.3 %fusion.1 = f32[16,48,1024]{2,1,0:T(8,128)S(1)} fusion(bf16[16,48,1536]{2,1,0:T(8,128)(2,1)} %all-to-all-done.2, bf16[1536,2,1024]{2,0,1:T(8,128)(2,1)} %all-gather.6.cloned.1.call-done), kind=kOutput, calls=%fused_computation.10 | convolution fusion | flops 2415919104 | bytes 8650752 | tf_op jit(solution)/shard_map/scd,df->scf/dot_general | solution.py:362
  169.2 2.9 %convolution_convert_fusion = bf16[16,48,1536]{2,1,0:T(8,128)(2,1)} fusion(bf16[1536,2,512]{2,0,1:T(8,128)(2,1)S(1)} %copy-done.11, f32[16,48,1024]{2,1,0:T(8,128)S(1)} %fusion.1), kind=kOutput, calls=%fused_computation.5 | convolution fusion | flops 1211498496 | bytes 7077888 | tf_op jit(solution)/shard_map/scf,df->scd/dot_general | solution.py:366
  172.1 24.8 %all-to-all-done.1 = bf16[16,48,1536]{2,1,0:T(8,128)(2,1)} async-done(((bf16[16,48,1536]{2,1,0:T(8,128)(2,1)}), bf16[16,48,1536]{2,1,0:T(8,128)(2,1)}, u32[]{:S(2)}, u32[]{:S(2)}) %all-to-all-start.1) | async-done | bytes 2359328 | tf_op jit(solution)/shard_map/all_to_all | solution.py:370
  196.8 4.4 %all-to-all-start.3 = ((bf16[16,48,1536]{2,1,0:T(8,128)(2,1)}), bf16[16,48,1536]{2,1,0:T(8,128)(2,1)}, u32[]{:S(2)}, u32[]{:S(2)}) async-start(bf16[16,48,1536]{2,1,0:T(8,128)(2,1)} %convolution_convert_fusion), calls=%async_computation.3 | async-start | bytes 4718592 | tf_op jit(solution)/shard_map/all_to_all | solution.py:370
  202.2 6.3 %fusion.3 = f32[1024,1536]{1,0:T(8,128)} fusion(bf16[768,1536]{1,0:T(8,128)(2,1)} %bitcast.17, s32[1024]{0:T(1024)S(1)} %get-tuple-element.24), kind=kOutput, calls=%fused_computation.15 | convolution fusion | flops 2416705536 | bytes 8654848 | tf_op jit(solution)/shard_map/dot_general | solution.py:382
  208.5 25.7 %all-to-all-done.3 = bf16[16,48,1536]{2,1,0:T(8,128)(2,1)} async-done(((bf16[16,48,1536]{2,1,0:T(8,128)(2,1)}), bf16[16,48,1536]{2,1,0:T(8,128)(2,1)}, u32[]{:S(2)}, u32[]{:S(2)}) %all-to-all-start.3) | async-done | bytes 2359328 | tf_op jit(solution)/shard_map/all_to_all | solution.py:370
  234.1 6.7 %fusion = f32[128,1536]{1,0:T(8,128)S(1)} fusion(f32[1024,1536]{1,0:T(8,128)} %fusion.3, bf16[768,1536]{1,0:T(8,128)(2,1)} %bitcast.23, f32[128,8]{1,0:T(8,128)S(1)} %copy.110, s32[1024]{0:T(1024)S(1)} %get-tuple-element.23), kind=kOutput, calls=%fused_computation.4 | convolution fusion | flops 2421227520 | bytes 9445376 | tf_op jit(solution)/shard_map/dot_general | solution.py:382
  (116 shorter events, 17.4 us)
Async XLA Ops:
  7.2 194.6 %copy-start = (bf16[1536,32]{0,1:T(8,128)(2,1)S(1)}, bf16[1536,32]{0,1:T(8,128)(2,1)}, u32[]{:S(2)}) copy-start(bf16[1536,32]{0,1:T(8,128)(2,1)} %param.26) | copy-start | bytes 294916
  7.2 3.1 %copy-start.2 = (bf16[192,2,512]{2,1,0:T(2,128)(2,1)S(1)}, bf16[192,2,512]{2,1,0:T(2,128)(2,1)}, u32[]{:S(2)}) copy-start(bf16[192,2,512]{2,1,0:T(2,128)(2,1)} %param.29) | copy-start | bytes 1179652
  7.2 3.9 %copy-start.8 = (s32[8]{0:T(128)S(1)}, s32[8]{0:T(128)}, u32[]{:S(2)}) copy-start(s32[8]{0:T(128)} %param.20) | copy-start | bytes 100
  7.2 4.7 %copy-start.5 = (bf16[16,1536]{1,0:T(8,128)(2,1)S(1)}, bf16[16,1536]{1,0:T(8,128)(2,1)}, u32[]{:S(2)}) copy-start(bf16[16,1536]{1,0:T(8,128)(2,1)} %param.15) | copy-start | bytes 147460
  7.2 4.2 %copy-start.10 = (s32[16]{0:T(128)S(1)}, s32[16]{0:T(128)}, u32[]{:S(2)}) copy-start(s32[16]{0:T(128)} %param.18) | copy-start | bytes 196
  7.2 74.1 %all-gather.4.cloned.1.call-start = ((), (), s32[]{:S(2)}) async-start(), calls=%async_computation.4 | async-start | bytes 5308416 | tf_op jit(solution)/shard_map/all_gather | solution.py:323
  8.0 119.8 %all-gather.6.cloned.1.call-start = ((), (), s32[]{:S(2)}) async-start(), calls=%async_computation.5 | async-start | bytes 7077888 | tf_op jit(solution)/shard_map/all_gather | solution.py:324
  10.2 124.3 %all-gather.8.cloned.1.call-start = ((), (), s32[]{:S(2)}) async-start(), calls=%async_computation.6 | async-start | bytes 3538944 | tf_op jit(solution)/shard_map/all_gather | solution.py:325
  47.5 13.1 %copy-start.6 = (s32[128,8]{0,1:T(8,128)S(1)}, s32[128,8]{0,1:T(8,128)}, u32[]{:S(2)}) copy-start(s32[128,8]{0,1:T(8,128)} %param.27) | copy-start | bytes 12292
  47.5 13.3 %copy-start.9 = (bf16[1536]{0:T(1024)(128)(2,1)S(1)}, bf16[1536]{0:T(1024)(128)(2,1)}, u32[]{:S(2)}) copy-start(bf16[1536]{0:T(1024)(128)(2,1)} %param.25) | copy-start | bytes 9220
  47.5 13.4 %slice-start = ((bf16[16,1536]{1,0:T(8,128)(2,1)}), bf16[8,1536]{1,0:T(8,128)(2,1)S(1)}, s32[]{:S(2)}) async-start(bf16[16,1536]{1,0:T(8,128)(2,1)} %param.15), calls=%async_computation.7 | async-start | bytes 49152 | tf_op jit(solution)/shard_map/slice | solution.py:277
  47.5 13.5 %copy-start.7 = (bf16[16,1024]{1,0:T(8,128)(2,1)S(1)}, bf16[16,1024]{1,0:T(8,128)(2,1)}, u32[]{:S(2)}) copy-start(bf16[16,1024]{1,0:T(8,128)(2,1)} %param.16) | copy-start | bytes 98308
  76.5 4.8 %copy-start.1 = (bf16[128,1536]{1,0:T(8,128)(2,1)S(1)}, bf16[128,1536]{1,0:T(8,128)(2,1)}, u32[]{:S(2)}) copy-start(bf16[128,1536]{1,0:T(8,128)(2,1)} %param.23) | copy-start | bytes 1179652
  76.5 4.8 %copy-start.3 = (bf16[112,1536]{1,0:T(8,128)(2,1)S(1)}, bf16[112,1536]{1,0:T(8,128)(2,1)}, u32[]{:S(2)}) copy-start(bf16[112,1536]{1,0:T(8,128)(2,1)} %param.22) | copy-start | bytes 1032196
  81.1 3.4 %copy-start.4 = (bf16[16,1536]{1,0:T(8,128)(2,1)}, bf16[16,1536]{1,0:T(8,128)(2,1)S(1)}, u32[]{:S(2)}) copy-start(bf16[16,1536]{1,0:T(8,128)(2,1)S(1)} %fusion.22) | copy-start | bytes 147460
  86.9 36.3 %all-to-all-start = ((bf16[16,48,1536]{2,1,0:T(8,128)(2,1)}), bf16[16,48,1536]{2,1,0:T(8,128)(2,1)}, u32[]{:S(2)}, u32[]{:S(2)}) async-start(bf16[16,48,1536]{2,1,0:T(8,128)(2,1)} %convolution_convert_fusion.3), calls=%async_computation | async-start | bytes 4718592 | tf_op jit(solution)/shard_map/all_to_all | solution.py:361
  123.2 36.1 %all-to-all-start.2 = ((bf16[16,48,1536]{2,1,0:T(8,128)(2,1)}), bf16[16,48,1536]{2,1,0:T(8,128)(2,1)}, u32[]{:S(2)}, u32[]{:S(2)}) async-start(bf16[16,48,1536]{2,1,0:T(8,128)(2,1)} %convolution_convert_fusion.1), calls=%async_computation.2 | async-start | bytes 4718592 | tf_op jit(solution)/shard_map/all_to_all | solution.py:361
  159.4 37.5 %all-to-all-start.1 = ((bf16[16,48,1536]{2,1,0:T(8,128)(2,1)}), bf16[16,48,1536]{2,1,0:T(8,128)(2,1)}, u32[]{:S(2)}, u32[]{:S(2)}) async-start(bf16[16,48,1536]{2,1,0:T(8,128)(2,1)} %convolution_convert_fusion.2), calls=%async_computation.1 | async-start | bytes 4718592 | tf_op jit(solution)/shard_map/all_to_all | solution.py:370
  163.8 5.4 %copy-start.11 = (bf16[1536,2,512]{2,0,1:T(8,128)(2,1)S(1)}, bf16[1536,2,512]{2,0,1:T(8,128)(2,1)}, u32[]{:S(2)}) copy-start(bf16[1536,2,512]{2,0,1:T(8,128)(2,1)} %all-gather.8.cloned.1.call-done) | copy-start | bytes 9437188
  196.8 37.3 %all-to-all-start.3 = ((bf16[16,48,1536]{2,1,0:T(8,128)(2,1)}), bf16[16,48,1536]{2,1,0:T(8,128)(2,1)}, u32[]{:S(2)}, u32[]{:S(2)}) async-start(bf16[16,48,1536]{2,1,0:T(8,128)(2,1)} %convolution_convert_fusion), calls=%async_computation.3 | async-start | bytes 4718592 | tf_op jit(solution)/shard_map/all_to_all | solution.py:370
Sparse Core Ops, SparseCore 0:
  9.7 33.6 all-gather.3
  45.1 40.9 all-gather.5
  87.8 28.6 all-gather.7

commit v8 on v6

--- a/solution.py
+++ b/solution.py
@@ -316,22 +316,25 @@
         returned_parts.append(
             lax.all_to_all(expert_rows, "gy", split_axis=0, concat_axis=0, tiled=True)
         )
-    flat_place = place_of.reshape(row_count * TOP)
-    flat_expert = routes.reshape(row_count * TOP)
-    picked = None
+    mixed = None
     for local, part in enumerate(returned_parts):
-        spot = jnp.where(
-            flat_expert % experts_dev == local, flat_expert // experts_dev * CAP + flat_place, -1
-        )
-        one_hot = (spot[:, None] == jnp.arange(columns * CAP, dtype=jnp.int32)[None, :]).astype(
-            jnp.bfloat16
+        spot = jnp.where(routes % experts_dev == local, routes // experts_dev * CAP + place_of, -1)
+        gate_spot = jnp.sum(
+            jnp.where(
+                spot[:, :, None] == jnp.arange(columns * CAP, dtype=jnp.int32)[None, None, :],
+                gate_weights[:, :, None],
+                0.0,
+            ),
+            axis=1,
         )
         share = jnp.dot(
-            one_hot, part.reshape(columns * CAP, D), preferred_element_type=jnp.float32
-        )
-        picked = share if picked is None else picked + share
-    picked = picked.reshape(row_count, TOP, D)
-    layer_out = stream + jnp.sum(gate_weights[:, :, None] * picked, axis=1)
+            gate_spot,
+            part.reshape(columns * CAP, D),
+            precision=lax.Precision.HIGHEST,
+            preferred_element_type=jnp.float32,
+        )
+        mixed = share if mixed is None else mixed + share
+    layer_out = stream + mixed
     return (attended, layer_out)
 
 

time: 253 us -> 251 us (level)
  matrix products: 41.7 us -> 36.7 us
  waiting for transfers between devices: 110 us -> 114 us
  starting transfers between devices: 33 us -> 29.9 us
    dot_general x2, matrix products: 13.1 us -> 6.9 us  [body(): jnp.dot(gate_spot, part.reshape(columns * CAP, D), precision=lax.Precisio...]
    reduce_sum x0 -> x1, other arithmetic: none -> 3.16 us  [body(): jnp.sum(jnp.where(spot[:, :, None] == jnp.arange(columns * CAP, dtype=jnp...]
    unnamed x29 -> x38, local copies, waits for them, and re-layouts: 3.6 us -> 6.45 us
where the time goes in v8:
time: 251 us; the launch traced here: 249 us
  waiting for transfers between devices  114 us (45%)
  matrix products  36.7 us (15%)
  starting transfers between devices  29.9 us (12%)
  Pallas kernels  24.8 us (10%)
  local copies, waits for them, and re-layouts  20.8 us (8%)
  between operations  14.3 us (6%)
  other arithmetic  8.54 us (3%)
    all_to_all x2, waiting for transfers between devices, body(): lax.all_to_all(outgoing, 'gy', split_axis=0, concat_axis=0, tiled=True)  53.3 us
    all_to_all x2, waiting for transfers between devices, body(): lax.all_to_all(expert_rows, 'gy', split_axis=0, concat_axis=0, tiled=True)  51.2 us
    pallas_call x2, Pallas kernels, paged_attend(): pl.pallas_call(attend_kernel, grid_spec=grid_spec, out_shape=[jax.ShapeDt...  24.8 us
    all_to_all x2, starting transfers between devices, in_one_piece(): lax.all_to_all(both, axis, split_axis=split_dim, concat_axis=concat_dim,...  14 us
    dot_general x2, matrix products, body(): jnp.einsum('scd,df->scf', arrived, full_pair[:, local], preferred_element...  12.2 us
    all_to_all x2, starting transfers between devices, body(): lax.all_to_all(outgoing, 'gy', split_axis=0, concat_axis=0, tiled=True)  8.36 us
    all_to_all x2, waiting for transfers between devices, in_one_piece(): lax.all_to_all(both, axis, split_axis=split_dim, concat_axis=concat_dim,...  8.33 us
    dot_general x2, matrix products, body(): jnp.einsum('scf,df->scd', hidden, full_down[:, local], preferred_element_...  8.03 us
  transfers between devices with their start and end apart: 9, of which 5 were waited for; matrix products, arithmetic and copies ran while one was open for 24% of the time, Pallas kernels for 10%

profile of v8, /device:TPU:96, one launch (start us, length us, event | category | flops | bytes accessed | tf_op | source)
XLA Modules:
  0.0 248.7 jit_solution(11731394020357332356)
XLA Ops:
  8.0 2.2 copy.129
  12.3 7.0 %all-to-all-start = ((f32[16,1,1537]{2,1,0:T(1,128)}), f32[16,1,1537]{2,1,0:T(1,128)S(1)}, u32[]{:S(2)}, u32[]{:S(2)}) async-start(f32[16,1,1537]{2,1,0:T(1,128)} %copy.105), calls=%async_computation | async-start | bytes 212992 | tf_op jit(solution)/shard_map/all_to_all | solution.py:135
  21.7 10.0 %shard_map.158 = (f32[8,24,128]{2,1,0:T(8,128)}, f32[8,24,128]{2,1,0:T(8,128)}, f32[8,24,512]{2,1,0:T(8,128)}) custom-call(s32[8,32]{1,0:T(8,128)} %tables.2, s32[8]{0:T(128)} %get-tuple-element.32.lengths, bf16[8,24,512]{2,1,0:T(8,128)(2,1)} %broadcast_select_fusion.1.q_ref, bf16[128,16,1024]{2,1,0:T(8,128)(2,1)} %pool_ref.3), custom_call_target="tpu_custom_call" | custom-call | flops 201326592 | bytes 8388608 | tf_op jit(solution)/shard_map/pallas_call | solution.py:107
  31.8 1.0 slice_reduce_fusion.1
  33.0 1.0 slice_reduce_fusion
  34.9 1.2 reshape.138
  38.8 0.9 fusion.24.lengths
  39.7 14.8 %shard_map.159 = (f32[16,24,128]{2,1,0:T(8,128)}, f32[16,24,128]{2,1,0:T(8,128)}, f32[16,24,512]{2,1,0:T(8,128)}) custom-call(s32[16,32]{1,0:T(8,128)} %tables.3, s32[16]{0:T(128)} %fusion.24.lengths, bf16[16,24,512]{2,1,0:T(8,128)(2,1)} %broadcast_select_fusion.q_ref, bf16[128,16,1024]{2,1,0:T(8,128)(2,1)} %pool_ref.3), custom_call_target="tpu_custom_call" | custom-call | flops 402653184 | bytes 16777216 | tf_op jit(solution)/shard_map/pallas_call | solution.py:107
  54.5 1.6 reshape.134
  58.9 6.9 %all-to-all-start.1 = ((f32[16,1,8,3,66]{4,2,3,1,0:T(8,128)}), f32[16,1,8,3,66]{4,2,3,1,0:T(8,128)S(1)}, u32[]{:S(2)}, u32[]{:S(2)}) async-start(f32[16,1,8,3,66]{4,2,3,1,0:T(8,128)} %copy.110), calls=%async_computation.1 | async-start | bytes 393216 | tf_op jit(solution)/shard_map/all_to_all | solution.py:135
  65.9 8.3 %all-to-all-done.1 = f32[16,1,8,3,66]{4,2,3,1,0:T(8,128)S(1)} async-done(((f32[16,1,8,3,66]{4,2,3,1,0:T(8,128)}), f32[16,1,8,3,66]{4,2,3,1,0:T(8,128)S(1)}, u32[]{:S(2)}, u32[]{:S(2)}) %all-to-all-start.1) | async-done | bytes 101408 | tf_op jit(solution)/shard_map/all_to_all | solution.py:135
  79.0 3.2 %multiply_reduce_fusion = (f32[128]{0:T(128)S(1)}, f32[128,1536]{1,0:T(8,128)S(1)}) fusion(bf16[1536,1536]{1,0:T(8,128)(2,1)} %all-gather.4.cloned.1.call-done, bf16[112,1536]{1,0:T(8,128)(2,1)S(1)} %copy-done.6, bf16[16,1536]{1,0:T(8,128)(2,1)S(1)} %fusion.19, bf16[128,1536]{1,0:T(8,128)(2,1)S(1)} %copy-done.4), kind=kOutput, calls=%fused_computation.31 | convolution fusion | flops 605552512 | bytes 6291968 | tf_op jit(solution)/shard_map/dot_general | solution.py:273
  82.3 2.2 convolution_convert_fusion.3
  84.5 4.5 %all-to-all-start.2 = ((bf16[16,48,1536]{2,1,0:T(8,128)(2,1)}), bf16[16,48,1536]{2,1,0:T(8,128)(2,1)}, u32[]{:S(2)}, u32[]{:S(2)}) async-start(bf16[16,48,1536]{2,1,0:T(8,128)(2,1)} %convolution_convert_fusion.3), calls=%async_computation.2 | async-start | bytes 4718592 | tf_op jit(solution)/shard_map/all_to_all | solution.py:308
  89.0 2.3 convolution_convert_fusion.1
  91.3 30.9 %all-to-all-done.2 = bf16[16,48,1536]{2,1,0:T(8,128)(2,1)} async-done(((bf16[16,48,1536]{2,1,0:T(8,128)(2,1)}), bf16[16,48,1536]{2,1,0:T(8,128)(2,1)}, u32[]{:S(2)}, u32[]{:S(2)}) %all-to-all-start.2) | async-done | bytes 2359328 | tf_op jit(solution)/shard_map/all_to_all | solution.py:308
  122.2 3.9 %all-to-all-start.4 = ((bf16[16,48,1536]{2,1,0:T(8,128)(2,1)}), bf16[16,48,1536]{2,1,0:T(8,128)(2,1)S(1)}, u32[]{:S(2)}, u32[]{:S(2)}) async-start(bf16[16,48,1536]{2,1,0:T(8,128)(2,1)} %convolution_convert_fusion.1), calls=%async_computation.4 | async-start | bytes 4718592 | tf_op jit(solution)/shard_map/all_to_all | solution.py:308
  126.2 6.9 %fusion.1 = f32[16,48,1024]{2,1,0:T(8,128)} fusion(bf16[16,48,1536]{2,1,0:T(8,128)(2,1)} %all-to-all-done.2, bf16[1536,2,1024]{2,0,1:T(8,128)(2,1)} %all-gather.6.cloned.1.call-done), kind=kOutput, calls=%fused_computation.10 | convolution fusion | flops 2415919104 | bytes 8650752 | tf_op jit(solution)/shard_map/scd,df->scf/dot_general | solution.py:309
  133.0 5.2 %convolution_convert_fusion.2 = bf16[16,48,1536]{2,1,0:T(8,128)(2,1)} fusion(bf16[1536,2,512]{2,0,1:T(8,128)(2,1)} %all-gather.8.cloned.1.call-done, f32[16,48,1024]{2,1,0:T(8,128)} %fusion.1), kind=kOutput, calls=%fused_computation.5 | convolution fusion | flops 1211498496 | bytes 7077888 | tf_op jit(solution)/shard_map/scf,df->scd/dot_general | solution.py:313
  138.2 22.4 %all-to-all-done.4 = bf16[16,48,1536]{2,1,0:T(8,128)(2,1)S(1)} async-done(((bf16[16,48,1536]{2,1,0:T(8,128)(2,1)}), bf16[16,48,1536]{2,1,0:T(8,128)(2,1)S(1)}, u32[]{:S(2)}, u32[]{:S(2)}) %all-to-all-start.4) | async-done | bytes 2359328 | tf_op jit(solution)/shard_map/all_to_all | solution.py:308
  160.6 1.5 copy-done.3
  162.1 3.7 %all-to-all-start.3 = ((bf16[16,48,1536]{2,1,0:T(8,128)(2,1)}), bf16[16,48,1536]{2,1,0:T(8,128)(2,1)S(1)}, u32[]{:S(2)}, u32[]{:S(2)}) async-start(bf16[16,48,1536]{2,1,0:T(8,128)(2,1)} %convolution_convert_fusion.2), calls=%async_computation.3 | async-start | bytes 4718592 | tf_op jit(solution)/shard_map/all_to_all | solution.py:317
  165.8 5.3 %fusion = f32[16,48,1024]{2,1,0:T(8,128)S(1)} fusion(bf16[16,48,1536]{2,1,0:T(8,128)(2,1)} %copy-done.3, bf16[1536,2,1024]{2,0,1:T(8,128)(2,1)} %all-gather.6.cloned.1.call-done), kind=kOutput, calls=%fused_computation.8 | convolution fusion | flops 2415919104 | bytes 8650752 | tf_op jit(solution)/shard_map/scd,df->scf/dot_general | solution.py:309
  171.2 2.9 %convolution_convert_fusion = bf16[16,48,1536]{2,1,0:T(8,128)(2,1)} fusion(bf16[1536,2,512]{2,0,1:T(8,128)(2,1)S(1)} %copy-done.16, f32[16,48,1024]{2,1,0:T(8,128)S(1)} %fusion), kind=kOutput, calls=%fused_computation.3 | convolution fusion | flops 1211498496 | bytes 7077888 | tf_op jit(solution)/shard_map/scf,df->scd/dot_general | solution.py:313
  174.0 25.5 %all-to-all-done.3 = bf16[16,48,1536]{2,1,0:T(8,128)(2,1)S(1)} async-done(((bf16[16,48,1536]{2,1,0:T(8,128)(2,1)}), bf16[16,48,1536]{2,1,0:T(8,128)(2,1)S(1)}, u32[]{:S(2)}, u32[]{:S(2)}) %all-to-all-start.3) | async-done | bytes 2359328 | tf_op jit(solution)/shard_map/all_to_all | solution.py:317
  199.5 1.4 copy-done.1
  201.0 3.7 %all-to-all-start.5 = ((bf16[16,48,1536]{2,1,0:T(8,128)(2,1)}), bf16[16,48,1536]{2,1,0:T(8,128)(2,1)S(1)}, u32[]{:S(2)}, u32[]{:S(2)}) async-start(bf16[16,48,1536]{2,1,0:T(8,128)(2,1)} %convolution_convert_fusion), calls=%async_computation.5 | async-start | bytes 4718592 | tf_op jit(solution)/shard_map/all_to_all | solution.py:317
  205.0 1.2 fusion.41
  206.4 3.2 %select_reduce_fusion = (f32[128,768]{1,0:T(8,128)}, f32[128,768]{1,0:T(8,128)S(1)}) fusion(s32[128,8]{1,0:T(8,128)S(1)} %copy.131, f32[128,8]{1,0:T(8,128)S(1)} %copy.126, s32[128,8]{1,0:T(8,128)S(1)} %copy.125), kind=kLoop, calls=%fused_computation.11 | loop fusion | flops 4521984 | bytes 798720 | tf_op jit(solution)/shard_map/reduce_sum | solution.py:322
  209.6 3.6 %fusion.42 = f32[128,1536]{1,0:T(8,128)} fusion(f32[128,768]{1,0:T(8,128)S(1)} %get-tuple-element.15, bf16[768,1536]{1,0:T(8,128)(2,1)} %bitcast.73), kind=kOutput, calls=%fused_computation.105 | convolution fusion | flops 1811939328 | bytes 3538944 | tf_op jit(solution)/shard_map/dot_general | solution.py:330
  213.2 25.7 %all-to-all-done.5 = bf16[16,48,1536]{2,1,0:T(8,128)(2,1)S(1)} async-done(((bf16[16,48,1536]{2,1,0:T(8,128)(2,1)}), bf16[16,48,1536]{2,1,0:T(8,128)(2,1)S(1)}, u32[]{:S(2)}, u32[]{:S(2)}) %all-to-all-start.5) | async-done | bytes 2359328 | tf_op jit(solution)/shard_map/all_to_all | solution.py:317
  238.9 3.2 %fusion.2 = f32[128,1536]{1,0:T(8,128)} fusion(f32[128,1536]{1,0:T(8,128)S(1)} %get-tuple-element.30, f32[128,1536]{1,0:T(8,128)} %fusion.42, f32[128,768]{1,0:T(8,128)} %get-tuple-element.14, bf16[768,1536]{1,0:T(8,128)(2,1)S(1)} %bitcast.72), kind=kOutput, calls=%fused_computation.16 | convolution fusion | flops 1812332544 | bytes 5111808 | tf_op jit(solution)/shard_map/dot_general | solution.py:330
  (128 shorter events, 16.9 us)
Async XLA Ops:
  7.2 197.8 %copy-start = (bf16[1536,32]{0,1:T(8,128)(2,1)S(1)}, bf16[1536,32]{0,1:T(8,128)(2,1)}, u32[]{:S(2)}) copy-start(bf16[1536,32]{0,1:T(8,128)(2,1)} %param.26) | copy-start | bytes 294916
  7.2 3.1 %copy-start.13 = (s32[8]{0:T(128)S(1)}, s32[8]{0:T(128)}, u32[]{:S(2)}) copy-start(s32[8]{0:T(128)} %param.20) | copy-start | bytes 100
  7.2 3.4 %copy-start.15 = (s32[16]{0:T(128)S(1)}, s32[16]{0:T(128)}, u32[]{:S(2)}) copy-start(s32[16]{0:T(128)} %param.18) | copy-start | bytes 196
  7.2 4.0 %copy-start.10 = (bf16[16,1536]{1,0:T(8,128)(2,1)S(1)}, bf16[16,1536]{1,0:T(8,128)(2,1)}, u32[]{:S(2)}) copy-start(bf16[16,1536]{1,0:T(8,128)(2,1)} %param.15) | copy-start | bytes 147460
  7.2 12.2 %copy-start.5 = (bf16[192,2,512]{2,1,0:T(2,128)(2,1)S(1)}, bf16[192,2,512]{2,1,0:T(2,128)(2,1)}, u32[]{:S(2)}) copy-start(bf16[192,2,512]{2,1,0:T(2,128)(2,1)} %param.29) | copy-start | bytes 1179652
  7.2 71.7 %all-gather.4.cloned.1.call-start = ((), (), s32[]{:S(2)}) async-start(), calls=%async_computation.6 | async-start | bytes 5308416 | tf_op jit(solution)/shard_map/all_gather | solution.py:270
  8.0 12.6 %slice-start = ((bf16[16,1536]{1,0:T(8,128)(2,1)}), bf16[8,1536]{1,0:T(8,128)(2,1)S(1)}, s32[]{:S(2)}) async-start(bf16[16,1536]{1,0:T(8,128)(2,1)} %param.15), calls=%async_computation.9 | async-start | bytes 49152 | tf_op jit(solution)/shard_map/slice | solution.py:220
  8.0 118.2 %all-gather.6.cloned.1.call-start = ((), (), s32[]{:S(2)}) async-start(), calls=%async_computation.7 | async-start | bytes 7077888 | tf_op jit(solution)/shard_map/all_gather | solution.py:271
  12.3 24.6 %all-to-all-start = ((f32[16,1,1537]{2,1,0:T(1,128)}), f32[16,1,1537]{2,1,0:T(1,128)S(1)}, u32[]{:S(2)}, u32[]{:S(2)}) async-start(f32[16,1,1537]{2,1,0:T(1,128)} %copy.105), calls=%async_computation | async-start | bytes 212992 | tf_op jit(solution)/shard_map/all_to_all | solution.py:135
  19.3 113.7 %all-gather.8.cloned.1.call-start = ((), (), s32[]{:S(2)}) async-start(), calls=%async_computation.8 | async-start | bytes 3538944 | tf_op jit(solution)/shard_map/all_gather | solution.py:272
  21.7 12.5 %copy-start.12 = (bf16[16,1024]{1,0:T(8,128)(2,1)S(1)}, bf16[16,1024]{1,0:T(8,128)(2,1)}, u32[]{:S(2)}) copy-start(bf16[16,1024]{1,0:T(8,128)(2,1)} %param.16) | copy-start | bytes 98308
  21.7 14.3 %copy-start.11 = (s32[128,8]{0,1:T(8,128)S(1)}, s32[128,8]{0,1:T(8,128)}, u32[]{:S(2)}) copy-start(s32[128,8]{0,1:T(8,128)} %param.27) | copy-start | bytes 12292
  31.8 5.1 %copy-start.14 = (bf16[1536]{0:T(1024)(128)(2,1)S(1)}, bf16[1536]{0:T(1024)(128)(2,1)}, u32[]{:S(2)}) copy-start(bf16[1536]{0:T(1024)(128)(2,1)} %param.25) | copy-start | bytes 9220
  54.5 2.2 copy-start.9
  54.5 2.8 %copy-start.8 = (f32[16,24,128]{2,1,0:T(8,128)S(1)}, f32[16,24,128]{2,1,0:T(8,128)}, u32[]{:S(2)}) copy-start(f32[16,24,128]{2,1,0:T(8,128)} %get-tuple-element.10) | copy-start | bytes 589828
  58.9 15.3 %all-to-all-start.1 = ((f32[16,1,8,3,66]{4,2,3,1,0:T(8,128)}), f32[16,1,8,3,66]{4,2,3,1,0:T(8,128)S(1)}, u32[]{:S(2)}, u32[]{:S(2)}) async-start(f32[16,1,8,3,66]{4,2,3,1,0:T(8,128)} %copy.110), calls=%async_computation.1 | async-start | bytes 393216 | tf_op jit(solution)/shard_map/all_to_all | solution.py:135
  74.3 4.6 %copy-start.4 = (bf16[128,1536]{1,0:T(8,128)(2,1)S(1)}, bf16[128,1536]{1,0:T(8,128)(2,1)}, u32[]{:S(2)}) copy-start(bf16[128,1536]{1,0:T(8,128)(2,1)} %param.23) | copy-start | bytes 1179652
  74.3 4.6 %copy-start.6 = (bf16[112,1536]{1,0:T(8,128)(2,1)S(1)}, bf16[112,1536]{1,0:T(8,128)(2,1)}, u32[]{:S(2)}) copy-start(bf16[112,1536]{1,0:T(8,128)(2,1)} %param.22) | copy-start | bytes 1032196
  78.9 3.3 %copy-start.7 = (bf16[16,1536]{1,0:T(8,128)(2,1)}, bf16[16,1536]{1,0:T(8,128)(2,1)S(1)}, u32[]{:S(2)}) copy-start(bf16[16,1536]{1,0:T(8,128)(2,1)S(1)} %fusion.19) | copy-start | bytes 147460
  82.3 6.7 %copy-start.2 = (bf16[128,1536]{1,0:T(8,128)(2,1)}, bf16[128,1536]{1,0:T(8,128)(2,1)S(1)}, u32[]{:S(2)}) copy-start(bf16[128,1536]{1,0:T(8,128)(2,1)S(1)} %multiply_convert_fusion) | copy-start | bytes 1179652
  84.5 37.7 %all-to-all-start.2 = ((bf16[16,48,1536]{2,1,0:T(8,128)(2,1)}), bf16[16,48,1536]{2,1,0:T(8,128)(2,1)}, u32[]{:S(2)}, u32[]{:S(2)}) async-start(bf16[16,48,1536]{2,1,0:T(8,128)(2,1)} %convolution_convert_fusion.3), calls=%async_computation.2 | async-start | bytes 4718592 | tf_op jit(solution)/shard_map/all_to_all | solution.py:308
  122.2 38.4 %all-to-all-start.4 = ((bf16[16,48,1536]{2,1,0:T(8,128)(2,1)}), bf16[16,48,1536]{2,1,0:T(8,128)(2,1)S(1)}, u32[]{:S(2)}, u32[]{:S(2)}) async-start(bf16[16,48,1536]{2,1,0:T(8,128)(2,1)} %convolution_convert_fusion.1), calls=%async_computation.4 | async-start | bytes 4718592 | tf_op jit(solution)/shard_map/all_to_all | solution.py:308
  160.6 1.5 copy-start.3
  162.1 37.4 %all-to-all-start.3 = ((bf16[16,48,1536]{2,1,0:T(8,128)(2,1)}), bf16[16,48,1536]{2,1,0:T(8,128)(2,1)S(1)}, u32[]{:S(2)}, u32[]{:S(2)}) async-start(bf16[16,48,1536]{2,1,0:T(8,128)(2,1)} %convolution_convert_fusion.2), calls=%async_computation.3 | async-start | bytes 4718592 | tf_op jit(solution)/shard_map/all_to_all | solution.py:317
  165.8 5.4 %copy-start.16 = (bf16[1536,2,512]{2,0,1:T(8,128)(2,1)S(1)}, bf16[1536,2,512]{2,0,1:T(8,128)(2,1)}, u32[]{:S(2)}) copy-start(bf16[1536,2,512]{2,0,1:T(8,128)(2,1)} %all-gather.8.cloned.1.call-done) | copy-start | bytes 9437188
  199.5 1.4 copy-start.1
  201.0 37.9 %all-to-all-start.5 = ((bf16[16,48,1536]{2,1,0:T(8,128)(2,1)}), bf16[16,48,1536]{2,1,0:T(8,128)(2,1)S(1)}, u32[]{:S(2)}, u32[]{:S(2)}) async-start(bf16[16,48,1536]{2,1,0:T(8,128)(2,1)} %convolution_convert_fusion), calls=%async_computation.5 | async-start | bytes 4718592 | tf_op jit(solution)/shard_map/all_to_all | solution.py:317
Sparse Core Ops, SparseCore 0:
  9.7 33.6 all-gather.3
  45.2 40.9 all-gather.5
  87.9 28.7 all-gather.7

commit v9 on v8

--- a/solution.py
+++ b/solution.py
@@ -63,15 +63,18 @@
     keys = kv[:, :, :half].reshape(MAXLEN, half)
     values = kv[:, :, half:].reshape(MAXLEN, half)
     q = q_ref[0]
-    scores = lax.dot_general(
-        q, keys, (((1,), (1,)), ((), ())), preferred_element_type=jnp.float32
-    ) * (1.0 / math.sqrt(HEAD))
-    valid = lax.broadcasted_iota(jnp.int32, scores.shape, 1) < lengths[r]
+    scores = jnp.dot(keys, q, preferred_element_type=jnp.float32) * (1.0 / math.sqrt(HEAD))
+    valid = lax.broadcasted_iota(jnp.int32, scores.shape, 0) < lengths[r]
     masked = jnp.where(valid, scores, -1e30)
-    top = jnp.max(masked, axis=1, keepdims=True)
+    top = jnp.max(masked, axis=0, keepdims=True)
     expos = jnp.where(valid, jnp.exp(masked - top), 0.0)
-    total = jnp.sum(expos, axis=1, keepdims=True)
-    mix = jnp.dot(expos.astype(jnp.bfloat16), values, preferred_element_type=jnp.float32)
+    total = jnp.sum(expos, axis=0, keepdims=True)
+    mix = lax.dot_general(
+        expos.astype(jnp.bfloat16),
+        values,
+        (((0,), (0,)), ((), ())),
+        preferred_element_type=jnp.float32,
+    )
     max_ref[0] = jnp.broadcast_to(top, max_ref.shape[1:])
     tot_ref[0] = jnp.broadcast_to(total, tot_ref.shape[1:])
     mix_ref[0] = mix
@@ -85,18 +88,18 @@
     mask = (jnp.arange(KV_HEADS)[:, None] == jnp.arange(KV_HEADS)[None, :])
     spread = jnp.where(
         mask[None, :, None, :, None], heads, jnp.zeros((), query_rows.dtype)
-    ).reshape(count, HEADS, half)
+    ).transpose(0, 3, 4, 1, 2).reshape(count, half, HEADS)
     kv_width = pool.shape[2]
     grid_spec = pltpu.PrefetchScalarGridSpec(
         num_scalar_prefetch=2,
         grid=(count,),
         in_specs=[
-            pl.BlockSpec((1, HEADS, half), lambda r, t, l: (r, 0, 0)),
+            pl.BlockSpec((1, half, HEADS), lambda r, t, l: (r, 0, 0)),
             pl.BlockSpec(memory_space=pl.ANY),
         ],
         out_specs=[
-            pl.BlockSpec((1, HEADS, 128), lambda r, t, l: (r, 0, 0)),
-            pl.BlockSpec((1, HEADS, 128), lambda r, t, l: (r, 0, 0)),
+            pl.BlockSpec((1, 8, HEADS), lambda r, t, l: (r, 0, 0)),
+            pl.BlockSpec((1, 8, HEADS), lambda r, t, l: (r, 0, 0)),
             pl.BlockSpec((1, HEADS, half), lambda r, t, l: (r, 0, 0)),
         ],
         scratch_shapes=[
@@ -108,8 +111,8 @@
         attend_kernel,
         grid_spec=grid_spec,
         out_shape=[
-            jax.ShapeDtypeStruct((count, HEADS, 128), jnp.float32),
-            jax.ShapeDtypeStruct((count, HEADS, 128), jnp.float32),
+            jax.ShapeDtypeStruct((count, 8, HEADS), jnp.float32),
+            jax.ShapeDtypeStruct((count, 8, HEADS), jnp.float32),
             jax.ShapeDtypeStruct((count, HEADS, half), jnp.float32),
         ],
         compiler_params=pltpu.CompilerParams(dimension_semantics=("arbitrary",)),
@@ -122,8 +125,8 @@
     blocks = mix.reshape(count, KV_HEADS, group_size, KV_HEADS, HEAD)
     mixture = jnp.sum(jnp.where(mask[None, :, None, :, None], blocks, 0.0), axis=3)
     return (
-        top[:, :, 0].reshape(count, KV_HEADS, group_size),
-        total[:, :, 0].reshape(count, KV_HEADS, group_size),
+        top[:, 0, :].reshape(count, KV_HEADS, group_size),
+        total[:, 0, :].reshape(count, KV_HEADS, group_size),
         mixture,
     )
 

time: 251 us -> 257 us (1.024)
  Pallas kernels: 24.8 us -> 27.8 us
  waiting for transfers between devices: 114 us -> 111 us
  local copies, waits for them, and re-layouts: 20.8 us -> 23.4 us
    pallas_call x2, Pallas kernels: 24.8 us -> 27.8 us  [paged_attend(): pl.pallas_call(attend_kernel, grid_spec=grid_spec, out_shape=[jax.ShapeDt...]
    all_to_all x2, waiting for transfers between devices: 53.3 us -> 50.6 us  [body(): lax.all_to_all(outgoing, 'gy', split_axis=0, concat_axis=0, tiled=True)]
    unnamed x38 -> x34, local copies, waits for them, and re-layouts: 6.45 us -> 6.44 us
  transfers between devices with their start and end apart: 9 -> 9, of which waited for: 5 -> 5; matrix products, arithmetic and copies ran while one was open for 24% -> 25% of each run, Pallas kernels for 10% -> 11%
where the time goes in v9:
time: 257 us; the launch traced here: 254 us
  waiting for transfers between devices  111 us (43%)
  matrix products  36.7 us (14%)
  starting transfers between devices  31.4 us (12%)
  Pallas kernels  27.8 us (11%)
  local copies, waits for them, and re-layouts  23.4 us (9%)
  between operations  14.3 us (6%)
  other arithmetic  9.64 us (4%)
    all_to_all x2, waiting for transfers between devices, body(): lax.all_to_all(expert_rows, 'gy', split_axis=0, concat_axis=0, tiled=True)  51.5 us
    all_to_all x2, waiting for transfers between devices, body(): lax.all_to_all(outgoing, 'gy', split_axis=0, concat_axis=0, tiled=True)  50.6 us
    pallas_call x2, Pallas kernels, paged_attend(): pl.pallas_call(attend_kernel, grid_spec=grid_spec, out_shape=[jax.ShapeDt...  27.8 us
    all_to_all x2, starting transfers between devices, in_one_piece(): lax.all_to_all(both, axis, split_axis=split_dim, concat_axis=concat_dim,...  15.4 us
    dot_general x2, matrix products, body(): jnp.einsum('scd,df->scf', arrived, full_pair[:, local], preferred_element...  12.2 us
    all_to_all x2, starting transfers between devices, body(): lax.all_to_all(outgoing, 'gy', split_axis=0, concat_axis=0, tiled=True)  8.36 us
    all_to_all x2, waiting for transfers between devices, in_one_piece(): lax.all_to_all(both, axis, split_axis=split_dim, concat_axis=concat_dim,...  8.33 us
    dot_general x2, matrix products, body(): jnp.einsum('scf,df->scd', hidden, full_down[:, local], preferred_element_...  8.03 us
  transfers between devices with their start and end apart: 9, of which 5 were waited for; matrix products, arithmetic and copies ran while one was open for 25% of the time, Pallas kernels for 11%

profile of v9, /device:TPU:96, one launch (start us, length us, event | category | flops | bytes accessed | tf_op | source)
XLA Modules:
  0.0 254.3 jit_solution(2479173142029813631)
XLA Ops:
  8.0 2.2 copy.147
  12.3 7.0 %all-to-all-start = ((f32[16,1,1537]{2,1,0:T(1,128)}), f32[16,1,1537]{2,1,0:T(1,128)S(1)}, u32[]{:S(2)}, u32[]{:S(2)}) async-start(f32[16,1,1537]{2,1,0:T(1,128)} %copy.121), calls=%async_computation | async-start | bytes 212992 | tf_op jit(solution)/shard_map/all_to_all | solution.py:138
  21.7 1.1 broadcast_select_fusion.1.q_ref
  22.8 11.0 %shard_map.158 = (f32[8,8,24]{2,1,0:T(8,128)}, f32[8,8,24]{2,1,0:T(8,128)}, f32[8,24,512]{2,1,0:T(8,128)}) custom-call(s32[8,32]{1,0:T(8,128)} %tables.2, s32[8]{0:T(128)} %get-tuple-element.32.lengths, bf16[8,512,24]{2,1,0:T(8,128)(2,1)} %broadcast_select_fusion.1.q_ref, bf16[128,16,1024]{2,1,0:T(8,128)(2,1)} %pool_ref.3), custom_call_target="tpu_custom_call" | custom-call | flops 201326592 | bytes 8388608 | tf_op jit(solution)/shard_map/pallas_call | solution.py:110
  36.5 1.2 reshape.138
  39.6 1.0 copy.123
  40.7 1.5 broadcast_select_fusion.q_ref
  43.0 16.8 %shard_map.159 = (f32[16,8,24]{2,1,0:T(8,128)}, f32[16,8,24]{2,1,0:T(8,128)}, f32[16,24,512]{2,1,0:T(8,128)}) custom-call(s32[16,32]{1,0:T(8,128)} %tables.3, s32[16]{0:T(128)} %fusion.24.lengths, bf16[16,512,24]{2,1,0:T(8,128)(2,1)} %broadcast_select_fusion.q_ref, bf16[128,16,1024]{2,1,0:T(8,128)(2,1)} %pool_ref.3), custom_call_target="tpu_custom_call" | custom-call | flops 402653184 | bytes 16777216 | tf_op jit(solution)/shard_map/pallas_call | solution.py:110
  59.8 1.5 reshape.134
  65.5 8.4 %all-to-all-start.1 = ((f32[16,1,8,3,66]{4,2,3,1,0:T(8,128)}), f32[16,1,8,3,66]{4,2,3,1,0:T(8,128)S(1)}, u32[]{:S(2)}, u32[]{:S(2)}) async-start(f32[16,1,8,3,66]{4,2,3,1,0:T(8,128)} %copy.128), calls=%async_computation.1 | async-start | bytes 393216 | tf_op jit(solution)/shard_map/all_to_all | solution.py:138
  73.9 8.3 %all-to-all-done.1 = f32[16,1,8,3,66]{4,2,3,1,0:T(8,128)S(1)} async-done(((f32[16,1,8,3,66]{4,2,3,1,0:T(8,128)}), f32[16,1,8,3,66]{4,2,3,1,0:T(8,128)S(1)}, u32[]{:S(2)}, u32[]{:S(2)}) %all-to-all-start.1) | async-done | bytes 101408 | tf_op jit(solution)/shard_map/all_to_all | solution.py:138
  87.0 3.2 %multiply_reduce_fusion = (f32[128]{0:T(128)S(1)}, f32[128,1536]{1,0:T(8,128)S(1)}) fusion(bf16[1536,1536]{1,0:T(8,128)(2,1)} %all-gather.4.cloned.1.call-done, bf16[112,1536]{1,0:T(8,128)(2,1)S(1)} %copy-done.6, bf16[16,1536]{1,0:T(8,128)(2,1)S(1)} %fusion.19, bf16[128,1536]{1,0:T(8,128)(2,1)S(1)} %copy-done.4), kind=kOutput, calls=%fused_computation.33 | convolution fusion | flops 605552512 | bytes 6291968 | tf_op jit(solution)/shard_map/dot_general | solution.py:276
  90.4 2.2 convolution_convert_fusion.3
  92.6 4.6 %all-to-all-start.2 = ((bf16[16,48,1536]{2,1,0:T(8,128)(2,1)}), bf16[16,48,1536]{2,1,0:T(8,128)(2,1)}, u32[]{:S(2)}, u32[]{:S(2)}) async-start(bf16[16,48,1536]{2,1,0:T(8,128)(2,1)} %convolution_convert_fusion.3), calls=%async_computation.2 | async-start | bytes 4718592 | tf_op jit(solution)/shard_map/all_to_all | solution.py:311
  97.2 2.3 convolution_convert_fusion.1
  99.5 28.8 %all-to-all-done.2 = bf16[16,48,1536]{2,1,0:T(8,128)(2,1)} async-done(((bf16[16,48,1536]{2,1,0:T(8,128)(2,1)}), bf16[16,48,1536]{2,1,0:T(8,128)(2,1)}, u32[]{:S(2)}, u32[]{:S(2)}) %all-to-all-start.2) | async-done | bytes 2359328 | tf_op jit(solution)/shard_map/all_to_all | solution.py:311
  128.4 3.7 %all-to-all-start.4 = ((bf16[16,48,1536]{2,1,0:T(8,128)(2,1)}), bf16[16,48,1536]{2,1,0:T(8,128)(2,1)S(1)}, u32[]{:S(2)}, u32[]{:S(2)}) async-start(bf16[16,48,1536]{2,1,0:T(8,128)(2,1)} %convolution_convert_fusion.1), calls=%async_computation.4 | async-start | bytes 4718592 | tf_op jit(solution)/shard_map/all_to_all | solution.py:311
  132.1 6.9 %fusion.1 = f32[16,48,1024]{2,1,0:T(8,128)} fusion(bf16[16,48,1536]{2,1,0:T(8,128)(2,1)} %all-to-all-done.2, bf16[1536,2,1024]{2,0,1:T(8,128)(2,1)} %all-gather.6.cloned.1.call-done), kind=kOutput, calls=%fused_computation.10 | convolution fusion | flops 2415919104 | bytes 8650752 | tf_op jit(solution)/shard_map/scd,df->scf/dot_general | solution.py:312
  139.0 5.2 %convolution_convert_fusion.2 = bf16[16,48,1536]{2,1,0:T(8,128)(2,1)} fusion(bf16[1536,2,512]{2,0,1:T(8,128)(2,1)} %all-gather.8.cloned.1.call-done, f32[16,48,1024]{2,1,0:T(8,128)} %fusion.1), kind=kOutput, calls=%fused_computation.5 | convolution fusion | flops 1211498496 | bytes 7077888 | tf_op jit(solution)/shard_map/scf,df->scd/dot_general | solution.py:316
  144.2 21.7 %all-to-all-done.4 = bf16[16,48,1536]{2,1,0:T(8,128)(2,1)S(1)} async-done(((bf16[16,48,1536]{2,1,0:T(8,128)(2,1)}), bf16[16,48,1536]{2,1,0:T(8,128)(2,1)S(1)}, u32[]{:S(2)}, u32[]{:S(2)}) %all-to-all-start.4) | async-done | bytes 2359328 | tf_op jit(solution)/shard_map/all_to_all | solution.py:311
  165.9 1.5 copy-done.3
  167.4 3.7 %all-to-all-start.3 = ((bf16[16,48,1536]{2,1,0:T(8,128)(2,1)}), bf16[16,48,1536]{2,1,0:T(8,128)(2,1)S(1)}, u32[]{:S(2)}, u32[]{:S(2)}) async-start(bf16[16,48,1536]{2,1,0:T(8,128)(2,1)} %convolution_convert_fusion.2), calls=%async_computation.3 | async-start | bytes 4718592 | tf_op jit(solution)/shard_map/all_to_all | solution.py:320
  171.2 5.3 %fusion = f32[16,48,1024]{2,1,0:T(8,128)S(1)} fusion(bf16[16,48,1536]{2,1,0:T(8,128)(2,1)} %copy-done.3, bf16[1536,2,1024]{2,0,1:T(8,128)(2,1)} %all-gather.6.cloned.1.call-done), kind=kOutput, calls=%fused_computation.8 | convolution fusion | flops 2415919104 | bytes 8650752 | tf_op jit(solution)/shard_map/scd,df->scf/dot_general | solution.py:312
  176.5 2.9 %convolution_convert_fusion = bf16[16,48,1536]{2,1,0:T(8,128)(2,1)} fusion(bf16[1536,2,512]{2,0,1:T(8,128)(2,1)S(1)} %copy-done.14, f32[16,48,1024]{2,1,0:T(8,128)S(1)} %fusion), kind=kOutput, calls=%fused_computation.3 | convolution fusion | flops 1211498496 | bytes 7077888 | tf_op jit(solution)/shard_map/scf,df->scd/dot_general | solution.py:316
  179.4 26.0 %all-to-all-done.3 = bf16[16,48,1536]{2,1,0:T(8,128)(2,1)S(1)} async-done(((bf16[16,48,1536]{2,1,0:T(8,128)(2,1)}), bf16[16,48,1536]{2,1,0:T(8,128)(2,1)S(1)}, u32[]{:S(2)}, u32[]{:S(2)}) %all-to-all-start.3) | async-done | bytes 2359328 | tf_op jit(solution)/shard_map/all_to_all | solution.py:320
  205.3 1.4 copy-done.1
  206.8 3.7 %all-to-all-start.5 = ((bf16[16,48,1536]{2,1,0:T(8,128)(2,1)}), bf16[16,48,1536]{2,1,0:T(8,128)(2,1)S(1)}, u32[]{:S(2)}, u32[]{:S(2)}) async-start(bf16[16,48,1536]{2,1,0:T(8,128)(2,1)} %convolution_convert_fusion), calls=%async_computation.5 | async-start | bytes 4718592 | tf_op jit(solution)/shard_map/all_to_all | solution.py:320
  210.8 1.2 fusion.41
  212.2 3.2 %select_reduce_fusion = (f32[128,768]{1,0:T(8,128)}, f32[128,768]{1,0:T(8,128)S(1)}) fusion(s32[128,8]{1,0:T(8,128)S(1)} %copy.149, f32[128,8]{1,0:T(8,128)S(1)} %copy.144, s32[128,8]{1,0:T(8,128)S(1)} %copy.143), kind=kLoop, calls=%fused_computation.11 | loop fusion | flops 4521984 | bytes 798720 | tf_op jit(solution)/shard_map/reduce_sum | solution.py:325
  215.4 3.6 %fusion.42 = f32[128,1536]{1,0:T(8,128)} fusion(f32[128,768]{1,0:T(8,128)S(1)} %get-tuple-element.15, bf16[768,1536]{1,0:T(8,128)(2,1)} %bitcast.79), kind=kOutput, calls=%fused_computation.106 | convolution fusion | flops 1811939328 | bytes 3538944 | tf_op jit(solution)/shard_map/dot_general | solution.py:333
  219.0 25.5 %all-to-all-done.5 = bf16[16,48,1536]{2,1,0:T(8,128)(2,1)S(1)} async-done(((bf16[16,48,1536]{2,1,0:T(8,128)(2,1)}), bf16[16,48,1536]{2,1,0:T(8,128)(2,1)S(1)}, u32[]{:S(2)}, u32[]{:S(2)}) %all-to-all-start.5) | async-done | bytes 2359328 | tf_op jit(solution)/shard_map/all_to_all | solution.py:320
  244.5 3.2 %fusion.2 = f32[128,1536]{1,0:T(8,128)} fusion(f32[128,1536]{1,0:T(8,128)S(1)} %get-tuple-element.30, f32[128,1536]{1,0:T(8,128)} %fusion.42, f32[128,768]{1,0:T(8,128)} %get-tuple-element.14, bf16[768,1536]{1,0:T(8,128)(2,1)S(1)} %bitcast.78), kind=kOutput, calls=%fused_computation.16 | convolution fusion | flops 1812332544 | bytes 5111808 | tf_op jit(solution)/shard_map/dot_general | solution.py:333
  (130 shorter events, 20.0 us)
Async XLA Ops:
  7.2 203.6 %copy-start = (bf16[1536,32]{0,1:T(8,128)(2,1)S(1)}, bf16[1536,32]{0,1:T(8,128)(2,1)}, u32[]{:S(2)}) copy-start(bf16[1536,32]{0,1:T(8,128)(2,1)} %param.26) | copy-start | bytes 294916
  7.2 3.1 %copy-start.11 = (s32[8]{0:T(128)S(1)}, s32[8]{0:T(128)}, u32[]{:S(2)}) copy-start(s32[8]{0:T(128)} %param.20) | copy-start | bytes 100
  7.2 3.4 %copy-start.13 = (s32[16]{0:T(128)S(1)}, s32[16]{0:T(128)}, u32[]{:S(2)}) copy-start(s32[16]{0:T(128)} %param.18) | copy-start | bytes 196
  7.2 4.1 %copy-start.8 = (bf16[16,1536]{1,0:T(8,128)(2,1)S(1)}, bf16[16,1536]{1,0:T(8,128)(2,1)}, u32[]{:S(2)}) copy-start(bf16[16,1536]{1,0:T(8,128)(2,1)} %param.15) | copy-start | bytes 147460
  7.2 12.2 %copy-start.5 = (bf16[192,2,512]{2,1,0:T(2,128)(2,1)S(1)}, bf16[192,2,512]{2,1,0:T(2,128)(2,1)}, u32[]{:S(2)}) copy-start(bf16[192,2,512]{2,1,0:T(2,128)(2,1)} %param.29) | copy-start | bytes 1179652
  7.2 79.8 %all-gather.4.cloned.1.call-start = ((), (), s32[]{:S(2)}) async-start(), calls=%async_computation.6 | async-start | bytes 5308416 | tf_op jit(solution)/shard_map/all_gather | solution.py:273
  8.0 12.8 %slice-start = ((bf16[16,1536]{1,0:T(8,128)(2,1)}), bf16[8,1536]{1,0:T(8,128)(2,1)S(1)}, s32[]{:S(2)}) async-start(bf16[16,1536]{1,0:T(8,128)(2,1)} %param.15), calls=%async_computation.9 | async-start | bytes 49152 | tf_op jit(solution)/shard_map/slice | solution.py:223
  8.0 124.1 %all-gather.6.cloned.1.call-start = ((), (), s32[]{:S(2)}) async-start(), calls=%async_computation.7 | async-start | bytes 7077888 | tf_op jit(solution)/shard_map/all_gather | solution.py:274
  12.3 26.2 %all-to-all-start = ((f32[16,1,1537]{2,1,0:T(1,128)}), f32[16,1,1537]{2,1,0:T(1,128)S(1)}, u32[]{:S(2)}, u32[]{:S(2)}) async-start(f32[16,1,1537]{2,1,0:T(1,128)} %copy.121), calls=%async_computation | async-start | bytes 212992 | tf_op jit(solution)/shard_map/all_to_all | solution.py:138
  19.4 119.6 %all-gather.8.cloned.1.call-start = ((), (), s32[]{:S(2)}) async-start(), calls=%async_computation.8 | async-start | bytes 3538944 | tf_op jit(solution)/shard_map/all_gather | solution.py:275
  22.8 13.0 %copy-start.10 = (bf16[16,1024]{1,0:T(8,128)(2,1)S(1)}, bf16[16,1024]{1,0:T(8,128)(2,1)}, u32[]{:S(2)}) copy-start(bf16[16,1024]{1,0:T(8,128)(2,1)} %param.16) | copy-start | bytes 98308
  22.8 14.8 %copy-start.9 = (s32[128,8]{0,1:T(8,128)S(1)}, s32[128,8]{0,1:T(8,128)}, u32[]{:S(2)}) copy-start(s32[128,8]{0,1:T(8,128)} %param.27) | copy-start | bytes 12292
  33.9 4.7 %copy-start.12 = (bf16[1536]{0:T(1024)(128)(2,1)S(1)}, bf16[1536]{0:T(1024)(128)(2,1)}, u32[]{:S(2)}) copy-start(bf16[1536]{0:T(1024)(128)(2,1)} %param.25) | copy-start | bytes 9220
  65.5 16.7 %all-to-all-start.1 = ((f32[16,1,8,3,66]{4,2,3,1,0:T(8,128)}), f32[16,1,8,3,66]{4,2,3,1,0:T(8,128)S(1)}, u32[]{:S(2)}, u32[]{:S(2)}) async-start(f32[16,1,8,3,66]{4,2,3,1,0:T(8,128)} %copy.128), calls=%async_computation.1 | async-start | bytes 393216 | tf_op jit(solution)/shard_map/all_to_all | solution.py:138
  82.4 4.6 %copy-start.4 = (bf16[128,1536]{1,0:T(8,128)(2,1)S(1)}, bf16[128,1536]{1,0:T(8,128)(2,1)}, u32[]{:S(2)}) copy-start(bf16[128,1536]{1,0:T(8,128)(2,1)} %param.23) | copy-start | bytes 1179652
  82.4 4.6 %copy-start.6 = (bf16[112,1536]{1,0:T(8,128)(2,1)S(1)}, bf16[112,1536]{1,0:T(8,128)(2,1)}, u32[]{:S(2)}) copy-start(bf16[112,1536]{1,0:T(8,128)(2,1)} %param.22) | copy-start | bytes 1032196
  86.9 3.3 %copy-start.7 = (bf16[16,1536]{1,0:T(8,128)(2,1)}, bf16[16,1536]{1,0:T(8,128)(2,1)S(1)}, u32[]{:S(2)}) copy-start(bf16[16,1536]{1,0:T(8,128)(2,1)S(1)} %fusion.19) | copy-start | bytes 147460
  90.4 6.8 %copy-start.2 = (bf16[128,1536]{1,0:T(8,128)(2,1)}, bf16[128,1536]{1,0:T(8,128)(2,1)S(1)}, u32[]{:S(2)}) copy-start(bf16[128,1536]{1,0:T(8,128)(2,1)S(1)} %multiply_convert_fusion) | copy-start | bytes 1179652
  92.6 35.8 %all-to-all-start.2 = ((bf16[16,48,1536]{2,1,0:T(8,128)(2,1)}), bf16[16,48,1536]{2,1,0:T(8,128)(2,1)}, u32[]{:S(2)}, u32[]{:S(2)}) async-start(bf16[16,48,1536]{2,1,0:T(8,128)(2,1)} %convolution_convert_fusion.3), calls=%async_computation.2 | async-start | bytes 4718592 | tf_op jit(solution)/shard_map/all_to_all | solution.py:311
  128.4 37.5 %all-to-all-start.4 = ((bf16[16,48,1536]{2,1,0:T(8,128)(2,1)}), bf16[16,48,1536]{2,1,0:T(8,128)(2,1)S(1)}, u32[]{:S(2)}, u32[]{:S(2)}) async-start(bf16[16,48,1536]{2,1,0:T(8,128)(2,1)} %convolution_convert_fusion.1), calls=%async_computation.4 | async-start | bytes 4718592 | tf_op jit(solution)/shard_map/all_to_all | solution.py:311
  165.9 1.5 copy-start.3
  167.4 37.9 %all-to-all-start.3 = ((bf16[16,48,1536]{2,1,0:T(8,128)(2,1)}), bf16[16,48,1536]{2,1,0:T(8,128)(2,1)S(1)}, u32[]{:S(2)}, u32[]{:S(2)}) async-start(bf16[16,48,1536]{2,1,0:T(8,128)(2,1)} %convolution_convert_fusion.2), calls=%async_computation.3 | async-start | bytes 4718592 | tf_op jit(solution)/shard_map/all_to_all | solution.py:320
  171.1 5.4 %copy-start.14 = (bf16[1536,2,512]{2,0,1:T(8,128)(2,1)S(1)}, bf16[1536,2,512]{2,0,1:T(8,128)(2,1)}, u32[]{:S(2)}) copy-start(bf16[1536,2,512]{2,0,1:T(8,128)(2,1)} %all-gather.8.cloned.1.call-done) | copy-start | bytes 9437188
  205.3 1.4 copy-start.1
  206.8 37.7 %all-to-all-start.5 = ((bf16[16,48,1536]{2,1,0:T(8,128)(2,1)}), bf16[16,48,1536]{2,1,0:T(8,128)(2,1)S(1)}, u32[]{:S(2)}, u32[]{:S(2)}) async-start(bf16[16,48,1536]{2,1,0:T(8,128)(2,1)} %convolution_convert_fusion), calls=%async_computation.5 | async-start | bytes 4718592 | tf_op jit(solution)/shard_map/all_to_all | solution.py:320
Sparse Core Ops, SparseCore 0:
  9.7 33.6 all-gather.3
  45.2 40.9 all-gather.5
  87.9 28.7 all-gather.7

commit v10 on v6

--- a/solution.py
+++ b/solution.py
@@ -74,7 +74,11 @@
     mix = jnp.dot(expos.astype(jnp.bfloat16), values, preferred_element_type=jnp.float32)
     max_ref[0] = jnp.broadcast_to(top, max_ref.shape[1:])
     tot_ref[0] = jnp.broadcast_to(total, tot_ref.shape[1:])
-    mix_ref[0] = mix
+    group = lax.broadcasted_iota(jnp.int32, (HEADS, HEAD), 0) // (HEADS // KV_HEADS)
+    picked = jnp.zeros((HEADS, HEAD), jnp.float32)
+    for h in range(KV_HEADS):
+        picked = picked + jnp.where(group == h, mix[:, h * HEAD : (h + 1) * HEAD], 0.0)
+    mix_ref[0] = picked
 
 
 def paged_attend(query_rows, tables, lengths, pool):
@@ -97,7 +101,7 @@
         out_specs=[
             pl.BlockSpec((1, HEADS, 128), lambda r, t, l: (r, 0, 0)),
             pl.BlockSpec((1, HEADS, 128), lambda r, t, l: (r, 0, 0)),
-            pl.BlockSpec((1, HEADS, half), lambda r, t, l: (r, 0, 0)),
+            pl.BlockSpec((1, HEADS, HEAD), lambda r, t, l: (r, 0, 0)),
         ],
         scratch_shapes=[
             pltpu.VMEM((2, NPAGE, PAGE, kv_width), pool.dtype),
@@ -110,7 +114,7 @@
         out_shape=[
             jax.ShapeDtypeStruct((count, HEADS, 128), jnp.float32),
             jax.ShapeDtypeStruct((count, HEADS, 128), jnp.float32),
-            jax.ShapeDtypeStruct((count, HEADS, half), jnp.float32),
+            jax.ShapeDtypeStruct((count, HEADS, HEAD), jnp.float32),
         ],
         compiler_params=pltpu.CompilerParams(dimension_semantics=("arbitrary",)),
         cost_estimate=pl.CostEstimate(
@@ -119,8 +123,7 @@
             bytes_accessed=count * MAXLEN * kv_width * 2,
         ),
     )(tables, lengths, spread, pool)
-    blocks = mix.reshape(count, KV_HEADS, group_size, KV_HEADS, HEAD)
-    mixture = jnp.sum(jnp.where(mask[None, :, None, :, None], blocks, 0.0), axis=3)
+    mixture = mix.reshape(count, KV_HEADS, group_size, HEAD)
     return (
         top[:, :, 0].reshape(count, KV_HEADS, group_size),
         total[:, :, 0].reshape(count, KV_HEADS, group_size),

time: 253 us -> 251 us (level)
    reshape x2 -> x0, local copies, waits for them, and re-layouts: 2.79 us -> none  [paged_attend(): blocks = mix.reshape(count, KV_HEADS, group_size, KV_HEADS, HEAD)]
  transfers between devices with their start and end apart: 9 -> 9, of which waited for: 5 -> 5; matrix products, arithmetic and copies ran while one was open for 24% -> 23% of each run, Pallas kernels for 10% -> 11%
where the time goes in v10:
time: 251 us; the launch traced here: 249 us
  waiting for transfers between devices  109 us (43%)
  matrix products  41.8 us (17%)
  starting transfers between devices  32.6 us (13%)
  Pallas kernels  26.6 us (11%)
  local copies, waits for them, and re-layouts  18.7 us (7%)
  between operations  14.3 us (6%)
  other arithmetic  5.24 us (2%)
    all_to_all x2, waiting for transfers between devices, body(): lax.all_to_all(outgoing, 'gy', split_axis=0, concat_axis=0, tiled=True)  50.6 us
    all_to_all x2, waiting for transfers between devices, body(): lax.all_to_all(expert_rows, 'gy', split_axis=0, concat_axis=0, tiled=True)  49.8 us
    pallas_call x2, Pallas kernels, paged_attend(): pl.pallas_call(attend_kernel, grid_spec=grid_spec, out_shape=[jax.ShapeDt...  26.6 us
    all_to_all x2, starting transfers between devices, in_one_piece(): lax.all_to_all(both, axis, split_axis=split_dim, concat_axis=concat_dim,...  14.6 us
    dot_general x2, matrix products, body(): jnp.dot(one_hot, part.reshape(columns * CAP, D), preferred_element_type=j...  13.1 us
    dot_general x2, matrix products, body(): jnp.einsum('scd,df->scf', arrived, full_pair[:, local], preferred_element...  12.2 us
    all_to_all x2, starting transfers between devices, body(): lax.all_to_all(outgoing, 'gy', split_axis=0, concat_axis=0, tiled=True)  9.07 us
    all_to_all x2, starting transfers between devices, body(): lax.all_to_all(expert_rows, 'gy', split_axis=0, concat_axis=0, tiled=True)  8.89 us
  transfers between devices with their start and end apart: 9, of which 5 were waited for; matrix products, arithmetic and copies ran while one was open for 23% of the time, Pallas kernels for 11%

profile of v10, /device:TPU:96, one launch (start us, length us, event | category | flops | bytes accessed | tf_op | source)
XLA Modules:
  0.0 248.7 jit_solution(18223527426063822907)
XLA Ops:
  8.0 2.2 copy.132
  12.3 7.0 %all-to-all-start = ((f32[16,1,1537]{2,1,0:T(1,128)}), f32[16,1,1537]{2,1,0:T(1,128)S(1)}, u32[]{:S(2)}, u32[]{:S(2)}) async-start(f32[16,1,1537]{2,1,0:T(1,128)} %copy.106), calls=%async_computation | async-start | bytes 212992 | tf_op jit(solution)/shard_map/all_to_all | solution.py:138
  22.6 10.8 %shard_map.158 = (f32[8,24,128]{2,1,0:T(8,128)}, f32[8,24,128]{2,1,0:T(8,128)}, f32[8,24,64]{2,1,0:T(8,128)}) custom-call(s32[8,32]{1,0:T(8,128)} %tables.2, s32[8]{0:T(128)} %get-tuple-element.30.lengths, bf16[8,24,512]{2,1,0:T(8,128)(2,1)} %broadcast_select_fusion.1.q_ref, bf16[128,16,1024]{2,1,0:T(8,128)(2,1)} %pool_ref.3), custom_call_target="tpu_custom_call" | custom-call | flops 201326592 | bytes 8388608 | tf_op jit(solution)/shard_map/pallas_call | solution.py:111
  33.4 1.0 slice_reduce_fusion
  34.8 1.0 slice_reduce_fusion.1
  36.0 1.0 concatenate.26
  38.1 0.8 broadcast_select_fusion.q_ref
  38.9 0.9 fusion.27.lengths
  39.8 15.8 %shard_map.159 = (f32[16,24,128]{2,1,0:T(8,128)}, f32[16,24,128]{2,1,0:T(8,128)}, f32[16,24,64]{2,1,0:T(8,128)}) custom-call(s32[16,32]{1,0:T(8,128)} %tables.3, s32[16]{0:T(128)} %fusion.27.lengths, bf16[16,24,512]{2,1,0:T(8,128)(2,1)} %broadcast_select_fusion.q_ref, bf16[128,16,1024]{2,1,0:T(8,128)(2,1)} %pool_ref.3), custom_call_target="tpu_custom_call" | custom-call | flops 402653184 | bytes 16777216 | tf_op jit(solution)/shard_map/pallas_call | solution.py:111
  55.6 1.2 copy.107
  56.7 1.2 copy.108
  58.3 1.0 copy.109
  60.2 7.5 %all-to-all-start.1 = ((f32[16,1,8,3,66]{4,2,3,1,0:T(8,128)}), f32[16,1,8,3,66]{4,2,3,1,0:T(8,128)S(1)}, u32[]{:S(2)}, u32[]{:S(2)}) async-start(f32[16,1,8,3,66]{4,2,3,1,0:T(8,128)} %copy.112), calls=%async_computation.1 | async-start | bytes 393216 | tf_op jit(solution)/shard_map/all_to_all | solution.py:138
  67.8 8.3 %all-to-all-done.1 = f32[16,1,8,3,66]{4,2,3,1,0:T(8,128)S(1)} async-done(((f32[16,1,8,3,66]{4,2,3,1,0:T(8,128)}), f32[16,1,8,3,66]{4,2,3,1,0:T(8,128)S(1)}, u32[]{:S(2)}, u32[]{:S(2)}) %all-to-all-start.1) | async-done | bytes 101408 | tf_op jit(solution)/shard_map/all_to_all | solution.py:138
  80.8 3.3 %multiply_reduce_fusion = (f32[128]{0:T(128)S(1)}, f32[128,1536]{1,0:T(8,128)S(1)}) fusion(bf16[1536,1536]{1,0:T(8,128)(2,1)} %all-gather.4.cloned.1.call-done, bf16[112,1536]{1,0:T(8,128)(2,1)S(1)} %copy-done.3, bf16[16,1536]{1,0:T(8,128)(2,1)S(1)} %fusion.22, bf16[128,1536]{1,0:T(8,128)(2,1)S(1)} %copy-done.1), kind=kOutput, calls=%fused_computation.31 | convolution fusion | flops 605552512 | bytes 6291968 | tf_op jit(solution)/shard_map/dot_general | solution.py:276
  84.3 2.2 convolution_convert_fusion.3
  86.4 4.4 %all-to-all-start.2 = ((bf16[16,48,1536]{2,1,0:T(8,128)(2,1)}), bf16[16,48,1536]{2,1,0:T(8,128)(2,1)}, u32[]{:S(2)}, u32[]{:S(2)}) async-start(bf16[16,48,1536]{2,1,0:T(8,128)(2,1)} %convolution_convert_fusion.3), calls=%async_computation.2 | async-start | bytes 4718592 | tf_op jit(solution)/shard_map/all_to_all | solution.py:311
  90.9 2.2 convolution_convert_fusion.1
  93.1 29.9 %all-to-all-done.2 = bf16[16,48,1536]{2,1,0:T(8,128)(2,1)} async-done(((bf16[16,48,1536]{2,1,0:T(8,128)(2,1)}), bf16[16,48,1536]{2,1,0:T(8,128)(2,1)}, u32[]{:S(2)}, u32[]{:S(2)}) %all-to-all-start.2) | async-done | bytes 2359328 | tf_op jit(solution)/shard_map/all_to_all | solution.py:311
  123.0 4.6 %all-to-all-start.4 = ((bf16[16,48,1536]{2,1,0:T(8,128)(2,1)}), bf16[16,48,1536]{2,1,0:T(8,128)(2,1)}, u32[]{:S(2)}, u32[]{:S(2)}) async-start(bf16[16,48,1536]{2,1,0:T(8,128)(2,1)} %convolution_convert_fusion.1), calls=%async_computation.4 | async-start | bytes 4718592 | tf_op jit(solution)/shard_map/all_to_all | solution.py:311
  127.7 6.8 %fusion.2 = f32[16,48,1024]{2,1,0:T(8,128)} fusion(bf16[16,48,1536]{2,1,0:T(8,128)(2,1)} %all-to-all-done.2, bf16[1536,2,1024]{2,0,1:T(8,128)(2,1)} %all-gather.6.cloned.1.call-done), kind=kOutput, calls=%fused_computation.12 | convolution fusion | flops 2415919104 | bytes 8650752 | tf_op jit(solution)/shard_map/scd,df->scf/dot_general | solution.py:312
  134.5 5.2 %convolution_convert_fusion.2 = bf16[16,48,1536]{2,1,0:T(8,128)(2,1)} fusion(bf16[1536,2,512]{2,0,1:T(8,128)(2,1)} %all-gather.8.cloned.1.call-done, f32[16,48,1024]{2,1,0:T(8,128)} %fusion.2), kind=kOutput, calls=%fused_computation.7 | convolution fusion | flops 1211498496 | bytes 7077888 | tf_op jit(solution)/shard_map/scf,df->scd/dot_general | solution.py:316
  139.7 20.6 %all-to-all-done.4 = bf16[16,48,1536]{2,1,0:T(8,128)(2,1)} async-done(((bf16[16,48,1536]{2,1,0:T(8,128)(2,1)}), bf16[16,48,1536]{2,1,0:T(8,128)(2,1)}, u32[]{:S(2)}, u32[]{:S(2)}) %all-to-all-start.4) | async-done | bytes 2359328 | tf_op jit(solution)/shard_map/all_to_all | solution.py:311
  160.3 4.5 %all-to-all-start.3 = ((bf16[16,48,1536]{2,1,0:T(8,128)(2,1)}), bf16[16,48,1536]{2,1,0:T(8,128)(2,1)}, u32[]{:S(2)}, u32[]{:S(2)}) async-start(bf16[16,48,1536]{2,1,0:T(8,128)(2,1)} %convolution_convert_fusion.2), calls=%async_computation.3 | async-start | bytes 4718592 | tf_op jit(solution)/shard_map/all_to_all | solution.py:320
  164.8 5.3 %fusion.1 = f32[16,48,1024]{2,1,0:T(8,128)S(1)} fusion(bf16[16,48,1536]{2,1,0:T(8,128)(2,1)} %all-to-all-done.4, bf16[1536,2,1024]{2,0,1:T(8,128)(2,1)} %all-gather.6.cloned.1.call-done), kind=kOutput, calls=%fused_computation.10 | convolution fusion | flops 2415919104 | bytes 8650752 | tf_op jit(solution)/shard_map/scd,df->scf/dot_general | solution.py:312
  170.1 2.9 %convolution_convert_fusion = bf16[16,48,1536]{2,1,0:T(8,128)(2,1)} fusion(bf16[1536,2,512]{2,0,1:T(8,128)(2,1)S(1)} %copy-done.11, f32[16,48,1024]{2,1,0:T(8,128)S(1)} %fusion.1), kind=kOutput, calls=%fused_computation.5 | convolution fusion | flops 1211498496 | bytes 7077888 | tf_op jit(solution)/shard_map/scf,df->scd/dot_general | solution.py:316
  173.0 24.4 %all-to-all-done.3 = bf16[16,48,1536]{2,1,0:T(8,128)(2,1)} async-done(((bf16[16,48,1536]{2,1,0:T(8,128)(2,1)}), bf16[16,48,1536]{2,1,0:T(8,128)(2,1)}, u32[]{:S(2)}, u32[]{:S(2)}) %all-to-all-start.3) | async-done | bytes 2359328 | tf_op jit(solution)/shard_map/all_to_all | solution.py:320
  197.4 4.4 %all-to-all-start.5 = ((bf16[16,48,1536]{2,1,0:T(8,128)(2,1)}), bf16[16,48,1536]{2,1,0:T(8,128)(2,1)}, u32[]{:S(2)}, u32[]{:S(2)}) async-start(bf16[16,48,1536]{2,1,0:T(8,128)(2,1)} %convolution_convert_fusion), calls=%async_computation.5 | async-start | bytes 4718592 | tf_op jit(solution)/shard_map/all_to_all | solution.py:320
  202.8 6.3 %fusion.3 = f32[1024,1536]{1,0:T(8,128)} fusion(bf16[768,1536]{1,0:T(8,128)(2,1)} %bitcast.19, s32[1024]{0:T(1024)S(1)} %get-tuple-element.24), kind=kOutput, calls=%fused_computation.15 | convolution fusion | flops 2416705536 | bytes 8654848 | tf_op jit(solution)/shard_map/dot_general | solution.py:332
  209.1 25.4 %all-to-all-done.5 = bf16[16,48,1536]{2,1,0:T(8,128)(2,1)} async-done(((bf16[16,48,1536]{2,1,0:T(8,128)(2,1)}), bf16[16,48,1536]{2,1,0:T(8,128)(2,1)}, u32[]{:S(2)}, u32[]{:S(2)}) %all-to-all-start.5) | async-done | bytes 2359328 | tf_op jit(solution)/shard_map/all_to_all | solution.py:320
  234.5 6.7 %fusion = f32[128,1536]{1,0:T(8,128)S(1)} fusion(f32[1024,1536]{1,0:T(8,128)} %fusion.3, bf16[768,1536]{1,0:T(8,128)(2,1)} %bitcast.25, f32[128,8]{1,0:T(8,128)S(1)} %copy.127, s32[1024]{0:T(1024)S(1)} %get-tuple-element.23), kind=kOutput, calls=%fused_computation.4 | convolution fusion | flops 2421227520 | bytes 9445376 | tf_op jit(solution)/shard_map/dot_general | solution.py:332
  241.2 1.0 add.89
  (117 shorter events, 14.6 us)
Async XLA Ops:
  7.2 195.2 %copy-start = (bf16[1536,32]{0,1:T(8,128)(2,1)S(1)}, bf16[1536,32]{0,1:T(8,128)(2,1)}, u32[]{:S(2)}) copy-start(bf16[1536,32]{0,1:T(8,128)(2,1)} %param.26) | copy-start | bytes 294916
  7.2 3.1 %copy-start.8 = (s32[8]{0:T(128)S(1)}, s32[8]{0:T(128)}, u32[]{:S(2)}) copy-start(s32[8]{0:T(128)} %param.20) | copy-start | bytes 100
  7.2 3.4 %copy-start.10 = (s32[16]{0:T(128)S(1)}, s32[16]{0:T(128)}, u32[]{:S(2)}) copy-start(s32[16]{0:T(128)} %param.18) | copy-start | bytes 196
  7.2 4.1 %copy-start.5 = (bf16[16,1536]{1,0:T(8,128)(2,1)S(1)}, bf16[16,1536]{1,0:T(8,128)(2,1)}, u32[]{:S(2)}) copy-start(bf16[16,1536]{1,0:T(8,128)(2,1)} %param.15) | copy-start | bytes 147460
  7.2 12.2 %copy-start.2 = (bf16[192,2,512]{2,1,0:T(2,128)(2,1)S(1)}, bf16[192,2,512]{2,1,0:T(2,128)(2,1)}, u32[]{:S(2)}) copy-start(bf16[192,2,512]{2,1,0:T(2,128)(2,1)} %param.29) | copy-start | bytes 1179652
  7.2 73.6 %all-gather.4.cloned.1.call-start = ((), (), s32[]{:S(2)}) async-start(), calls=%async_computation.6 | async-start | bytes 5308416 | tf_op jit(solution)/shard_map/all_gather | solution.py:273
  8.0 12.4 %copy-start.6 = (s32[128,8]{0,1:T(8,128)S(1)}, s32[128,8]{0,1:T(8,128)}, u32[]{:S(2)}) copy-start(s32[128,8]{0,1:T(8,128)} %param.27) | copy-start | bytes 12292
  8.0 12.6 %copy-start.9 = (bf16[1536]{0:T(1024)(128)(2,1)S(1)}, bf16[1536]{0:T(1024)(128)(2,1)}, u32[]{:S(2)}) copy-start(bf16[1536]{0:T(1024)(128)(2,1)} %param.25) | copy-start | bytes 9220
  8.0 12.9 %slice-start = ((bf16[16,1536]{1,0:T(8,128)(2,1)}), bf16[8,1536]{1,0:T(8,128)(2,1)S(1)}, s32[]{:S(2)}) async-start(bf16[16,1536]{1,0:T(8,128)(2,1)} %param.15), calls=%async_computation.9 | async-start | bytes 49152 | tf_op jit(solution)/shard_map/slice | solution.py:223
  8.0 13.0 %copy-start.7 = (bf16[16,1024]{1,0:T(8,128)(2,1)S(1)}, bf16[16,1024]{1,0:T(8,128)(2,1)}, u32[]{:S(2)}) copy-start(bf16[16,1024]{1,0:T(8,128)(2,1)} %param.16) | copy-start | bytes 98308
  8.0 119.7 %all-gather.6.cloned.1.call-start = ((), (), s32[]{:S(2)}) async-start(), calls=%async_computation.7 | async-start | bytes 7077888 | tf_op jit(solution)/shard_map/all_gather | solution.py:274
  12.3 24.7 %all-to-all-start = ((f32[16,1,1537]{2,1,0:T(1,128)}), f32[16,1,1537]{2,1,0:T(1,128)S(1)}, u32[]{:S(2)}, u32[]{:S(2)}) async-start(f32[16,1,1537]{2,1,0:T(1,128)} %copy.106), calls=%async_computation | async-start | bytes 212992 | tf_op jit(solution)/shard_map/all_to_all | solution.py:138
  19.3 115.2 %all-gather.8.cloned.1.call-start = ((), (), s32[]{:S(2)}) async-start(), calls=%async_computation.8 | async-start | bytes 3538944 | tf_op jit(solution)/shard_map/all_gather | solution.py:275
  60.2 15.9 %all-to-all-start.1 = ((f32[16,1,8,3,66]{4,2,3,1,0:T(8,128)}), f32[16,1,8,3,66]{4,2,3,1,0:T(8,128)S(1)}, u32[]{:S(2)}, u32[]{:S(2)}) async-start(f32[16,1,8,3,66]{4,2,3,1,0:T(8,128)} %copy.112), calls=%async_computation.1 | async-start | bytes 393216 | tf_op jit(solution)/shard_map/all_to_all | solution.py:138
  76.8 4.0 %copy-start.1 = (bf16[128,1536]{1,0:T(8,128)(2,1)S(1)}, bf16[128,1536]{1,0:T(8,128)(2,1)}, u32[]{:S(2)}) copy-start(bf16[128,1536]{1,0:T(8,128)(2,1)} %param.23) | copy-start | bytes 1179652
  76.8 4.0 %copy-start.3 = (bf16[112,1536]{1,0:T(8,128)(2,1)S(1)}, bf16[112,1536]{1,0:T(8,128)(2,1)}, u32[]{:S(2)}) copy-start(bf16[112,1536]{1,0:T(8,128)(2,1)} %param.22) | copy-start | bytes 1032196
  80.8 3.3 %copy-start.4 = (bf16[16,1536]{1,0:T(8,128)(2,1)}, bf16[16,1536]{1,0:T(8,128)(2,1)S(1)}, u32[]{:S(2)}) copy-start(bf16[16,1536]{1,0:T(8,128)(2,1)S(1)} %fusion.22) | copy-start | bytes 147460
  86.4 36.6 %all-to-all-start.2 = ((bf16[16,48,1536]{2,1,0:T(8,128)(2,1)}), bf16[16,48,1536]{2,1,0:T(8,128)(2,1)}, u32[]{:S(2)}, u32[]{:S(2)}) async-start(bf16[16,48,1536]{2,1,0:T(8,128)(2,1)} %convolution_convert_fusion.3), calls=%async_computation.2 | async-start | bytes 4718592 | tf_op jit(solution)/shard_map/all_to_all | solution.py:311
  123.0 37.3 %all-to-all-start.4 = ((bf16[16,48,1536]{2,1,0:T(8,128)(2,1)}), bf16[16,48,1536]{2,1,0:T(8,128)(2,1)}, u32[]{:S(2)}, u32[]{:S(2)}) async-start(bf16[16,48,1536]{2,1,0:T(8,128)(2,1)} %convolution_convert_fusion.1), calls=%async_computation.4 | async-start | bytes 4718592 | tf_op jit(solution)/shard_map/all_to_all | solution.py:311
  160.3 37.1 %all-to-all-start.3 = ((bf16[16,48,1536]{2,1,0:T(8,128)(2,1)}), bf16[16,48,1536]{2,1,0:T(8,128)(2,1)}, u32[]{:S(2)}, u32[]{:S(2)}) async-start(bf16[16,48,1536]{2,1,0:T(8,128)(2,1)} %convolution_convert_fusion.2), calls=%async_computation.3 | async-start | bytes 4718592 | tf_op jit(solution)/shard_map/all_to_all | solution.py:320
  164.8 5.4 %copy-start.11 = (bf16[1536,2,512]{2,0,1:T(8,128)(2,1)S(1)}, bf16[1536,2,512]{2,0,1:T(8,128)(2,1)}, u32[]{:S(2)}) copy-start(bf16[1536,2,512]{2,0,1:T(8,128)(2,1)} %all-gather.8.cloned.1.call-done) | copy-start | bytes 9437188
  197.4 37.0 %all-to-all-start.5 = ((bf16[16,48,1536]{2,1,0:T(8,128)(2,1)}), bf16[16,48,1536]{2,1,0:T(8,128)(2,1)}, u32[]{:S(2)}, u32[]{:S(2)}) async-start(bf16[16,48,1536]{2,1,0:T(8,128)(2,1)} %convolution_convert_fusion), calls=%async_computation.5 | async-start | bytes 4718592 | tf_op jit(solution)/shard_map/all_to_all | solution.py:320
Sparse Core Ops, SparseCore 0:
  9.7 33.6 all-gather.3
  45.7 40.9 all-gather.5
  88.5 28.7 all-gather.7

commit v11 on v6

--- a/solution.py
+++ b/solution.py
@@ -59,22 +59,30 @@
         return carry
 
     lax.fori_loop(0, pages_of(r), wait_one, 0)
-    kv = kvbuf.at[slot]
-    keys = kv[:, :, :half].reshape(MAXLEN, half)
-    values = kv[:, :, half:].reshape(MAXLEN, half)
-    q = q_ref[0]
-    scores = lax.dot_general(
-        q, keys, (((1,), (1,)), ((), ())), preferred_element_type=jnp.float32
-    ) * (1.0 / math.sqrt(HEAD))
-    valid = lax.broadcasted_iota(jnp.int32, scores.shape, 1) < lengths[r]
-    masked = jnp.where(valid, scores, -1e30)
-    top = jnp.max(masked, axis=1, keepdims=True)
-    expos = jnp.where(valid, jnp.exp(masked - top), 0.0)
-    total = jnp.sum(expos, axis=1, keepdims=True)
-    mix = jnp.dot(expos.astype(jnp.bfloat16), values, preferred_element_type=jnp.float32)
-    max_ref[0] = jnp.broadcast_to(top, max_ref.shape[1:])
-    tot_ref[0] = jnp.broadcast_to(total, tot_ref.shape[1:])
-    mix_ref[0] = mix
+    @pl.when(lengths[r] == 0)
+    def _():
+        max_ref[...] = jnp.full(max_ref.shape, -1e30, max_ref.dtype)
+        tot_ref[...] = jnp.zeros(tot_ref.shape, tot_ref.dtype)
+        mix_ref[...] = jnp.zeros(mix_ref.shape, mix_ref.dtype)
+
+    @pl.when(lengths[r] > 0)
+    def _():
+        kv = kvbuf.at[slot]
+        keys = kv[:, :, :half].reshape(MAXLEN, half)
+        values = kv[:, :, half:].reshape(MAXLEN, half)
+        q = q_ref[0]
+        scores = lax.dot_general(
+            q, keys, (((1,), (1,)), ((), ())), preferred_element_type=jnp.float32
+        ) * (1.0 / math.sqrt(HEAD))
+        valid = lax.broadcasted_iota(jnp.int32, scores.shape, 1) < lengths[r]
+        masked = jnp.where(valid, scores, -1e30)
+        top = jnp.max(masked, axis=1, keepdims=True)
+        expos = jnp.where(valid, jnp.exp(masked - top), 0.0)
+        total = jnp.sum(expos, axis=1, keepdims=True)
+        mix = jnp.dot(expos.astype(jnp.bfloat16), values, preferred_element_type=jnp.float32)
+        max_ref[0] = jnp.broadcast_to(top, max_ref.shape[1:])
+        tot_ref[0] = jnp.broadcast_to(total, tot_ref.shape[1:])
+        mix_ref[0] = mix
 
 
 def paged_attend(query_rows, tables, lengths, pool):

time: 253 us -> 253 us (level)
  no operation moved by 1% of the time
where the time goes in v11:
time: 253 us; the launch traced here: 248 us
  waiting for transfers between devices  108 us (43%)
  matrix products  41.8 us (17%)
  starting transfers between devices  34.1 us (13%)
  Pallas kernels  23.6 us (9%)
  local copies, waits for them, and re-layouts  19.8 us (8%)
  between operations  14.3 us (6%)
  other arithmetic  6.35 us (3%)
    all_to_all x2, waiting for transfers between devices, body(): lax.all_to_all(expert_rows, 'gy', split_axis=0, concat_axis=0, tiled=True)  49.7 us
    all_to_all x2, waiting for transfers between devices, body(): lax.all_to_all(outgoing, 'gy', split_axis=0, concat_axis=0, tiled=True)  49.5 us
    pallas_call x2, Pallas kernels, paged_attend(): pl.pallas_call(attend_kernel, grid_spec=grid_spec, out_shape=[jax.ShapeDt...  23.6 us
    all_to_all x2, starting transfers between devices, in_one_piece(): lax.all_to_all(both, axis, split_axis=split_dim, concat_axis=concat_dim,...  16 us
    dot_general x2, matrix products, body(): jnp.dot(one_hot, part.reshape(columns * CAP, D), preferred_element_type=j...  13.1 us
    dot_general x2, matrix products, body(): jnp.einsum('scd,df->scf', arrived, full_pair[:, local], preferred_element...  12.2 us
    all_to_all x2, starting transfers between devices, body(): lax.all_to_all(outgoing, 'gy', split_axis=0, concat_axis=0, tiled=True)  9.08 us
    all_to_all x2, starting transfers between devices, body(): lax.all_to_all(expert_rows, 'gy', split_axis=0, concat_axis=0, tiled=True)  8.89 us
  transfers between devices with their start and end apart: 9, of which 5 were waited for; matrix products, arithmetic and copies ran while one was open for 24% of the time, Pallas kernels for 10%

profile of v11, /device:TPU:96, one launch (start us, length us, event | category | flops | bytes accessed | tf_op | source)
XLA Modules:
  0.0 248.3 jit_solution(4838823053489474468)
XLA Ops:
  8.0 2.2 copy.125
  12.3 7.0 %all-to-all-start = ((f32[16,1,1537]{2,1,0:T(1,128)}), f32[16,1,1537]{2,1,0:T(1,128)S(1)}, u32[]{:S(2)}, u32[]{:S(2)}) async-start(f32[16,1,1537]{2,1,0:T(1,128)} %copy.100), calls=%async_computation | async-start | bytes 212992 | tf_op jit(solution)/shard_map/all_to_all | solution.py:143
  22.6 9.8 %shard_map.158 = (f32[8,24,128]{2,1,0:T(8,128)}, f32[8,24,128]{2,1,0:T(8,128)}, f32[8,24,512]{2,1,0:T(8,128)}) custom-call(s32[8,32]{1,0:T(8,128)} %tables.2, s32[8]{0:T(128)} %get-tuple-element.30.lengths, bf16[8,24,512]{2,1,0:T(8,128)(2,1)} %broadcast_select_fusion.1.q_ref, bf16[128,16,1024]{2,1,0:T(8,128)(2,1)} %pool_ref.3), custom_call_target="tpu_custom_call" | custom-call | flops 201326592 | bytes 8388608 | tf_op jit(solution)/shard_map/pallas_call | solution.py:115
  32.4 1.0 slice_reduce_fusion.1
  33.4 1.0 slice_reduce_fusion
  34.9 1.2 reshape.221
  37.8 0.8 broadcast_select_fusion.q_ref
  38.6 0.9 fusion.27.lengths
  39.5 13.8 %shard_map.159 = (f32[16,24,128]{2,1,0:T(8,128)}, f32[16,24,128]{2,1,0:T(8,128)}, f32[16,24,512]{2,1,0:T(8,128)}) custom-call(s32[16,32]{1,0:T(8,128)} %tables.3, s32[16]{0:T(128)} %fusion.27.lengths, bf16[16,24,512]{2,1,0:T(8,128)(2,1)} %broadcast_select_fusion.q_ref, bf16[128,16,1024]{2,1,0:T(8,128)(2,1)} %pool_ref.3), custom_call_target="tpu_custom_call" | custom-call | flops 402653184 | bytes 16777216 | tf_op jit(solution)/shard_map/pallas_call | solution.py:115
  53.3 1.1 copy.101
  54.4 1.1 copy.102
  56.3 1.6 reshape.217
  59.5 9.0 %all-to-all-start.1 = ((f32[16,1,8,3,66]{4,2,3,1,0:T(8,128)}), f32[16,1,8,3,66]{4,2,3,1,0:T(8,128)S(1)}, u32[]{:S(2)}, u32[]{:S(2)}) async-start(f32[16,1,8,3,66]{4,2,3,1,0:T(8,128)} %copy.105), calls=%async_computation.1 | async-start | bytes 393216 | tf_op jit(solution)/shard_map/all_to_all | solution.py:143
  68.5 8.3 %all-to-all-done.1 = f32[16,1,8,3,66]{4,2,3,1,0:T(8,128)S(1)} async-done(((f32[16,1,8,3,66]{4,2,3,1,0:T(8,128)}), f32[16,1,8,3,66]{4,2,3,1,0:T(8,128)S(1)}, u32[]{:S(2)}, u32[]{:S(2)}) %all-to-all-start.1) | async-done | bytes 101408 | tf_op jit(solution)/shard_map/all_to_all | solution.py:143
  81.6 3.3 %multiply_reduce_fusion = (f32[128]{0:T(128)S(1)}, f32[128,1536]{1,0:T(8,128)S(1)}) fusion(bf16[1536,1536]{1,0:T(8,128)(2,1)} %all-gather.4.cloned.1.call-done, bf16[112,1536]{1,0:T(8,128)(2,1)S(1)} %copy-done.3, bf16[16,1536]{1,0:T(8,128)(2,1)S(1)} %fusion.22, bf16[128,1536]{1,0:T(8,128)(2,1)S(1)} %copy-done.1), kind=kOutput, calls=%fused_computation.32 | convolution fusion | flops 605552512 | bytes 6291968 | tf_op jit(solution)/shard_map/dot_general | solution.py:281
  85.0 2.2 convolution_convert_fusion.3
  87.2 4.4 %all-to-all-start.2 = ((bf16[16,48,1536]{2,1,0:T(8,128)(2,1)}), bf16[16,48,1536]{2,1,0:T(8,128)(2,1)}, u32[]{:S(2)}, u32[]{:S(2)}) async-start(bf16[16,48,1536]{2,1,0:T(8,128)(2,1)} %convolution_convert_fusion.3), calls=%async_computation.2 | async-start | bytes 4718592 | tf_op jit(solution)/shard_map/all_to_all | solution.py:316
  91.7 2.2 convolution_convert_fusion.1
  93.8 29.1 %all-to-all-done.2 = bf16[16,48,1536]{2,1,0:T(8,128)(2,1)} async-done(((bf16[16,48,1536]{2,1,0:T(8,128)(2,1)}), bf16[16,48,1536]{2,1,0:T(8,128)(2,1)}, u32[]{:S(2)}, u32[]{:S(2)}) %all-to-all-start.2) | async-done | bytes 2359328 | tf_op jit(solution)/shard_map/all_to_all | solution.py:316
  122.9 4.6 %all-to-all-start.4 = ((bf16[16,48,1536]{2,1,0:T(8,128)(2,1)}), bf16[16,48,1536]{2,1,0:T(8,128)(2,1)}, u32[]{:S(2)}, u32[]{:S(2)}) async-start(bf16[16,48,1536]{2,1,0:T(8,128)(2,1)} %convolution_convert_fusion.1), calls=%async_computation.4 | async-start | bytes 4718592 | tf_op jit(solution)/shard_map/all_to_all | solution.py:316
  127.6 6.8 %fusion.2 = f32[16,48,1024]{2,1,0:T(8,128)} fusion(bf16[16,48,1536]{2,1,0:T(8,128)(2,1)} %all-to-all-done.2, bf16[1536,2,1024]{2,0,1:T(8,128)(2,1)} %all-gather.6.cloned.1.call-done), kind=kOutput, calls=%fused_computation.12 | convolution fusion | flops 2415919104 | bytes 8650752 | tf_op jit(solution)/shard_map/scd,df->scf/dot_general | solution.py:317
  134.4 5.2 %convolution_convert_fusion.2 = bf16[16,48,1536]{2,1,0:T(8,128)(2,1)} fusion(bf16[1536,2,512]{2,0,1:T(8,128)(2,1)} %all-gather.8.cloned.1.call-done, f32[16,48,1024]{2,1,0:T(8,128)} %fusion.2), kind=kOutput, calls=%fused_computation.7 | convolution fusion | flops 1211498496 | bytes 7077888 | tf_op jit(solution)/shard_map/scf,df->scd/dot_general | solution.py:321
  139.6 20.4 %all-to-all-done.4 = bf16[16,48,1536]{2,1,0:T(8,128)(2,1)} async-done(((bf16[16,48,1536]{2,1,0:T(8,128)(2,1)}), bf16[16,48,1536]{2,1,0:T(8,128)(2,1)}, u32[]{:S(2)}, u32[]{:S(2)}) %all-to-all-start.4) | async-done | bytes 2359328 | tf_op jit(solution)/shard_map/all_to_all | solution.py:316
  160.0 4.5 %all-to-all-start.3 = ((bf16[16,48,1536]{2,1,0:T(8,128)(2,1)}), bf16[16,48,1536]{2,1,0:T(8,128)(2,1)}, u32[]{:S(2)}, u32[]{:S(2)}) async-start(bf16[16,48,1536]{2,1,0:T(8,128)(2,1)} %convolution_convert_fusion.2), calls=%async_computation.3 | async-start | bytes 4718592 | tf_op jit(solution)/shard_map/all_to_all | solution.py:325
  164.5 5.3 %fusion.1 = f32[16,48,1024]{2,1,0:T(8,128)S(1)} fusion(bf16[16,48,1536]{2,1,0:T(8,128)(2,1)} %all-to-all-done.4, bf16[1536,2,1024]{2,0,1:T(8,128)(2,1)} %all-gather.6.cloned.1.call-done), kind=kOutput, calls=%fused_computation.10 | convolution fusion | flops 2415919104 | bytes 8650752 | tf_op jit(solution)/shard_map/scd,df->scf/dot_general | solution.py:317
  169.9 2.9 %convolution_convert_fusion = bf16[16,48,1536]{2,1,0:T(8,128)(2,1)} fusion(bf16[1536,2,512]{2,0,1:T(8,128)(2,1)S(1)} %copy-done.11, f32[16,48,1024]{2,1,0:T(8,128)S(1)} %fusion.1), kind=kOutput, calls=%fused_computation.5 | convolution fusion | flops 1211498496 | bytes 7077888 | tf_op jit(solution)/shard_map/scf,df->scd/dot_general | solution.py:321
  172.7 24.4 %all-to-all-done.3 = bf16[16,48,1536]{2,1,0:T(8,128)(2,1)} async-done(((bf16[16,48,1536]{2,1,0:T(8,128)(2,1)}), bf16[16,48,1536]{2,1,0:T(8,128)(2,1)}, u32[]{:S(2)}, u32[]{:S(2)}) %all-to-all-start.3) | async-done | bytes 2359328 | tf_op jit(solution)/shard_map/all_to_all | solution.py:325
  197.1 4.4 %all-to-all-start.5 = ((bf16[16,48,1536]{2,1,0:T(8,128)(2,1)}), bf16[16,48,1536]{2,1,0:T(8,128)(2,1)}, u32[]{:S(2)}, u32[]{:S(2)}) async-start(bf16[16,48,1536]{2,1,0:T(8,128)(2,1)} %convolution_convert_fusion), calls=%async_computation.5 | async-start | bytes 4718592 | tf_op jit(solution)/shard_map/all_to_all | solution.py:325
  202.4 6.3 %fusion.3 = f32[1024,1536]{1,0:T(8,128)} fusion(bf16[768,1536]{1,0:T(8,128)(2,1)} %bitcast.19, s32[1024]{0:T(1024)S(1)} %get-tuple-element.24), kind=kOutput, calls=%fused_computation.15 | convolution fusion | flops 2416705536 | bytes 8654848 | tf_op jit(solution)/shard_map/dot_general | solution.py:337
  208.7 25.4 %all-to-all-done.5 = bf16[16,48,1536]{2,1,0:T(8,128)(2,1)} async-done(((bf16[16,48,1536]{2,1,0:T(8,128)(2,1)}), bf16[16,48,1536]{2,1,0:T(8,128)(2,1)}, u32[]{:S(2)}, u32[]{:S(2)}) %all-to-all-start.5) | async-done | bytes 2359328 | tf_op jit(solution)/shard_map/all_to_all | solution.py:325
  234.1 6.7 %fusion = f32[128,1536]{1,0:T(8,128)S(1)} fusion(f32[1024,1536]{1,0:T(8,128)} %fusion.3, bf16[768,1536]{1,0:T(8,128)(2,1)} %bitcast.25, f32[128,8]{1,0:T(8,128)S(1)} %copy.120, s32[1024]{0:T(1024)S(1)} %get-tuple-element.23), kind=kOutput, calls=%fused_computation.4 | convolution fusion | flops 2421227520 | bytes 9445376 | tf_op jit(solution)/shard_map/dot_general | solution.py:337
  240.8 1.0 add.89
  (120 shorter events, 16.0 us)
Async XLA Ops:
  7.2 194.8 %copy-start = (bf16[1536,32]{0,1:T(8,128)(2,1)S(1)}, bf16[1536,32]{0,1:T(8,128)(2,1)}, u32[]{:S(2)}) copy-start(bf16[1536,32]{0,1:T(8,128)(2,1)} %param.26) | copy-start | bytes 294916
  7.2 3.1 %copy-start.8 = (s32[8]{0:T(128)S(1)}, s32[8]{0:T(128)}, u32[]{:S(2)}) copy-start(s32[8]{0:T(128)} %param.20) | copy-start | bytes 100
  7.2 3.4 %copy-start.10 = (s32[16]{0:T(128)S(1)}, s32[16]{0:T(128)}, u32[]{:S(2)}) copy-start(s32[16]{0:T(128)} %param.18) | copy-start | bytes 196
  7.2 4.1 %copy-start.5 = (bf16[16,1536]{1,0:T(8,128)(2,1)S(1)}, bf16[16,1536]{1,0:T(8,128)(2,1)}, u32[]{:S(2)}) copy-start(bf16[16,1536]{1,0:T(8,128)(2,1)} %param.15) | copy-start | bytes 147460
  7.2 12.2 %copy-start.2 = (bf16[192,2,512]{2,1,0:T(2,128)(2,1)S(1)}, bf16[192,2,512]{2,1,0:T(2,128)(2,1)}, u32[]{:S(2)}) copy-start(bf16[192,2,512]{2,1,0:T(2,128)(2,1)} %param.29) | copy-start | bytes 1179652
  7.2 74.3 %all-gather.4.cloned.1.call-start = ((), (), s32[]{:S(2)}) async-start(), calls=%async_computation.6 | async-start | bytes 5308416 | tf_op jit(solution)/shard_map/all_gather | solution.py:278
  8.0 12.5 %copy-start.6 = (s32[128,8]{0,1:T(8,128)S(1)}, s32[128,8]{0,1:T(8,128)}, u32[]{:S(2)}) copy-start(s32[128,8]{0,1:T(8,128)} %param.27) | copy-start | bytes 12292
  8.0 12.7 %copy-start.9 = (bf16[1536]{0:T(1024)(128)(2,1)S(1)}, bf16[1536]{0:T(1024)(128)(2,1)}, u32[]{:S(2)}) copy-start(bf16[1536]{0:T(1024)(128)(2,1)} %param.25) | copy-start | bytes 9220
  8.0 12.9 %slice-start = ((bf16[16,1536]{1,0:T(8,128)(2,1)}), bf16[8,1536]{1,0:T(8,128)(2,1)S(1)}, s32[]{:S(2)}) async-start(bf16[16,1536]{1,0:T(8,128)(2,1)} %param.15), calls=%async_computation.9 | async-start | bytes 49152 | tf_op jit(solution)/shard_map/slice | solution.py:228
  8.0 13.0 %copy-start.7 = (bf16[16,1024]{1,0:T(8,128)(2,1)S(1)}, bf16[16,1024]{1,0:T(8,128)(2,1)}, u32[]{:S(2)}) copy-start(bf16[16,1024]{1,0:T(8,128)(2,1)} %param.16) | copy-start | bytes 98308
  8.0 119.6 %all-gather.6.cloned.1.call-start = ((), (), s32[]{:S(2)}) async-start(), calls=%async_computation.7 | async-start | bytes 7077888 | tf_op jit(solution)/shard_map/all_gather | solution.py:279
  12.3 24.4 %all-to-all-start = ((f32[16,1,1537]{2,1,0:T(1,128)}), f32[16,1,1537]{2,1,0:T(1,128)S(1)}, u32[]{:S(2)}, u32[]{:S(2)}) async-start(f32[16,1,1537]{2,1,0:T(1,128)} %copy.100), calls=%async_computation | async-start | bytes 212992 | tf_op jit(solution)/shard_map/all_to_all | solution.py:143
  19.4 115.1 %all-gather.8.cloned.1.call-start = ((), (), s32[]{:S(2)}) async-start(), calls=%async_computation.8 | async-start | bytes 3538944 | tf_op jit(solution)/shard_map/all_gather | solution.py:280
  59.5 17.3 %all-to-all-start.1 = ((f32[16,1,8,3,66]{4,2,3,1,0:T(8,128)}), f32[16,1,8,3,66]{4,2,3,1,0:T(8,128)S(1)}, u32[]{:S(2)}, u32[]{:S(2)}) async-start(f32[16,1,8,3,66]{4,2,3,1,0:T(8,128)} %copy.105), calls=%async_computation.1 | async-start | bytes 393216 | tf_op jit(solution)/shard_map/all_to_all | solution.py:143
  77.5 4.0 %copy-start.1 = (bf16[128,1536]{1,0:T(8,128)(2,1)S(1)}, bf16[128,1536]{1,0:T(8,128)(2,1)}, u32[]{:S(2)}) copy-start(bf16[128,1536]{1,0:T(8,128)(2,1)} %param.23) | copy-start | bytes 1179652
  77.5 4.0 %copy-start.3 = (bf16[112,1536]{1,0:T(8,128)(2,1)S(1)}, bf16[112,1536]{1,0:T(8,128)(2,1)}, u32[]{:S(2)}) copy-start(bf16[112,1536]{1,0:T(8,128)(2,1)} %param.22) | copy-start | bytes 1032196
  81.5 3.3 %copy-start.4 = (bf16[16,1536]{1,0:T(8,128)(2,1)}, bf16[16,1536]{1,0:T(8,128)(2,1)S(1)}, u32[]{:S(2)}) copy-start(bf16[16,1536]{1,0:T(8,128)(2,1)S(1)} %fusion.22) | copy-start | bytes 147460
  87.2 35.7 %all-to-all-start.2 = ((bf16[16,48,1536]{2,1,0:T(8,128)(2,1)}), bf16[16,48,1536]{2,1,0:T(8,128)(2,1)}, u32[]{:S(2)}, u32[]{:S(2)}) async-start(bf16[16,48,1536]{2,1,0:T(8,128)(2,1)} %convolution_convert_fusion.3), calls=%async_computation.2 | async-start | bytes 4718592 | tf_op jit(solution)/shard_map/all_to_all | solution.py:316
  122.9 37.1 %all-to-all-start.4 = ((bf16[16,48,1536]{2,1,0:T(8,128)(2,1)}), bf16[16,48,1536]{2,1,0:T(8,128)(2,1)}, u32[]{:S(2)}, u32[]{:S(2)}) async-start(bf16[16,48,1536]{2,1,0:T(8,128)(2,1)} %convolution_convert_fusion.1), calls=%async_computation.4 | async-start | bytes 4718592 | tf_op jit(solution)/shard_map/all_to_all | solution.py:316
  160.0 37.0 %all-to-all-start.3 = ((bf16[16,48,1536]{2,1,0:T(8,128)(2,1)}), bf16[16,48,1536]{2,1,0:T(8,128)(2,1)}, u32[]{:S(2)}, u32[]{:S(2)}) async-start(bf16[16,48,1536]{2,1,0:T(8,128)(2,1)} %convolution_convert_fusion.2), calls=%async_computation.3 | async-start | bytes 4718592 | tf_op jit(solution)/shard_map/all_to_all | solution.py:325
  164.5 5.4 %copy-start.11 = (bf16[1536,2,512]{2,0,1:T(8,128)(2,1)S(1)}, bf16[1536,2,512]{2,0,1:T(8,128)(2,1)}, u32[]{:S(2)}) copy-start(bf16[1536,2,512]{2,0,1:T(8,128)(2,1)} %all-gather.8.cloned.1.call-done) | copy-start | bytes 9437188
  197.1 37.0 %all-to-all-start.5 = ((bf16[16,48,1536]{2,1,0:T(8,128)(2,1)}), bf16[16,48,1536]{2,1,0:T(8,128)(2,1)}, u32[]{:S(2)}, u32[]{:S(2)}) async-start(bf16[16,48,1536]{2,1,0:T(8,128)(2,1)} %convolution_convert_fusion), calls=%async_computation.5 | async-start | bytes 4718592 | tf_op jit(solution)/shard_map/all_to_all | solution.py:325
Sparse Core Ops, SparseCore 0:
  9.7 33.6 all-gather.3
  45.1 41.0 all-gather.5
  87.9 28.6 all-gather.7

commit v12 on v11

--- a/solution.py
+++ b/solution.py
@@ -324,22 +324,25 @@
         returned_parts.append(
             lax.all_to_all(expert_rows, "gy", split_axis=0, concat_axis=0, tiled=True)
         )
-    flat_place = place_of.reshape(row_count * TOP)
-    flat_expert = routes.reshape(row_count * TOP)
-    picked = None
+    mixed = None
     for local, part in enumerate(returned_parts):
-        spot = jnp.where(
-            flat_expert % experts_dev == local, flat_expert // experts_dev * CAP + flat_place, -1
-        )
-        one_hot = (spot[:, None] == jnp.arange(columns * CAP, dtype=jnp.int32)[None, :]).astype(
-            jnp.bfloat16
+        spot = jnp.where(routes % experts_dev == local, routes // experts_dev * CAP + place_of, -1)
+        gate_spot = jnp.sum(
+            jnp.where(
+                spot[:, :, None] == jnp.arange(columns * CAP, dtype=jnp.int32)[None, None, :],
+                gate_weights[:, :, None],
+                0.0,
+            ),
+            axis=1,
         )
         share = jnp.dot(
-            one_hot, part.reshape(columns * CAP, D), preferred_element_type=jnp.float32
-        )
-        picked = share if picked is None else picked + share
-    picked = picked.reshape(row_count, TOP, D)
-    layer_out = stream + jnp.sum(gate_weights[:, :, None] * picked, axis=1)
+            gate_spot,
+            part.reshape(columns * CAP, D),
+            precision=lax.Precision.HIGHEST,
+            preferred_element_type=jnp.float32,
+        )
+        mixed = share if mixed is None else mixed + share
+    layer_out = stream + mixed
     return (attended, layer_out)
 
 

time: 253 us -> 252 us (level); the launches traced: 248 us -> 250 us
  waiting for transfers between devices: 108 us -> 114 us
  matrix products: 41.8 us -> 36.7 us
  starting transfers between devices: 34.1 us -> 30.4 us
    dot_general x2, matrix products: 13.1 us -> 6.9 us  [body(): jnp.dot(gate_spot, part.reshape(columns * CAP, D), precision=lax.Precisio...]
    all_to_all x2, waiting for transfers between devices: 49.5 us -> 53.6 us  [body(): lax.all_to_all(outgoing, 'gy', split_axis=0, concat_axis=0, tiled=True)]
    reduce_sum x0 -> x1, other arithmetic: none -> 3.16 us  [body(): jnp.sum(jnp.where(spot[:, :, None] == jnp.arange(columns * CAP, dtype=jnp...]
    unnamed x29 -> x38, local copies, waits for them, and re-layouts: 3.6 us -> 6.45 us
where the time goes in v12:
time: 252 us; the launch traced here: 250 us
  waiting for transfers between devices  114 us (45%)
  matrix products  36.7 us (15%)
  starting transfers between devices  30.4 us (12%)
  Pallas kernels  24.9 us (10%)
  local copies, waits for them, and re-layouts  20.8 us (8%)
  between operations  14.3 us (6%)
  other arithmetic  8.54 us (3%)
    all_to_all x2, waiting for transfers between devices, body(): lax.all_to_all(outgoing, 'gy', split_axis=0, concat_axis=0, tiled=True)  53.6 us
    all_to_all x2, waiting for transfers between devices, body(): lax.all_to_all(expert_rows, 'gy', split_axis=0, concat_axis=0, tiled=True)  51.5 us
    pallas_call x2, Pallas kernels, paged_attend(): pl.pallas_call(attend_kernel, grid_spec=grid_spec, out_shape=[jax.ShapeDt...  24.9 us
    all_to_all x2, starting transfers between devices, in_one_piece(): lax.all_to_all(both, axis, split_axis=split_dim, concat_axis=concat_dim,...  14.5 us
    dot_general x2, matrix products, body(): jnp.einsum('scd,df->scf', arrived, full_pair[:, local], preferred_element...  12.2 us
    all_to_all x2, waiting for transfers between devices, in_one_piece(): lax.all_to_all(both, axis, split_axis=split_dim, concat_axis=concat_dim,...  8.39 us
    all_to_all x2, starting transfers between devices, body(): lax.all_to_all(outgoing, 'gy', split_axis=0, concat_axis=0, tiled=True)  8.36 us
    dot_general x2, matrix products, body(): jnp.einsum('scf,df->scd', hidden, full_down[:, local], preferred_element_...  8.03 us
  transfers between devices with their start and end apart: 9, of which 5 were waited for; matrix products, arithmetic and copies ran while one was open for 24% of the time, Pallas kernels for 10%

profile of v12, /device:TPU:96, one launch (start us, length us, event | category | flops | bytes accessed | tf_op | source)
XLA Modules:
  0.0 249.9 jit_solution(14671026771919750957)
XLA Ops:
  8.0 2.2 copy.129
  12.3 7.0 %all-to-all-start = ((f32[16,1,1537]{2,1,0:T(1,128)}), f32[16,1,1537]{2,1,0:T(1,128)S(1)}, u32[]{:S(2)}, u32[]{:S(2)}) async-start(f32[16,1,1537]{2,1,0:T(1,128)} %copy.105), calls=%async_computation | async-start | bytes 212992 | tf_op jit(solution)/shard_map/all_to_all | solution.py:143
  21.7 9.9 %shard_map.158 = (f32[8,24,128]{2,1,0:T(8,128)}, f32[8,24,128]{2,1,0:T(8,128)}, f32[8,24,512]{2,1,0:T(8,128)}) custom-call(s32[8,32]{1,0:T(8,128)} %tables.2, s32[8]{0:T(128)} %get-tuple-element.32.lengths, bf16[8,24,512]{2,1,0:T(8,128)(2,1)} %broadcast_select_fusion.1.q_ref, bf16[128,16,1024]{2,1,0:T(8,128)(2,1)} %pool_ref.3), custom_call_target="tpu_custom_call" | custom-call | flops 201326592 | bytes 8388608 | tf_op jit(solution)/shard_map/pallas_call | solution.py:115
  31.7 1.0 slice_reduce_fusion.1
  32.9 1.0 slice_reduce_fusion
  34.7 1.2 reshape.138
  38.6 0.9 fusion.24.lengths
  39.5 15.0 %shard_map.159 = (f32[16,24,128]{2,1,0:T(8,128)}, f32[16,24,128]{2,1,0:T(8,128)}, f32[16,24,512]{2,1,0:T(8,128)}) custom-call(s32[16,32]{1,0:T(8,128)} %tables.3, s32[16]{0:T(128)} %fusion.24.lengths, bf16[16,24,512]{2,1,0:T(8,128)(2,1)} %broadcast_select_fusion.q_ref, bf16[128,16,1024]{2,1,0:T(8,128)(2,1)} %pool_ref.3), custom_call_target="tpu_custom_call" | custom-call | flops 402653184 | bytes 16777216 | tf_op jit(solution)/shard_map/pallas_call | solution.py:115
  54.6 1.6 reshape.134
  58.9 7.5 %all-to-all-start.1 = ((f32[16,1,8,3,66]{4,2,3,1,0:T(8,128)}), f32[16,1,8,3,66]{4,2,3,1,0:T(8,128)S(1)}, u32[]{:S(2)}, u32[]{:S(2)}) async-start(f32[16,1,8,3,66]{4,2,3,1,0:T(8,128)} %copy.110), calls=%async_computation.1 | async-start | bytes 393216 | tf_op jit(solution)/shard_map/all_to_all | solution.py:143
  66.4 8.4 %all-to-all-done.1 = f32[16,1,8,3,66]{4,2,3,1,0:T(8,128)S(1)} async-done(((f32[16,1,8,3,66]{4,2,3,1,0:T(8,128)}), f32[16,1,8,3,66]{4,2,3,1,0:T(8,128)S(1)}, u32[]{:S(2)}, u32[]{:S(2)}) %all-to-all-start.1) | async-done | bytes 101408 | tf_op jit(solution)/shard_map/all_to_all | solution.py:143
  79.6 3.3 %multiply_reduce_fusion = (f32[128]{0:T(128)S(1)}, f32[128,1536]{1,0:T(8,128)S(1)}) fusion(bf16[1536,1536]{1,0:T(8,128)(2,1)} %all-gather.4.cloned.1.call-done, bf16[112,1536]{1,0:T(8,128)(2,1)S(1)} %copy-done.6, bf16[16,1536]{1,0:T(8,128)(2,1)S(1)} %fusion.19, bf16[128,1536]{1,0:T(8,128)(2,1)S(1)} %copy-done.4), kind=kOutput, calls=%fused_computation.31 | convolution fusion | flops 605552512 | bytes 6291968 | tf_op jit(solution)/shard_map/dot_general | solution.py:281
  83.0 2.2 convolution_convert_fusion.3
  85.2 4.5 %all-to-all-start.2 = ((bf16[16,48,1536]{2,1,0:T(8,128)(2,1)}), bf16[16,48,1536]{2,1,0:T(8,128)(2,1)}, u32[]{:S(2)}, u32[]{:S(2)}) async-start(bf16[16,48,1536]{2,1,0:T(8,128)(2,1)} %convolution_convert_fusion.3), calls=%async_computation.2 | async-start | bytes 4718592 | tf_op jit(solution)/shard_map/all_to_all | solution.py:316
  89.7 2.3 convolution_convert_fusion.1
  91.9 31.9 %all-to-all-done.2 = bf16[16,48,1536]{2,1,0:T(8,128)(2,1)} async-done(((bf16[16,48,1536]{2,1,0:T(8,128)(2,1)}), bf16[16,48,1536]{2,1,0:T(8,128)(2,1)}, u32[]{:S(2)}, u32[]{:S(2)}) %all-to-all-start.2) | async-done | bytes 2359328 | tf_op jit(solution)/shard_map/all_to_all | solution.py:316
  123.8 3.9 %all-to-all-start.4 = ((bf16[16,48,1536]{2,1,0:T(8,128)(2,1)}), bf16[16,48,1536]{2,1,0:T(8,128)(2,1)S(1)}, u32[]{:S(2)}, u32[]{:S(2)}) async-start(bf16[16,48,1536]{2,1,0:T(8,128)(2,1)} %convolution_convert_fusion.1), calls=%async_computation.4 | async-start | bytes 4718592 | tf_op jit(solution)/shard_map/all_to_all | solution.py:316
  127.8 6.9 %fusion.1 = f32[16,48,1024]{2,1,0:T(8,128)} fusion(bf16[16,48,1536]{2,1,0:T(8,128)(2,1)} %all-to-all-done.2, bf16[1536,2,1024]{2,0,1:T(8,128)(2,1)} %all-gather.6.cloned.1.call-done), kind=kOutput, calls=%fused_computation.10 | convolution fusion | flops 2415919104 | bytes 8650752 | tf_op jit(solution)/shard_map/scd,df->scf/dot_general | solution.py:317
  134.6 5.2 %convolution_convert_fusion.2 = bf16[16,48,1536]{2,1,0:T(8,128)(2,1)} fusion(bf16[1536,2,512]{2,0,1:T(8,128)(2,1)} %all-gather.8.cloned.1.call-done, f32[16,48,1024]{2,1,0:T(8,128)} %fusion.1), kind=kOutput, calls=%fused_computation.5 | convolution fusion | flops 1211498496 | bytes 7077888 | tf_op jit(solution)/shard_map/scf,df->scd/dot_general | solution.py:321
  139.8 21.7 %all-to-all-done.4 = bf16[16,48,1536]{2,1,0:T(8,128)(2,1)S(1)} async-done(((bf16[16,48,1536]{2,1,0:T(8,128)(2,1)}), bf16[16,48,1536]{2,1,0:T(8,128)(2,1)S(1)}, u32[]{:S(2)}, u32[]{:S(2)}) %all-to-all-start.4) | async-done | bytes 2359328 | tf_op jit(solution)/shard_map/all_to_all | solution.py:316
  161.5 1.5 copy-done.3
  163.0 3.7 %all-to-all-start.3 = ((bf16[16,48,1536]{2,1,0:T(8,128)(2,1)}), bf16[16,48,1536]{2,1,0:T(8,128)(2,1)S(1)}, u32[]{:S(2)}, u32[]{:S(2)}) async-start(bf16[16,48,1536]{2,1,0:T(8,128)(2,1)} %convolution_convert_fusion.2), calls=%async_computation.3 | async-start | bytes 4718592 | tf_op jit(solution)/shard_map/all_to_all | solution.py:325
  166.8 5.3 %fusion = f32[16,48,1024]{2,1,0:T(8,128)S(1)} fusion(bf16[16,48,1536]{2,1,0:T(8,128)(2,1)} %copy-done.3, bf16[1536,2,1024]{2,0,1:T(8,128)(2,1)} %all-gather.6.cloned.1.call-done), kind=kOutput, calls=%fused_computation.8 | convolution fusion | flops 2415919104 | bytes 8650752 | tf_op jit(solution)/shard_map/scd,df->scf/dot_general | solution.py:317
  172.1 2.9 %convolution_convert_fusion = bf16[16,48,1536]{2,1,0:T(8,128)(2,1)} fusion(bf16[1536,2,512]{2,0,1:T(8,128)(2,1)S(1)} %copy-done.16, f32[16,48,1024]{2,1,0:T(8,128)S(1)} %fusion), kind=kOutput, calls=%fused_computation.3 | convolution fusion | flops 1211498496 | bytes 7077888 | tf_op jit(solution)/shard_map/scf,df->scd/dot_general | solution.py:321
  175.0 25.9 %all-to-all-done.3 = bf16[16,48,1536]{2,1,0:T(8,128)(2,1)S(1)} async-done(((bf16[16,48,1536]{2,1,0:T(8,128)(2,1)}), bf16[16,48,1536]{2,1,0:T(8,128)(2,1)S(1)}, u32[]{:S(2)}, u32[]{:S(2)}) %all-to-all-start.3) | async-done | bytes 2359328 | tf_op jit(solution)/shard_map/all_to_all | solution.py:325
  200.9 1.4 copy-done.1
  202.3 3.7 %all-to-all-start.5 = ((bf16[16,48,1536]{2,1,0:T(8,128)(2,1)}), bf16[16,48,1536]{2,1,0:T(8,128)(2,1)S(1)}, u32[]{:S(2)}, u32[]{:S(2)}) async-start(bf16[16,48,1536]{2,1,0:T(8,128)(2,1)} %convolution_convert_fusion), calls=%async_computation.5 | async-start | bytes 4718592 | tf_op jit(solution)/shard_map/all_to_all | solution.py:325
  206.3 1.2 fusion.41
  207.8 3.2 %select_reduce_fusion = (f32[128,768]{1,0:T(8,128)}, f32[128,768]{1,0:T(8,128)S(1)}) fusion(s32[128,8]{1,0:T(8,128)S(1)} %copy.131, f32[128,8]{1,0:T(8,128)S(1)} %copy.126, s32[128,8]{1,0:T(8,128)S(1)} %copy.125), kind=kLoop, calls=%fused_computation.11 | loop fusion | flops 4521984 | bytes 798720 | tf_op jit(solution)/shard_map/reduce_sum | solution.py:330
  210.9 3.6 %fusion.42 = f32[128,1536]{1,0:T(8,128)} fusion(f32[128,768]{1,0:T(8,128)S(1)} %get-tuple-element.15, bf16[768,1536]{1,0:T(8,128)(2,1)} %bitcast.73), kind=kOutput, calls=%fused_computation.105 | convolution fusion | flops 1811939328 | bytes 3538944 | tf_op jit(solution)/shard_map/dot_general | solution.py:338
  214.6 25.6 %all-to-all-done.5 = bf16[16,48,1536]{2,1,0:T(8,128)(2,1)S(1)} async-done(((bf16[16,48,1536]{2,1,0:T(8,128)(2,1)}), bf16[16,48,1536]{2,1,0:T(8,128)(2,1)S(1)}, u32[]{:S(2)}, u32[]{:S(2)}) %all-to-all-start.5) | async-done | bytes 2359328 | tf_op jit(solution)/shard_map/all_to_all | solution.py:325
  240.1 3.2 %fusion.2 = f32[128,1536]{1,0:T(8,128)} fusion(f32[128,1536]{1,0:T(8,128)S(1)} %get-tuple-element.30, f32[128,1536]{1,0:T(8,128)} %fusion.42, f32[128,768]{1,0:T(8,128)} %get-tuple-element.14, bf16[768,1536]{1,0:T(8,128)(2,1)S(1)} %bitcast.72), kind=kOutput, calls=%fused_computation.16 | convolution fusion | flops 1812332544 | bytes 5111808 | tf_op jit(solution)/shard_map/dot_general | solution.py:338
  (128 shorter events, 16.9 us)
Async XLA Ops:
  7.2 199.2 %copy-start = (bf16[1536,32]{0,1:T(8,128)(2,1)S(1)}, bf16[1536,32]{0,1:T(8,128)(2,1)}, u32[]{:S(2)}) copy-start(bf16[1536,32]{0,1:T(8,128)(2,1)} %param.26) | copy-start | bytes 294916
  7.2 3.1 %copy-start.13 = (s32[8]{0:T(128)S(1)}, s32[8]{0:T(128)}, u32[]{:S(2)}) copy-start(s32[8]{0:T(128)} %param.20) | copy-start | bytes 100
  7.2 3.4 %copy-start.15 = (s32[16]{0:T(128)S(1)}, s32[16]{0:T(128)}, u32[]{:S(2)}) copy-start(s32[16]{0:T(128)} %param.18) | copy-start | bytes 196
  7.2 4.0 %copy-start.10 = (bf16[16,1536]{1,0:T(8,128)(2,1)S(1)}, bf16[16,1536]{1,0:T(8,128)(2,1)}, u32[]{:S(2)}) copy-start(bf16[16,1536]{1,0:T(8,128)(2,1)} %param.15) | copy-start | bytes 147460
  7.2 12.2 %copy-start.5 = (bf16[192,2,512]{2,1,0:T(2,128)(2,1)S(1)}, bf16[192,2,512]{2,1,0:T(2,128)(2,1)}, u32[]{:S(2)}) copy-start(bf16[192,2,512]{2,1,0:T(2,128)(2,1)} %param.29) | copy-start | bytes 1179652
  7.2 72.3 %all-gather.4.cloned.1.call-start = ((), (), s32[]{:S(2)}) async-start(), calls=%async_computation.6 | async-start | bytes 5308416 | tf_op jit(solution)/shard_map/all_gather | solution.py:278
  8.0 12.6 %slice-start = ((bf16[16,1536]{1,0:T(8,128)(2,1)}), bf16[8,1536]{1,0:T(8,128)(2,1)S(1)}, s32[]{:S(2)}) async-start(bf16[16,1536]{1,0:T(8,128)(2,1)} %param.15), calls=%async_computation.9 | async-start | bytes 49152 | tf_op jit(solution)/shard_map/slice | solution.py:228
  8.0 119.8 %all-gather.6.cloned.1.call-start = ((), (), s32[]{:S(2)}) async-start(), calls=%async_computation.7 | async-start | bytes 7077888 | tf_op jit(solution)/shard_map/all_gather | solution.py:279
  12.3 24.5 %all-to-all-start = ((f32[16,1,1537]{2,1,0:T(1,128)}), f32[16,1,1537]{2,1,0:T(1,128)S(1)}, u32[]{:S(2)}, u32[]{:S(2)}) async-start(f32[16,1,1537]{2,1,0:T(1,128)} %copy.105), calls=%async_computation | async-start | bytes 212992 | tf_op jit(solution)/shard_map/all_to_all | solution.py:143
  19.3 115.3 %all-gather.8.cloned.1.call-start = ((), (), s32[]{:S(2)}) async-start(), calls=%async_computation.8 | async-start | bytes 3538944 | tf_op jit(solution)/shard_map/all_gather | solution.py:280
  21.7 12.3 %copy-start.12 = (bf16[16,1024]{1,0:T(8,128)(2,1)S(1)}, bf16[16,1024]{1,0:T(8,128)(2,1)}, u32[]{:S(2)}) copy-start(bf16[16,1024]{1,0:T(8,128)(2,1)} %param.16) | copy-start | bytes 98308
  21.7 14.1 %copy-start.11 = (s32[128,8]{0,1:T(8,128)S(1)}, s32[128,8]{0,1:T(8,128)}, u32[]{:S(2)}) copy-start(s32[128,8]{0,1:T(8,128)} %param.27) | copy-start | bytes 12292
  31.6 5.1 %copy-start.14 = (bf16[1536]{0:T(1024)(128)(2,1)S(1)}, bf16[1536]{0:T(1024)(128)(2,1)}, u32[]{:S(2)}) copy-start(bf16[1536]{0:T(1024)(128)(2,1)} %param.25) | copy-start | bytes 9220
  54.5 2.2 copy-start.9
  54.6 2.8 %copy-start.8 = (f32[16,24,128]{2,1,0:T(8,128)S(1)}, f32[16,24,128]{2,1,0:T(8,128)}, u32[]{:S(2)}) copy-start(f32[16,24,128]{2,1,0:T(8,128)} %get-tuple-element.10) | copy-start | bytes 589828
  58.9 15.9 %all-to-all-start.1 = ((f32[16,1,8,3,66]{4,2,3,1,0:T(8,128)}), f32[16,1,8,3,66]{4,2,3,1,0:T(8,128)S(1)}, u32[]{:S(2)}, u32[]{:S(2)}) async-start(f32[16,1,8,3,66]{4,2,3,1,0:T(8,128)} %copy.110), calls=%async_computation.1 | async-start | bytes 393216 | tf_op jit(solution)/shard_map/all_to_all | solution.py:143
  74.9 4.6 %copy-start.4 = (bf16[128,1536]{1,0:T(8,128)(2,1)S(1)}, bf16[128,1536]{1,0:T(8,128)(2,1)}, u32[]{:S(2)}) copy-start(bf16[128,1536]{1,0:T(8,128)(2,1)} %param.23) | copy-start | bytes 1179652
  74.9 4.6 %copy-start.6 = (bf16[112,1536]{1,0:T(8,128)(2,1)S(1)}, bf16[112,1536]{1,0:T(8,128)(2,1)}, u32[]{:S(2)}) copy-start(bf16[112,1536]{1,0:T(8,128)(2,1)} %param.22) | copy-start | bytes 1032196
  79.5 3.3 %copy-start.7 = (bf16[16,1536]{1,0:T(8,128)(2,1)}, bf16[16,1536]{1,0:T(8,128)(2,1)S(1)}, u32[]{:S(2)}) copy-start(bf16[16,1536]{1,0:T(8,128)(2,1)S(1)} %fusion.19) | copy-start | bytes 147460
  83.0 6.7 %copy-start.2 = (bf16[128,1536]{1,0:T(8,128)(2,1)}, bf16[128,1536]{1,0:T(8,128)(2,1)S(1)}, u32[]{:S(2)}) copy-start(bf16[128,1536]{1,0:T(8,128)(2,1)S(1)} %multiply_convert_fusion) | copy-start | bytes 1179652
  85.2 38.6 %all-to-all-start.2 = ((bf16[16,48,1536]{2,1,0:T(8,128)(2,1)}), bf16[16,48,1536]{2,1,0:T(8,128)(2,1)}, u32[]{:S(2)}, u32[]{:S(2)}) async-start(bf16[16,48,1536]{2,1,0:T(8,128)(2,1)} %convolution_convert_fusion.3), calls=%async_computation.2 | async-start | bytes 4718592 | tf_op jit(solution)/shard_map/all_to_all | solution.py:316
  123.8 37.7 %all-to-all-start.4 = ((bf16[16,48,1536]{2,1,0:T(8,128)(2,1)}), bf16[16,48,1536]{2,1,0:T(8,128)(2,1)S(1)}, u32[]{:S(2)}, u32[]{:S(2)}) async-start(bf16[16,48,1536]{2,1,0:T(8,128)(2,1)} %convolution_convert_fusion.1), calls=%async_computation.4 | async-start | bytes 4718592 | tf_op jit(solution)/shard_map/all_to_all | solution.py:316
  161.5 1.5 copy-start.3
  163.0 37.9 %all-to-all-start.3 = ((bf16[16,48,1536]{2,1,0:T(8,128)(2,1)}), bf16[16,48,1536]{2,1,0:T(8,128)(2,1)S(1)}, u32[]{:S(2)}, u32[]{:S(2)}) async-start(bf16[16,48,1536]{2,1,0:T(8,128)(2,1)} %convolution_convert_fusion.2), calls=%async_computation.3 | async-start | bytes 4718592 | tf_op jit(solution)/shard_map/all_to_all | solution.py:325
  166.8 5.4 %copy-start.16 = (bf16[1536,2,512]{2,0,1:T(8,128)(2,1)S(1)}, bf16[1536,2,512]{2,0,1:T(8,128)(2,1)}, u32[]{:S(2)}) copy-start(bf16[1536,2,512]{2,0,1:T(8,128)(2,1)} %all-gather.8.cloned.1.call-done) | copy-start | bytes 9437188
  200.9 1.4 copy-start.1
  202.3 37.8 %all-to-all-start.5 = ((bf16[16,48,1536]{2,1,0:T(8,128)(2,1)}), bf16[16,48,1536]{2,1,0:T(8,128)(2,1)S(1)}, u32[]{:S(2)}, u32[]{:S(2)}) async-start(bf16[16,48,1536]{2,1,0:T(8,128)(2,1)} %convolution_convert_fusion), calls=%async_computation.5 | async-start | bytes 4718592 | tf_op jit(solution)/shard_map/all_to_all | solution.py:325
Sparse Core Ops, SparseCore 0:
  9.7 33.7 all-gather.3
  45.2 40.9 all-gather.5
  87.8 28.7 all-gather.7
